TPU v7x, 256 devices: a whole 4x4x8 slice. The times are simulated.
256 devices in a mesh: dp: 32 (over y, x, core), tensor: 8 (over z).
Axes of the slice: x: 4, y: 4, z: 8, core: 2. Of those that a mesh axis runs over, the one named last changes fastest.
Arguments:
- patches: bfloat16 [16384, 1280], P('dp'), may hold values from -6 to 6
- window_ids: int32 [32, 512], P('dp'), may hold values from 0 to 15, never falling along the last dimension, each value on 1 to 64 neighbouring positions
- vit_gain: float32 [1280], replicated, may hold values from 0.5 to 2
- qkv_weight: bfloat16 [3, 1280, 1280], P(None, None, 'tensor'), may hold values from -0.15625 to 0.15625
- out_weight: bfloat16 [1280, 1280], P('tensor'), may hold values from -0.15625 to 0.15625
- merge_gain: float32 [1280], replicated, may hold values from 0.5 to 2
- merger_weight: bfloat16 [5120, 3584], P(None, 'tensor'), may hold values from -0.078125 to 0.078125
- audio: bfloat16 [12288, 3584], P('dp', 'tensor'), may hold values from -6 to 6
- span_lengths: int32 [32, 32], replicated, may hold values from 8 to 32, as said below
- span_time: int32 [32, 32], replicated, may hold values from 0 to 31, each once within a row
- llm_gain: float32 [3584], replicated, may hold values from 0.5 to 2
- gate_weight: bfloat16 [3584, 9472], P('dp', 'tensor'), may hold values from -0.09375 to 0.09375
- up_weight: bfloat16 [3584, 9472], P('dp', 'tensor'), may hold values from -0.09375 to 0.09375
- down_weight: bfloat16 [9472, 3584], P('tensor', 'dp'), may hold values from -0.0625 to 0.0625
Outputs:
- mixed: bfloat16 [16384, 3584], P(('dp', 'tensor'))
Inputs may be any that keep to these rules, and one draw needn't show every extreme that they name: `span_lengths`: every row and every column sums to 512; every row and every column holds the value 32 at least once. `span_time`: each row is a permutation of the owners' numbers. `window_ids`: window numbers never fall along a row; a window holds at most 64 patches.
All inputs are finite; a program needn't handle non-finite values.
Results may differ from a plain program's by a relative error of at most 0.017.
Values may be sent and summed in bfloat16 or wider, within the bound.
No kernel may reach another device: no remote copies, remote signals or barrier semaphores. Data moves between devices by JAX's collectives and lax.ppermute only.
A program may use at most 128 MiB of HBM per device.

v0:
```python
import functools
import math

import jax
import jax.numpy as jnp
from jax import lax
from jax.experimental import pallas as pl
from jax.experimental.pallas import tpu as pltpu
from jax.sharding import PartitionSpec as P

HEAD_VIT = 80
EPSILON = 1e-06
VMEM = pltpu.MemorySpace.VMEM
SMEM = pltpu.MemorySpace.SMEM
BF16 = jnp.bfloat16
F32 = jnp.float32


def ring_blocks(x, axis, beside=None, rounds_first=2):
    n = lax.axis_size(axis)
    up = [(i, (i + 1) % n) for i in range(n)]
    down = [(i, (i - 1) % n) for i in range(n)]
    blocks = {0: x}
    a = b = x
    for k in range(1, n // 2 + 1):
        a = lax.ppermute(a, axis, up)
        if k < n - n // 2:
            b = lax.ppermute(b, axis, down)
        if beside is not None and k == rounds_first:
            a, b, beside = lax.optimization_barrier((a, b, beside))
        blocks[-k] = a
        if k < n - n // 2:
            blocks[k] = b
    return blocks if beside is None else (blocks, beside)


def turned_dot(left, right):
    return lax.dot_general(left, right, (((1,), (1,)), ((), ())), preferred_element_type=F32)


def inverse_rms(wide):
    return lax.rsqrt(jnp.mean(wide * wide, axis=-1, keepdims=True) + EPSILON)


def vision_kernel(core_ref, patches_ref, column_ref, row_ref, gain_ref, weight_ref, out_ref):
    wide = patches_ref[...].astype(F32)
    normed = (wide * inverse_rms(wide) * gain_ref[...]).astype(BF16)
    query, keys, values = (
        turned_dot(normed, weight_ref[k]).astype(BF16) for k in range(3)
    )
    same = column_ref[...] == row_ref[...]
    for head in range(2):
        part = slice(head * HEAD_VIT, (head + 1) * HEAD_VIT)
        scores = turned_dot(query[:, part], keys[:, part])
        scores = jnp.where(same, scores * (1.0 / math.sqrt(HEAD_VIT)), -1e30)
        weights = jnp.exp(scores - jnp.max(scores, axis=-1, keepdims=True))
        probs = (weights / jnp.sum(weights, axis=-1, keepdims=True)).astype(BF16)
        context = lax.dot_general(
            values[:, part], probs, (((0,), (1,)), ((), ())), preferred_element_type=F32
        )
        place = pl.multiple_of(lax.rem(core_ref[0] + head, 2) * HEAD_VIT, 16)
        out_ref[pl.ds(place, HEAD_VIT), :] = context.astype(BF16)


def stack_kernel(*refs):
    for k, ref in enumerate(refs[:-1]):
        refs[-1][k] = ref[...]


def merge_kernel(n, *refs):
    contexts, mine = refs[:n], refs[n : 2 * n]
    other_ref, patches_ref, gain_ref, merger_hbm, slot_ref, audio_ref, out_ref = refs[2 * n : 2 * n + 7]
    context, weight, normed, merger, sem = refs[2 * n + 7 :]
    fetch = pltpu.make_async_copy(merger_hbm, merger, sem)
    fetch.start()
    for k in range(n):
        context[pl.ds(k * 2 * HEAD_VIT, 2 * HEAD_VIT), :] = contexts[k][...]
        weight[pl.ds(k * 2 * HEAD_VIT, HEAD_VIT), :] = mine[k][...]
        weight[pl.ds((2 * k + 1) * HEAD_VIT, HEAD_VIT), :] = other_ref[k]
    rows, d_vit = patches_ref.shape
    turned = context[...].T

    lanes = 128
    squares = jnp.zeros((rows, 1), F32)
    for j in range(d_vit // 256):
        columns = pl.ds(j * 256, 256)
        attended = jnp.dot(turned, weight[:, columns], preferred_element_type=F32)
        wide = (patches_ref[:, columns].astype(F32) + attended).astype(BF16).astype(F32)
        squares += jnp.sum(wide * wide, axis=-1, keepdims=True)
        normed[2 * j] = wide[:, :lanes]
        normed[2 * j + 1] = wide[:, lanes:]
    scale = lax.rsqrt(squares / d_vit + EPSILON)
    for j in range(d_vit // lanes):
        normed[j] = normed[j] * scale * gain_ref[:, pl.ds(j * lanes, lanes)]

    fetch.wait()
    video = jnp.zeros((rows // 4, merger.shape[0]), F32)
    for j in range(4):
        part = [normed[k, pl.ds(j, rows // 4, stride=4), :] for k in range(d_vit // lanes)]
        part = jnp.concatenate(part, axis=1).astype(BF16)
        video += turned_dot(part, merger[:, pl.ds(j * d_vit, d_vit)])
    video = video.astype(BF16)
    index = lax.broadcasted_iota(jnp.int32, (slot_ref.shape[0], rows // 4), 1)
    select = (slot_ref[...] == index).astype(F32).astype(BF16)
    placed = jnp.dot(select, video, preferred_element_type=F32)
    out_ref[...] = (placed + audio_ref[...].astype(F32)).astype(BF16)


def pick_kernel(target_ref, incoming_ref, out_ref):
    rows = lax.broadcasted_iota(jnp.int32, (out_ref.shape[0], incoming_ref.shape[0]), 0)
    pick = (rows == target_ref[...]).astype(F32).astype(BF16)
    out_ref[...] = jnp.dot(pick, incoming_ref[...], preferred_element_type=F32).astype(BF16)


def ffn_kernel(n, shifts, units, place_ref, *refs):
    blocks, gain_ref, whole_hbm, out_ref, own_ref = refs[:n], refs[n], refs[n + 1], refs[n + 2], refs[n + 3]
    whole, normed, both, hidden, sems = refs[n + 4 :]
    features, width = whole.shape
    tile = 256
    low = 2 * units // tile * tile
    tiles = low // tile

    def part(j):
        columns = pl.ds(pl.multiple_of(j * tile, tile), tile)
        return pltpu.make_async_copy(whole_hbm.at[:, columns], whole.at[:, columns], sems.at[j])

    rest = pltpu.make_async_copy(
        whole_hbm.at[:, pl.ds(low, width - low)], whole.at[:, pl.ds(low, width - low)], sems.at[tiles]
    )

    @pl.loop(0, tiles)
    def _(j):
        part(j).start()

    rest.start()

    rows, chunk = blocks[0].shape
    squares = jnp.zeros((rows, 1), F32)
    for block in blocks:
        wide = block[...].astype(F32)
        squares += jnp.sum(wide * wide, axis=-1, keepdims=True)
    scale = lax.rsqrt(squares / features + EPSILON)
    own = own_ref.shape[1]
    first = pl.multiple_of(place_ref[0] * own, own)
    for shift, block in zip(shifts, blocks):
        at = lax.rem(place_ref[0] + shift + n, n)
        gain = gain_ref[at]
        normed[at] = (block[...].astype(F32) * scale * gain).astype(BF16)
        own_ref[at] = block[pl.ds(first, own), :]

    def product(columns):
        total = jnp.dot(normed[0], whole[pl.ds(0, chunk), columns], preferred_element_type=F32)
        for k in range(1, n):
            total += jnp.dot(normed[k], whole[pl.ds(k * chunk, chunk), columns], preferred_element_type=F32)
        both[:, columns] = total

    @pl.loop(0, tiles)
    def _(j):
        part(j).wait()
        product(pl.ds(pl.multiple_of(j * tile, tile), tile))

    rest.wait()
    lead = 2 * units - low
    tail = (lead + 127) // 128 * 128
    product(pl.ds(low, tail))

    step = 64

    @pl.loop(0, rows // step)
    def _(j):
        here = pl.ds(pl.multiple_of(j * step, step), step)
        gate = both[here, pl.ds(0, units)]
        upward = both[here, pl.ds(units, units)]
        value = gate * (1.0 / (1.0 + jnp.exp(-gate))) * upward
        hidden[here, pl.ds(0, lead)] = jnp.zeros((step, lead), BF16)
        hidden[here, pl.ds(lead, units)] = value.astype(BF16)

    @pl.loop(0, features // tile)
    def _(j):
        here = pl.ds(pl.multiple_of(j * tile, tile), tile)
        out_ref[:, here] = turned_dot(hidden[...], whole[here, pl.ds(low, width - low)]).astype(BF16)


def call(kernel, out_shape, specs, flops, scratch=(), mib=48):
    def run(*args):
        moved = sum(a.size * a.dtype.itemsize for a in args)
        return pl.pallas_call(
            kernel,
            out_shape=out_shape,
            in_specs=specs,
            out_specs=jax.tree.map(lambda _: pl.BlockSpec(memory_space=VMEM), out_shape),
            scratch_shapes=scratch,
            compiler_params=pltpu.CompilerParams(vmem_limit_bytes=mib << 20),
            cost_estimate=pl.CostEstimate(flops=flops, bytes_accessed=moved, transcendentals=0),
        )(*args)

    return run


def body(
    patches,
    window_ids,
    vit_gain,
    qkv_weight,
    out_weight,
    merge_gain,
    merger_weight,
    audio,
    span_lengths,
    span_time,
    llm_gain,
    gate_weight,
    up_weight,
    down_weight,
):
    patch_count, d_vit = patches.shape
    n = lax.axis_size("tensor")
    owner_count = lax.axis_size("dp")
    owner = lax.axis_index("dp")
    plane = lax.axis_index("tensor")
    core = lax.rem(owner, 2)
    units = gate_weight.shape[1]
    vmem = pl.BlockSpec(memory_space=VMEM)
    smem = pl.BlockSpec(memory_space=SMEM)
    hbm = pl.BlockSpec(memory_space=pl.ANY)

    windows = window_ids[0]
    context = call(
        vision_kernel,
        jax.ShapeDtypeStruct((2 * HEAD_VIT, patch_count), BF16),
        [smem] + [vmem] * 5,
        2 * patch_count * (3 * d_vit * 160 + 4 * patch_count * HEAD_VIT),
    )(
        core.reshape(1),
        patches,
        windows[:, None],
        windows[None, :],
        vit_gain[None, :],
        jnp.swapaxes(qkv_weight, 1, 2),
    )

    own_head = lax.dynamic_slice_in_dim(out_weight, core * HEAD_VIT, HEAD_VIT, 0)
    heads, context = ring_blocks(own_head, "tensor", context)
    order = sorted(heads)
    mine = [heads[k] for k in order]
    swap = [(i, i ^ 1) for i in range(owner_count)]
    laid = call(stack_kernel, jax.ShapeDtypeStruct((n, *own_head.shape), BF16), [vmem] * n, 0)(*mine)
    other = lax.ppermute(laid, "dp", swap)

    stacked = jnp.concatenate([gate_weight, up_weight, down_weight.T], axis=1)
    whole = lax.all_gather(stacked, "dp", axis=0, tiled=True)

    context, laid = lax.optimization_barrier((context, laid))
    got = ring_blocks(context, "tensor")

    video_rows = patch_count // 4
    seq_count = video_rows + audio.shape[0]
    capacity = 2 * seq_count // owner_count
    sent_lengths = span_lengths[owner]
    starts = jnp.cumsum(sent_lengths) - sent_lengths
    slot_index = jnp.arange(capacity, dtype=jnp.int32)
    row_of_slot = jnp.where(
        slot_index[None, :] < sent_lengths[:, None], starts[:, None] + slot_index[None, :], -1
    ).reshape(-1)
    row = jnp.arange(seq_count, dtype=jnp.int32)
    select = (row_of_slot[:, None] == row[None, video_rows:]).astype(BF16)
    from_audio = jnp.dot(select, audio, preferred_element_type=F32).astype(BF16)
    slots = owner_count * capacity
    width = audio.shape[1]
    outgoing = call(
        functools.partial(merge_kernel, n),
        jax.ShapeDtypeStruct((slots, width), BF16),
        [vmem] * (2 * n + 3) + [hbm, vmem, vmem],
        2 * patch_count * d_vit * (d_vit + width),
        scratch=[
            pltpu.VMEM((d_vit, patch_count), BF16),
            pltpu.VMEM((d_vit, d_vit), BF16),
            pltpu.VMEM((d_vit // 128, patch_count, 128), F32),
            pltpu.VMEM(merger_weight.shape[::-1], BF16),
            pltpu.SemaphoreType.DMA,
        ],
    )(
        *[got[k] for k in order],
        *mine,
        other,
        patches,
        merge_gain[None, :],
        merger_weight.T,
        row_of_slot[:, None],
        from_audio,
    )
    incoming = lax.all_to_all(
        outgoing.reshape(owner_count, capacity, width), "dp", split_axis=0, concat_axis=0, tiled=True
    ).reshape(slots, width)
    taken_lengths = span_lengths[:, owner]
    arrival = span_time[owner]
    earlier = arrival[:, None] < arrival[None, :]
    offsets = jnp.sum(jnp.where(earlier, taken_lengths[:, None], 0), axis=0)
    target = jnp.where(
        slot_index[None, :] < taken_lengths[:, None], offsets[:, None] + slot_index[None, :], -1
    ).reshape(1, -1)
    sequence = call(
        pick_kernel,
        jax.ShapeDtypeStruct((seq_count, width), BF16),
        [vmem] * 2,
        2 * slots * seq_count * width,
    )(target, incoming)

    got = ring_blocks(sequence, "tensor")
    features = n * width
    low = 2 * units // 256 * 256
    tail = (2 * units - low + 127) // 128 * 128
    own_count = seq_count // n
    terms, own_rows = call(
        functools.partial(ffn_kernel, n, tuple(order), units),
        (
            jax.ShapeDtypeStruct((seq_count, features), BF16),
            jax.ShapeDtypeStruct((n, own_count, width), BF16),
        ),
        [smem] + [vmem] * (n + 1) + [hbm],
        6 * seq_count * features * units,
        scratch=[
            pltpu.VMEM((features, 3 * units), BF16),
            pltpu.VMEM((n, seq_count, width), BF16),
            pltpu.VMEM((seq_count, low + tail), F32),
            pltpu.VMEM((seq_count, 3 * units - low), BF16),
            pltpu.SemaphoreType.DMA((low // 256 + 1,)),
        ],
        mib=60,
    )(
        plane.reshape(1),
        *[got[k] for k in order],
        llm_gain.reshape(n, 1, width),
        whole,
    )
    summed = lax.psum_scatter(terms, "tensor", scatter_dimension=0, tiled=True).astype(F32)
    own_rows = jnp.moveaxis(own_rows, 0, 1).reshape(own_count, features)
    return (own_rows.astype(F32) + summed).astype(BF16)


def solution(mesh):
    return jax.shard_map(
        body,
        mesh=mesh,
        in_specs=(
            P("dp", None),
            P("dp", None),
            P(),
            P(None, None, "tensor"),
            P("tensor", None),
            P(),
            P(None, "tensor"),
            P("dp", "tensor"),
            P(),
            P(),
            P(),
            P("dp", "tensor"),
            P("dp", "tensor"),
            P("tensor", "dp"),
        ),
        out_specs=P(("dp", "tensor"), None),
        check_vma=False,
    )
```

profile of v0, /device:TPU:1, one launch (start us, length us, event | category | flops | bytes accessed | tf_op | source)
XLA Modules:
  0.0 264.3 jit_solution(7145647126284879606)
XLA Ops:
  6.6 2.5 concatenate.3
  9.1 6.5 %collective-permute-start.2 = (bf16[80,1280]{1,0:T(8,128)(2,1)S(1)}, bf16[80,1280]{1,0:T(8,128)(2,1)}, u32[]{:S(2)}, u32[]{:S(2)}) collective-permute-start(bf16[80,1280]{1,0:T(8,128)(2,1)S(1)} %constant_dynamic-slice_fusion.1.refs_4_.refs_12_), channel_id=1, source_target_pairs={{0,7},{1,0},{2,1},{3,2},{4,3},{5,4},{6,5},{7,6},{8,15},{9,8},{10,9... | collective-permute-start | bytes 614408 | tf_op jit(solution)/shard_map/ppermute | solution.py:28
  15.6 3.7 %collective-permute-done.2.refs_5_.refs_13_ = bf16[80,1280]{1,0:T(8,128)(2,1)} collective-permute-done((bf16[80,1280]{1,0:T(8,128)(2,1)S(1)}, bf16[80,1280]{1,0:T(8,128)(2,1)}, u32[]{:S(2)}, u32[]{:S(2)}) %collective-permute-start.2) | collective-permute-done | bytes 204832 | tf_op jit(solution)/shard_map/ppermute | solution.py:28
  19.3 3.5 %collective-permute-start.3 = (bf16[80,1280]{1,0:T(8,128)(2,1)}, bf16[80,1280]{1,0:T(8,128)(2,1)}, u32[]{:S(2)}, u32[]{:S(2)}) collective-permute-start(bf16[80,1280]{1,0:T(8,128)(2,1)} %collective-permute-done.2.refs_5_.refs_13_), channel_id=1, source_target_pairs={{0,7},{1,0},{2,1},{3,2},{4,3},{5,4},{6,5},{7,6},{8,15},{9,8},{10,9... | collective-permute-start | bytes 614408 | tf_op jit(solution)/shard_map/ppermute | solution.py:28
  22.9 0.1 copy.22.column_ref
  23.1 3.6 %shard_map.136.refs_4_ = bf16[160,512]{1,0:T(8,128)(2,1)} custom-call(s32[1]{0:T(128)} %bitcast.2.core_ref, bf16[512,1280]{1,0:T(8,128)(2,1)S(1)} %copy-done.1, s32[512,1]{1,0:T(8,128)S(1)} %copy.22.column_ref, s32[1,512]{1,0:T(1,128)S(1)} %copy-done.3, f32[1,1280]{1,0:T(1,128)S(1)} %broadcast_in_dim.30.gain_ref, bf16[3,160,1280]{2,1,0:T(8,128)(2,1)S(1)} %bitcast.18), custom_call_target="tpu_custom_call" | custom-call | flops 796917760 | bytes 2548740 | tf_op jit(solution)/shard_map/pallas_call | solution.py:187
  26.7 2.3 collective-permute-done.1.refs_2_.refs_10_
  29.0 2.7 %collective-permute-start.6 = (bf16[80,1280]{1,0:T(8,128)(2,1)}, bf16[80,1280]{1,0:T(8,128)(2,1)S(1)}, u32[]{:S(2)}, u32[]{:S(2)}) collective-permute-start(bf16[80,1280]{1,0:T(8,128)(2,1)} %collective-permute-done.3.refs_6_.refs_14_), channel_id=1, source_target_pairs={{0,7},{1,0},{2,1},{3,2},{4,3},{5,4},{6,5},{7,6},{8,15},{9,8},{10,9... | collective-permute-start | bytes 614408 | tf_op jit(solution)/shard_map/ppermute | solution.py:28
  31.7 3.8 %collective-permute-done.4.refs_1_.refs_9_ = bf16[80,1280]{1,0:T(8,128)(2,1)S(1)} collective-permute-done((bf16[80,1280]{1,0:T(8,128)(2,1)}, bf16[80,1280]{1,0:T(8,128)(2,1)S(1)}, u32[]{:S(2)}, u32[]{:S(2)}) %collective-permute-start.4) | collective-permute-done | bytes 204832 | tf_op jit(solution)/shard_map/ppermute | solution.py:26
  35.4 6.2 %collective-permute-done.5.refs_0_.refs_8_ = bf16[80,1280]{1,0:T(8,128)(2,1)S(1)} collective-permute-done((bf16[80,1280]{1,0:T(8,128)(2,1)S(1)}, bf16[80,1280]{1,0:T(8,128)(2,1)S(1)}, u32[]{:S(2)}, u32[]{:S(2)}) %collective-permute-start.5) | collective-permute-done | bytes 204832 | tf_op jit(solution)/shard_map/ppermute | solution.py:26
  41.7 2.5 shard_map.137
  44.2 4.5 %collective-permute-start.14 = (bf16[8,80,1280]{2,1,0:T(8,128)(2,1)}, bf16[8,80,1280]{2,1,0:T(8,128)(2,1)}, u32[]{:S(2)}, u32[]{:S(2)}) collective-permute-start(bf16[8,80,1280]{2,1,0:T(8,128)(2,1)} %shard_map.137), channel_id=1, source_target_pairs={{0,8},{8,0},{16,24},{24,16},{32,40},{40,32},{48,56},{56,48},{64,72... | collective-permute-start | bytes 4915208 | tf_op jit(solution)/shard_map/ppermute | solution.py:248
  48.7 0.1 copy.23
  48.8 0.1 reduce.1
  48.9 2.7 %collective-permute-start.11 = (bf16[160,512]{1,0:T(8,128)(2,1)}, bf16[160,512]{1,0:T(8,128)(2,1)S(1)}, u32[]{:S(2)}, u32[]{:S(2)}) collective-permute-start(bf16[160,512]{1,0:T(8,128)(2,1)} %shard_map.136.refs_4_), channel_id=1, source_target_pairs={{0,7},{1,0},{2,1},{3,2},{4,3},{5,4},{6,5},{7,6},{8,15},{9,8},{10,9... | collective-permute-start | bytes 491528 | tf_op jit(solution)/shard_map/ppermute | solution.py:28
  51.7 4.2 %collective-permute-done.7.refs_3_ = bf16[160,512]{1,0:T(8,128)(2,1)S(1)} collective-permute-done((bf16[160,512]{1,0:T(8,128)(2,1)}, bf16[160,512]{1,0:T(8,128)(2,1)S(1)}, u32[]{:S(2)}, u32[]{:S(2)}) %collective-permute-start.7) | collective-permute-done | bytes 163872 | tf_op jit(solution)/shard_map/ppermute | solution.py:26
  55.9 2.9 %collective-permute-start.12 = (bf16[160,512]{1,0:T(8,128)(2,1)S(1)}, bf16[160,512]{1,0:T(8,128)(2,1)S(1)}, u32[]{:S(2)}, u32[]{:S(2)}) collective-permute-start(bf16[160,512]{1,0:T(8,128)(2,1)S(1)} %collective-permute-done.11.refs_5_), channel_id=1, source_target_pairs={{0,7},{1,0},{2,1},{3,2},{4,3},{5,4},{6,5},{7,6},{8,15},{9,8},{10,9... | collective-permute-start | bytes 491528 | tf_op jit(solution)/shard_map/ppermute | solution.py:28
  58.8 3.3 %collective-permute-done.8.refs_2_ = bf16[160,512]{1,0:T(8,128)(2,1)S(1)} collective-permute-done((bf16[160,512]{1,0:T(8,128)(2,1)S(1)}, bf16[160,512]{1,0:T(8,128)(2,1)S(1)}, u32[]{:S(2)}, u32[]{:S(2)}) %collective-permute-start.8) | collective-permute-done | bytes 163872 | tf_op jit(solution)/shard_map/ppermute | solution.py:26
  62.3 0.5 select_n.51.refs_20_
  62.9 2.7 %collective-permute-start.13 = (bf16[160,512]{1,0:T(8,128)(2,1)S(1)}, bf16[160,512]{1,0:T(8,128)(2,1)}, u32[]{:S(2)}, u32[]{:S(2)}) collective-permute-start(bf16[160,512]{1,0:T(8,128)(2,1)S(1)} %collective-permute-done.12.refs_6_), channel_id=1, source_target_pairs={{0,7},{1,0},{2,1},{3,2},{4,3},{5,4},{6,5},{7,6},{8,15},{9,8},{10,9... | collective-permute-start | bytes 491528 | tf_op jit(solution)/shard_map/ppermute | solution.py:28
  65.7 2.3 collective-permute-done.9.refs_1_
  67.9 1.7 fusion.2
  69.7 1.5 copy.25.refs_21_
  71.2 2.8 %collective-permute-done.10.refs_0_ = bf16[160,512]{1,0:T(8,128)(2,1)} collective-permute-done((bf16[160,512]{1,0:T(8,128)(2,1)}, bf16[160,512]{1,0:T(8,128)(2,1)}, u32[]{:S(2)}, u32[]{:S(2)}) %collective-permute-start.10) | collective-permute-done | bytes 163872 | tf_op jit(solution)/shard_map/ppermute | solution.py:26
  73.9 10.5 %shard_map.138 = bf16[1024,448]{1,0:T(8,128)(2,1)} custom-call(bf16[160,512]{1,0:T(8,128)(2,1)} %collective-permute-done.10.refs_0_, bf16[160,512]{1,0:T(8,128)(2,1)} %collective-permute-done.9.refs_1_, bf16[160,512]{1,0:T(8,128)(2,1)S(1)} %collective-permute-done.8.refs_2_, bf16[160,512]{1,0:T(8,128)(2,1)S(1)} %collective-permute-done.7.refs_3_, ...), custom_call_target="tpu_custom_call" | custom-call | flops 2264924160 | bytes 11412480 | tf_op jit(solution)/shard_map/pallas_call | solution.py:187
  84.5 10.6 %all-to-all-start = ((bf16[32,32,448]{2,1,0:T(8,128)(2,1)}), bf16[32,32,448]{2,1,0:T(8,128)(2,1)S(1)}, u32[]{:S(2)}, u32[]{:S(2)}) async-start(bf16[32,32,448]{2,1,0:T(8,128)(2,1)} %bitcast.8), calls=%async_computation | async-start | bytes 2097152 | tf_op jit(solution)/shard_map/all_to_all | solution.py:292
  95.1 0.2 dynamic-slice_reduce_fusion
  95.3 0.7 fusion.7
  95.9 0.1 select_reduce_fusion
  96.1 0.1 select_n.46.target_ref
  96.2 25.1 %all-to-all-done = bf16[32,32,448]{2,1,0:T(8,128)(2,1)S(1)} async-done(((bf16[32,32,448]{2,1,0:T(8,128)(2,1)}), bf16[32,32,448]{2,1,0:T(8,128)(2,1)S(1)}, u32[]{:S(2)}, u32[]{:S(2)}) %all-to-all-start) | async-done | bytes 917536 | tf_op jit(solution)/shard_map/all_to_all | solution.py:292
  121.3 0.7 shard_map.139.refs_4_
  122.0 0.1 collective-permute-start.15
  122.1 2.7 %collective-permute-start.19 = (bf16[512,448]{1,0:T(8,128)(2,1)S(1)}, bf16[512,448]{1,0:T(8,128)(2,1)S(1)}, u32[]{:S(2)}, u32[]{:S(2)}) collective-permute-start(bf16[512,448]{1,0:T(8,128)(2,1)S(1)} %shard_map.139.refs_4_), channel_id=1, source_target_pairs={{0,7},{1,0},{2,1},{3,2},{4,3},{5,4},{6,5},{7,6},{8,15},{9,8},{10,9... | collective-permute-start | bytes 1376264 | tf_op jit(solution)/shard_map/ppermute | solution.py:28
  124.8 9.6 %collective-permute-done.15.refs_3_ = bf16[512,448]{1,0:T(8,128)(2,1)S(1)} collective-permute-done((bf16[512,448]{1,0:T(8,128)(2,1)S(1)}, bf16[512,448]{1,0:T(8,128)(2,1)S(1)}, u32[]{:S(2)}, u32[]{:S(2)}) %collective-permute-start.15) | collective-permute-done | bytes 458784 | tf_op jit(solution)/shard_map/ppermute | solution.py:26
  134.4 2.7 %collective-permute-start.20 = (bf16[512,448]{1,0:T(8,128)(2,1)S(1)}, bf16[512,448]{1,0:T(8,128)(2,1)S(1)}, u32[]{:S(2)}, u32[]{:S(2)}) collective-permute-start(bf16[512,448]{1,0:T(8,128)(2,1)S(1)} %collective-permute-done.19.refs_5_), channel_id=1, source_target_pairs={{0,7},{1,0},{2,1},{3,2},{4,3},{5,4},{6,5},{7,6},{8,15},{9,8},{10,9... | collective-permute-start | bytes 1376264 | tf_op jit(solution)/shard_map/ppermute | solution.py:28
  137.0 8.6 %collective-permute-done.16.refs_2_ = bf16[512,448]{1,0:T(8,128)(2,1)S(1)} collective-permute-done((bf16[512,448]{1,0:T(8,128)(2,1)S(1)}, bf16[512,448]{1,0:T(8,128)(2,1)S(1)}, u32[]{:S(2)}, u32[]{:S(2)}) %collective-permute-start.16) | collective-permute-done | bytes 458784 | tf_op jit(solution)/shard_map/ppermute | solution.py:26
  145.7 2.7 %collective-permute-start.21 = (bf16[512,448]{1,0:T(8,128)(2,1)S(1)}, bf16[512,448]{1,0:T(8,128)(2,1)}, u32[]{:S(2)}, u32[]{:S(2)}) collective-permute-start(bf16[512,448]{1,0:T(8,128)(2,1)S(1)} %collective-permute-done.20.refs_6_), channel_id=1, source_target_pairs={{0,7},{1,0},{2,1},{3,2},{4,3},{5,4},{6,5},{7,6},{8,15},{9,8},{10,9... | collective-permute-start | bytes 1376264 | tf_op jit(solution)/shard_map/ppermute | solution.py:28
  148.4 7.8 %collective-permute-done.17.refs_1_ = bf16[512,448]{1,0:T(8,128)(2,1)} collective-permute-done((bf16[512,448]{1,0:T(8,128)(2,1)S(1)}, bf16[512,448]{1,0:T(8,128)(2,1)}, u32[]{:S(2)}, u32[]{:S(2)}) %collective-permute-start.17) | collective-permute-done | bytes 458784 | tf_op jit(solution)/shard_map/ppermute | solution.py:26
  156.2 0.7 reshape.164.refs_8_
  156.9 9.7 %collective-permute-done.18.refs_0_ = bf16[512,448]{1,0:T(8,128)(2,1)} collective-permute-done((bf16[512,448]{1,0:T(8,128)(2,1)}, bf16[512,448]{1,0:T(8,128)(2,1)}, u32[]{:S(2)}, u32[]{:S(2)}) %collective-permute-start.18) | collective-permute-done | bytes 458784 | tf_op jit(solution)/shard_map/ppermute | solution.py:26
  166.6 28.3 %shard_map.140 = (bf16[512,3584]{1,0:T(8,128)(2,1)}, bf16[8,64,448]{2,1,0:T(8,128)(2,1)}) custom-call(s32[1]{0:T(128)} %bitcast.place_ref, bf16[512,448]{1,0:T(8,128)(2,1)} %collective-permute-done.18.refs_0_, bf16[512,448]{1,0:T(8,128)(2,1)} %collective-permute-done.17.refs_1_, bf16[512,448]{1,0:T(8,128)(2,1)} %copy-done.12, bf16[512,448]{1,0:T(8,128)(2,1)} %copy-done.10, ...), custom_call_target="tpu_custom_call" | custom-call | flops 13035896832 | bytes 29145092 | tf_op jit(solution)/shard_map/pallas_call | solution.py:187
  194.9 1.0 copy-done.5
  195.9 0.1 convert_bitcast_fusion
  196.1 0.6 copy.26
  196.7 0.4 reshape.165
  197.1 58.5 %reduce-scatter.2.cloned.1.call-done = bf16[64,3584]{1,0:T(8,128)(2,1)} async-done(((bf16[512,3584]{1,0:T(8,128)(2,1)}), bf16[64,3584]{1,0:T(8,128)(2,1)}) %reduce-scatter.2.cloned.1.call-update) | async-done | bytes 458768 | tf_op jit(solution)/shard_map/reduce_scatter | solution.py:336
  255.6 1.9 add_convert_fusion
  (66 shorter events, 0.6 us)
Async XLA Ops:
  6.5 2.5 copy-start
  6.5 16.3 %copy-start.8 = (f32[1280]{0:T(1024)S(1)}, f32[1280]{0:T(1024)}, u32[]{:S(2)}) copy-start(f32[1280]{0:T(1024)} %param.16) | copy-start | bytes 15364
  6.5 16.4 %copy-start.3 = (s32[1,512]{1,0:T(1,128)S(1)}, s32[1,512]{1,0:T(1,128)}, u32[]{:S(2)}) copy-start(s32[1,512]{1,0:T(1,128)} %row_ref.1) | copy-start | bytes 6148
  6.5 16.5 %copy-start.1 = (bf16[512,1280]{1,0:T(8,128)(2,1)S(1)}, bf16[512,1280]{1,0:T(8,128)(2,1)}, u32[]{:S(2)}) copy-start(bf16[512,1280]{1,0:T(8,128)(2,1)} %refs_17_.1) | copy-start | bytes 3932164
  6.5 16.5 %copy-start.2 = (bf16[3,1280,160]{1,2,0:T(8,128)(2,1)S(1)}, bf16[3,1280,160]{1,2,0:T(8,128)(2,1)}, u32[]{:S(2)}) copy-start(bf16[3,1280,160]{1,2,0:T(8,128)(2,1)} %param.17) | copy-start | bytes 3686404
  6.5 160.0 %all-gather.2.cloned.1.call-start = ((), (), s32[]{:S(2)}) async-start(), calls=%async_computation.2 | async-start | bytes 26492928 | tf_op jit(solution)/shard_map/all_gather | solution.py:251
  9.1 10.2 %collective-permute-start.2 = (bf16[80,1280]{1,0:T(8,128)(2,1)S(1)}, bf16[80,1280]{1,0:T(8,128)(2,1)}, u32[]{:S(2)}, u32[]{:S(2)}) collective-permute-start(bf16[80,1280]{1,0:T(8,128)(2,1)S(1)} %constant_dynamic-slice_fusion.1.refs_4_.refs_12_), channel_id=1, source_target_pairs={{0,7},{1,0},{2,1},{3,2},{4,3},{5,4},{6,5},{7,6},{8,15},{9,8},{10,9... | collective-permute-start | bytes 614408 | tf_op jit(solution)/shard_map/ppermute | solution.py:28
  15.6 7.3 %collective-permute-start = (bf16[80,1280]{1,0:T(8,128)(2,1)S(1)}, bf16[80,1280]{1,0:T(8,128)(2,1)}, u32[]{:S(2)}, u32[]{:S(2)}) collective-permute-start(bf16[80,1280]{1,0:T(8,128)(2,1)S(1)} %constant_dynamic-slice_fusion.1.refs_4_.refs_12_), channel_id=1, source_target_pairs={{0,1},{1,2},{2,3},{3,4},{4,5},{5,6},{6,7},{7,0},{8,9},{9,10},{10,1... | collective-permute-start | bytes 614408 | tf_op jit(solution)/shard_map/ppermute | solution.py:26
  19.3 7.4 %collective-permute-start.3 = (bf16[80,1280]{1,0:T(8,128)(2,1)}, bf16[80,1280]{1,0:T(8,128)(2,1)}, u32[]{:S(2)}, u32[]{:S(2)}) collective-permute-start(bf16[80,1280]{1,0:T(8,128)(2,1)} %collective-permute-done.2.refs_5_.refs_13_), channel_id=1, source_target_pairs={{0,7},{1,0},{2,1},{3,2},{4,3},{5,4},{6,5},{7,6},{8,15},{9,8},{10,9... | collective-permute-start | bytes 614408 | tf_op jit(solution)/shard_map/ppermute | solution.py:28
  22.9 6.1 %collective-permute-start.1 = (bf16[80,1280]{1,0:T(8,128)(2,1)}, bf16[80,1280]{1,0:T(8,128)(2,1)}, u32[]{:S(2)}, u32[]{:S(2)}) collective-permute-start(bf16[80,1280]{1,0:T(8,128)(2,1)} %collective-permute-done.refs_3_.refs_11_), channel_id=1, source_target_pairs={{0,1},{1,2},{2,3},{3,4},{4,5},{5,6},{6,7},{7,0},{8,9},{9,10},{10,1... | collective-permute-start | bytes 614408 | tf_op jit(solution)/shard_map/ppermute | solution.py:26
  26.7 22.0 %copy-start.6 = (s32[32,32]{1,0:T(8,128)S(1)}, s32[32,32]{1,0:T(8,128)}, u32[]{:S(2)}) copy-start(s32[32,32]{1,0:T(8,128)} %param.22) | copy-start | bytes 12292
  26.7 36.2 %copy-start.9 = (f32[1280]{0:T(1024)S(1)}, f32[1280]{0:T(1024)}, u32[]{:S(2)}) copy-start(f32[1280]{0:T(1024)} %param.19) | copy-start | bytes 15364
  26.7 41.2 %copy-start.14 = (bf16[384,448]{0,1:T(8,128)(2,1)S(1)}, bf16[384,448]{0,1:T(8,128)(2,1)}, u32[]{:S(2)}) copy-start(bf16[384,448]{0,1:T(8,128)(2,1)} %param.21) | copy-start | bytes 1032196
  29.0 6.4 %collective-permute-start.4 = (bf16[80,1280]{1,0:T(8,128)(2,1)}, bf16[80,1280]{1,0:T(8,128)(2,1)S(1)}, u32[]{:S(2)}, u32[]{:S(2)}) collective-permute-start(bf16[80,1280]{1,0:T(8,128)(2,1)} %collective-permute-done.1.refs_2_.refs_10_), channel_id=1, source_target_pairs={{0,1},{1,2},{2,3},{3,4},{4,5},{5,6},{6,7},{7,0},{8,9},{9,10},{10,1... | collective-permute-start | bytes 614408 | tf_op jit(solution)/shard_map/ppermute | solution.py:26
  29.0 6.4 %collective-permute-start.6 = (bf16[80,1280]{1,0:T(8,128)(2,1)}, bf16[80,1280]{1,0:T(8,128)(2,1)S(1)}, u32[]{:S(2)}, u32[]{:S(2)}) collective-permute-start(bf16[80,1280]{1,0:T(8,128)(2,1)} %collective-permute-done.3.refs_6_.refs_14_), channel_id=1, source_target_pairs={{0,7},{1,0},{2,1},{3,2},{4,3},{5,4},{6,5},{7,6},{8,15},{9,8},{10,9... | collective-permute-start | bytes 614408 | tf_op jit(solution)/shard_map/ppermute | solution.py:28
  35.4 6.2 %collective-permute-start.5 = (bf16[80,1280]{1,0:T(8,128)(2,1)S(1)}, bf16[80,1280]{1,0:T(8,128)(2,1)S(1)}, u32[]{:S(2)}, u32[]{:S(2)}) collective-permute-start(bf16[80,1280]{1,0:T(8,128)(2,1)S(1)} %collective-permute-done.4.refs_1_.refs_9_), channel_id=1, source_target_pairs={{0,1},{1,2},{2,3},{3,4},{4,5},{5,6},{6,7},{7,0},{8,9},{9,10},{10,1... | collective-permute-start | bytes 614408 | tf_op jit(solution)/shard_map/ppermute | solution.py:26
  44.2 29.8 %collective-permute-start.14 = (bf16[8,80,1280]{2,1,0:T(8,128)(2,1)}, bf16[8,80,1280]{2,1,0:T(8,128)(2,1)}, u32[]{:S(2)}, u32[]{:S(2)}) collective-permute-start(bf16[8,80,1280]{2,1,0:T(8,128)(2,1)} %shard_map.137), channel_id=1, source_target_pairs={{0,8},{8,0},{16,24},{24,16},{32,40},{40,32},{48,56},{56,48},{64,72... | collective-permute-start | bytes 4915208 | tf_op jit(solution)/shard_map/ppermute | solution.py:248
  48.6 7.3 %collective-permute-start.7 = (bf16[160,512]{1,0:T(8,128)(2,1)}, bf16[160,512]{1,0:T(8,128)(2,1)S(1)}, u32[]{:S(2)}, u32[]{:S(2)}) collective-permute-start(bf16[160,512]{1,0:T(8,128)(2,1)} %shard_map.136.refs_4_), channel_id=1, source_target_pairs={{0,1},{1,2},{2,3},{3,4},{4,5},{5,6},{6,7},{7,0},{8,9},{9,10},{10,1... | collective-permute-start | bytes 491528 | tf_op jit(solution)/shard_map/ppermute | solution.py:26
  48.9 7.0 %collective-permute-start.11 = (bf16[160,512]{1,0:T(8,128)(2,1)}, bf16[160,512]{1,0:T(8,128)(2,1)S(1)}, u32[]{:S(2)}, u32[]{:S(2)}) collective-permute-start(bf16[160,512]{1,0:T(8,128)(2,1)} %shard_map.136.refs_4_), channel_id=1, source_target_pairs={{0,7},{1,0},{2,1},{3,2},{4,3},{5,4},{6,5},{7,6},{8,15},{9,8},{10,9... | collective-permute-start | bytes 491528 | tf_op jit(solution)/shard_map/ppermute | solution.py:28
  55.9 6.3 %collective-permute-start.8 = (bf16[160,512]{1,0:T(8,128)(2,1)S(1)}, bf16[160,512]{1,0:T(8,128)(2,1)S(1)}, u32[]{:S(2)}, u32[]{:S(2)}) collective-permute-start(bf16[160,512]{1,0:T(8,128)(2,1)S(1)} %collective-permute-done.7.refs_3_), channel_id=1, source_target_pairs={{0,1},{1,2},{2,3},{3,4},{4,5},{5,6},{6,7},{7,0},{8,9},{9,10},{10,1... | collective-permute-start | bytes 491528 | tf_op jit(solution)/shard_map/ppermute | solution.py:26
  55.9 7.0 %collective-permute-start.12 = (bf16[160,512]{1,0:T(8,128)(2,1)S(1)}, bf16[160,512]{1,0:T(8,128)(2,1)S(1)}, u32[]{:S(2)}, u32[]{:S(2)}) collective-permute-start(bf16[160,512]{1,0:T(8,128)(2,1)S(1)} %collective-permute-done.11.refs_5_), channel_id=1, source_target_pairs={{0,7},{1,0},{2,1},{3,2},{4,3},{5,4},{6,5},{7,6},{8,15},{9,8},{10,9... | collective-permute-start | bytes 491528 | tf_op jit(solution)/shard_map/ppermute | solution.py:28
  62.2 5.8 %collective-permute-start.9 = (bf16[160,512]{1,0:T(8,128)(2,1)S(1)}, bf16[160,512]{1,0:T(8,128)(2,1)}, u32[]{:S(2)}, u32[]{:S(2)}) collective-permute-start(bf16[160,512]{1,0:T(8,128)(2,1)S(1)} %collective-permute-done.8.refs_2_), channel_id=1, source_target_pairs={{0,1},{1,2},{2,3},{3,4},{4,5},{5,6},{6,7},{7,0},{8,9},{9,10},{10,1... | collective-permute-start | bytes 491528 | tf_op jit(solution)/shard_map/ppermute | solution.py:26
  62.9 8.2 %collective-permute-start.13 = (bf16[160,512]{1,0:T(8,128)(2,1)S(1)}, bf16[160,512]{1,0:T(8,128)(2,1)}, u32[]{:S(2)}, u32[]{:S(2)}) collective-permute-start(bf16[160,512]{1,0:T(8,128)(2,1)S(1)} %collective-permute-done.12.refs_6_), channel_id=1, source_target_pairs={{0,7},{1,0},{2,1},{3,2},{4,3},{5,4},{6,5},{7,6},{8,15},{9,8},{10,9... | collective-permute-start | bytes 491528 | tf_op jit(solution)/shard_map/ppermute | solution.py:28
  67.9 6.0 %collective-permute-start.10 = (bf16[160,512]{1,0:T(8,128)(2,1)}, bf16[160,512]{1,0:T(8,128)(2,1)}, u32[]{:S(2)}, u32[]{:S(2)}) collective-permute-start(bf16[160,512]{1,0:T(8,128)(2,1)} %collective-permute-done.9.refs_1_), channel_id=1, source_target_pairs={{0,1},{1,2},{2,3},{3,4},{4,5},{5,6},{6,7},{7,0},{8,9},{9,10},{10,1... | collective-permute-start | bytes 491528 | tf_op jit(solution)/shard_map/ppermute | solution.py:26
  84.4 71.7 %copy-start.7 = (f32[3584]{0:T(1024)S(1)}, f32[3584]{0:T(1024)}, u32[]{:S(2)}) copy-start(f32[3584]{0:T(1024)} %param.24) | copy-start | bytes 43012
  84.5 36.8 %all-to-all-start = ((bf16[32,32,448]{2,1,0:T(8,128)(2,1)}), bf16[32,32,448]{2,1,0:T(8,128)(2,1)S(1)}, u32[]{:S(2)}, u32[]{:S(2)}) async-start(bf16[32,32,448]{2,1,0:T(8,128)(2,1)} %bitcast.8), calls=%async_computation | async-start | bytes 2097152 | tf_op jit(solution)/shard_map/all_to_all | solution.py:292
  95.0 160.6 %reduce-scatter.2.cloned.1.call-start = ((), (), s32[]{:S(2)}) async-start(), calls=%async_computation.3 | async-start | bytes 4128768 | tf_op jit(solution)/shard_map/reduce_scatter | solution.py:336
  122.0 44.6 %copy-start.4 = (bf16[512,448]{1,0:T(8,128)(2,1)}, bf16[512,448]{1,0:T(8,128)(2,1)S(1)}, u32[]{:S(2)}) copy-start(bf16[512,448]{1,0:T(8,128)(2,1)S(1)} %shard_map.139.refs_4_) | copy-start | bytes 1376260
  122.0 12.3 %collective-permute-start.15 = (bf16[512,448]{1,0:T(8,128)(2,1)S(1)}, bf16[512,448]{1,0:T(8,128)(2,1)S(1)}, u32[]{:S(2)}, u32[]{:S(2)}) collective-permute-start(bf16[512,448]{1,0:T(8,128)(2,1)S(1)} %shard_map.139.refs_4_), channel_id=1, source_target_pairs={{0,1},{1,2},{2,3},{3,4},{4,5},{5,6},{6,7},{7,0},{8,9},{9,10},{10,1... | collective-permute-start | bytes 1376264 | tf_op jit(solution)/shard_map/ppermute | solution.py:26
  122.1 12.2 %collective-permute-start.19 = (bf16[512,448]{1,0:T(8,128)(2,1)S(1)}, bf16[512,448]{1,0:T(8,128)(2,1)S(1)}, u32[]{:S(2)}, u32[]{:S(2)}) collective-permute-start(bf16[512,448]{1,0:T(8,128)(2,1)S(1)} %shard_map.139.refs_4_), channel_id=1, source_target_pairs={{0,7},{1,0},{2,1},{3,2},{4,3},{5,4},{6,5},{7,6},{8,15},{9,8},{10,9... | collective-permute-start | bytes 1376264 | tf_op jit(solution)/shard_map/ppermute | solution.py:28
  134.3 32.2 %copy-start.10 = (bf16[512,448]{1,0:T(8,128)(2,1)}, bf16[512,448]{1,0:T(8,128)(2,1)S(1)}, u32[]{:S(2)}) copy-start(bf16[512,448]{1,0:T(8,128)(2,1)S(1)} %collective-permute-done.15.refs_3_) | copy-start | bytes 1376260
  134.3 11.3 %collective-permute-start.16 = (bf16[512,448]{1,0:T(8,128)(2,1)S(1)}, bf16[512,448]{1,0:T(8,128)(2,1)S(1)}, u32[]{:S(2)}, u32[]{:S(2)}) collective-permute-start(bf16[512,448]{1,0:T(8,128)(2,1)S(1)} %collective-permute-done.15.refs_3_), channel_id=1, source_target_pairs={{0,1},{1,2},{2,3},{3,4},{4,5},{5,6},{6,7},{7,0},{8,9},{9,10},{10,1... | collective-permute-start | bytes 1376264 | tf_op jit(solution)/shard_map/ppermute | solution.py:26
  134.3 32.2 %copy-start.11 = (bf16[512,448]{1,0:T(8,128)(2,1)}, bf16[512,448]{1,0:T(8,128)(2,1)S(1)}, u32[]{:S(2)}) copy-start(bf16[512,448]{1,0:T(8,128)(2,1)S(1)} %collective-permute-done.19.refs_5_) | copy-start | bytes 1376260
  134.4 11.3 %collective-permute-start.20 = (bf16[512,448]{1,0:T(8,128)(2,1)S(1)}, bf16[512,448]{1,0:T(8,128)(2,1)S(1)}, u32[]{:S(2)}, u32[]{:S(2)}) collective-permute-start(bf16[512,448]{1,0:T(8,128)(2,1)S(1)} %collective-permute-done.19.refs_5_), channel_id=1, source_target_pairs={{0,7},{1,0},{2,1},{3,2},{4,3},{5,4},{6,5},{7,6},{8,15},{9,8},{10,9... | collective-permute-start | bytes 1376264 | tf_op jit(solution)/shard_map/ppermute | solution.py:28
  145.7 20.9 %copy-start.12 = (bf16[512,448]{1,0:T(8,128)(2,1)}, bf16[512,448]{1,0:T(8,128)(2,1)S(1)}, u32[]{:S(2)}) copy-start(bf16[512,448]{1,0:T(8,128)(2,1)S(1)} %collective-permute-done.16.refs_2_) | copy-start | bytes 1376260
  145.7 10.5 %collective-permute-start.17 = (bf16[512,448]{1,0:T(8,128)(2,1)S(1)}, bf16[512,448]{1,0:T(8,128)(2,1)}, u32[]{:S(2)}, u32[]{:S(2)}) collective-permute-start(bf16[512,448]{1,0:T(8,128)(2,1)S(1)} %collective-permute-done.16.refs_2_), channel_id=1, source_target_pairs={{0,1},{1,2},{2,3},{3,4},{4,5},{5,6},{6,7},{7,0},{8,9},{9,10},{10,1... | collective-permute-start | bytes 1376264 | tf_op jit(solution)/shard_map/ppermute | solution.py:26
  145.7 20.9 %copy-start.13 = (bf16[512,448]{1,0:T(8,128)(2,1)}, bf16[512,448]{1,0:T(8,128)(2,1)S(1)}, u32[]{:S(2)}) copy-start(bf16[512,448]{1,0:T(8,128)(2,1)S(1)} %collective-permute-done.20.refs_6_) | copy-start | bytes 1376260
  145.7 11.2 %collective-permute-start.21 = (bf16[512,448]{1,0:T(8,128)(2,1)S(1)}, bf16[512,448]{1,0:T(8,128)(2,1)}, u32[]{:S(2)}, u32[]{:S(2)}) collective-permute-start(bf16[512,448]{1,0:T(8,128)(2,1)S(1)} %collective-permute-done.20.refs_6_), channel_id=1, source_target_pairs={{0,7},{1,0},{2,1},{3,2},{4,3},{5,4},{6,5},{7,6},{8,15},{9,8},{10,9... | collective-permute-start | bytes 1376264 | tf_op jit(solution)/shard_map/ppermute | solution.py:28
  156.2 10.4 %collective-permute-start.18 = (bf16[512,448]{1,0:T(8,128)(2,1)}, bf16[512,448]{1,0:T(8,128)(2,1)}, u32[]{:S(2)}, u32[]{:S(2)}) collective-permute-start(bf16[512,448]{1,0:T(8,128)(2,1)} %collective-permute-done.17.refs_1_), channel_id=1, source_target_pairs={{0,1},{1,2},{2,3},{3,4},{4,5},{5,6},{6,7},{7,0},{8,9},{9,10},{10,1... | collective-permute-start | bytes 1376264 | tf_op jit(solution)/shard_map/ppermute | solution.py:26
  194.9 1.0 copy-start.5
Sparse Core Ops, SparseCore 0:
  9.9 113.4 all-gather.1
  195.1 60.4 reduce-scatter.1
where the time goes:
time: 265 us; the launch traced here: 264 us
  waiting for transfers between devices  148 us (56%)
  Pallas kernels  45.6 us (17%)
  starting transfers between devices  44.3 us (17%)
  between operations  13.7 us (5%)
  local copies, waits for them, and re-layouts  8.54 us (3%)
    ppermute x12, waiting for transfers between devices, ring_blocks(): a = lax.ppermute(a, axis, up)  60.6 us
    reduce_scatter x1, waiting for transfers between devices, body(): lax.psum_scatter(terms, 'tensor', scatter_dimension=0, tiled=True)  58.5 us
    pallas_call x5, Pallas kernels, run(): pl.pallas_call(kernel, out_shape=out_shape, in_specs=specs, out_specs=jax...  45.6 us
    ppermute x9, starting transfers between devices, ring_blocks(): b = lax.ppermute(b, axis, down)  29.1 us
    all_to_all x1, waiting for transfers between devices, body(): lax.all_to_all(outgoing.reshape(owner_count, capacity, width), 'dp', spli...  25.1 us
    all_to_all x1, starting transfers between devices, body(): lax.all_to_all(outgoing.reshape(owner_count, capacity, width), 'dp', spli...  10.6 us
  transfers between devices with their start and end apart: 25, of which 14 were waited for; matrix products, arithmetic and copies ran while one was open for 3% of the time, Pallas kernels for 7%

commit v1 on v0

--- a/solution.py
+++ b/solution.py
@@ -16,22 +16,22 @@
 F32 = jnp.float32
 
 
-def ring_blocks(x, axis, beside=None, rounds_first=2):
+def shifted(axis, step):
     n = lax.axis_size(axis)
-    up = [(i, (i + 1) % n) for i in range(n)]
-    down = [(i, (i - 1) % n) for i in range(n)]
+    return [(i, (i + step) % n) for i in range(n)]
+
+
+def ring_blocks(x, axis):
+    n = lax.axis_size(axis)
     blocks = {0: x}
     a = b = x
     for k in range(1, n // 2 + 1):
-        a = lax.ppermute(a, axis, up)
-        if k < n - n // 2:
-            b = lax.ppermute(b, axis, down)
-        if beside is not None and k == rounds_first:
-            a, b, beside = lax.optimization_barrier((a, b, beside))
+        a = lax.ppermute(a, axis, shifted(axis, 1))
         blocks[-k] = a
         if k < n - n // 2:
+            b = lax.ppermute(b, axis, shifted(axis, -1))
             blocks[k] = b
-    return blocks if beside is None else (blocks, beside)
+    return blocks
 
 
 def turned_dot(left, right):
@@ -62,21 +62,53 @@
         out_ref[pl.ds(place, HEAD_VIT), :] = context.astype(BF16)
 
 
-def stack_kernel(*refs):
-    for k, ref in enumerate(refs[:-1]):
-        refs[-1][k] = ref[...]
+def lay(into, at, wide):
+    rows, columns = wide.shape
+    for j in range(columns // 128):
+        into[pl.ds(at + j * rows, rows), :] = wide[:, pl.ds(j * 128, 128)]
+
+
+def spread(into, at, tall, start, rows):
+    for j in range(into.shape[1] // 128):
+        into[pl.ds(at, rows), pl.ds(j * 128, 128)] = tall[pl.ds(start + j * rows, rows), :]
+
+
+def pack_kernel(context_ref, above_ref, below_ref, up_ref, down_ref):
+    split = context_ref.size // 128
+    for out_ref, block_ref in ((up_ref, above_ref), (down_ref, below_ref)):
+        lay(out_ref, 0, context_ref)
+        lay(out_ref, split, block_ref)
+
+
+def stack_kernel(wide_count, *refs):
+    blocks, out_ref = refs[:-1], refs[-1]
+    rows = out_ref.shape[1]
+    for k, ref in enumerate(blocks):
+        if k < wide_count:
+            lay(out_ref.at[k], 0, ref)
+        else:
+            out_ref[k] = ref[pl.ds(ref.shape[0] - rows, rows), :]
 
 
 def merge_kernel(n, *refs):
-    contexts, mine = refs[:n], refs[n : 2 * n]
-    other_ref, patches_ref, gain_ref, merger_hbm, slot_ref, audio_ref, out_ref = refs[2 * n : 2 * n + 7]
-    context, weight, normed, merger, sem = refs[2 * n + 7 :]
+    contexts, wide, tall = refs[:n], refs[n : n + 3], refs[n + 3 : 2 * n]
+    other_ref, last_ref = refs[2 * n : 2 * n + 2]
+    patches_ref, gain_ref, merger_hbm, slot_ref, audio_ref, out_ref = refs[2 * n + 2 : 2 * n + 8]
+    context, weight, normed, merger, sem = refs[2 * n + 8 :]
     fetch = pltpu.make_async_copy(merger_hbm, merger, sem)
     fetch.start()
+    group = 2 * HEAD_VIT
+    split = group * context.shape[1] // 128
     for k in range(n):
-        context[pl.ds(k * 2 * HEAD_VIT, 2 * HEAD_VIT), :] = contexts[k][...]
-        weight[pl.ds(k * 2 * HEAD_VIT, HEAD_VIT), :] = mine[k][...]
-        weight[pl.ds((2 * k + 1) * HEAD_VIT, HEAD_VIT), :] = other_ref[k]
+        spread(context, k * group, contexts[k], 0, group)
+        if k < 3:
+            weight[pl.ds(k * group, HEAD_VIT), :] = wide[k][...]
+        else:
+            spread(weight, k * group, tall[k - 3], split, HEAD_VIT)
+        if k < n - 1:
+            spread(weight, k * group + HEAD_VIT, other_ref.at[k], 0, HEAD_VIT)
+        else:
+            spread(weight, k * group + HEAD_VIT, last_ref, split, HEAD_VIT)
     rows, d_vit = patches_ref.shape
     turned = context[...].T
 
@@ -106,10 +138,14 @@
     out_ref[...] = (placed + audio_ref[...].astype(F32)).astype(BF16)
 
 
-def pick_kernel(target_ref, incoming_ref, out_ref):
-    rows = lax.broadcasted_iota(jnp.int32, (out_ref.shape[0], incoming_ref.shape[0]), 0)
-    pick = (rows == target_ref[...]).astype(F32).astype(BF16)
-    out_ref[...] = jnp.dot(pick, incoming_ref[...], preferred_element_type=F32).astype(BF16)
+def pick_kernel(n, target_ref, incoming_ref, *outs):
+    count = len(outs)
+    for k, out_ref in enumerate(outs):
+        run = out_ref.shape[0] // n
+        row = lax.broadcasted_iota(jnp.int32, (out_ref.shape[0], incoming_ref.shape[0]), 0)
+        position = row // run * (run * count) + k * run + row % run
+        pick = (position == target_ref[...]).astype(F32).astype(BF16)
+        out_ref[...] = jnp.dot(pick, incoming_ref[...], preferred_element_type=F32).astype(BF16)
 
 
 def ffn_kernel(n, shifts, units, place_ref, *refs):
@@ -239,19 +275,40 @@
         jnp.swapaxes(qkv_weight, 1, 2),
     )
 
+    group = 2 * HEAD_VIT
     own_head = lax.dynamic_slice_in_dim(out_weight, core * HEAD_VIT, HEAD_VIT, 0)
-    heads, context = ring_blocks(own_head, "tensor", context)
-    order = sorted(heads)
-    mine = [heads[k] for k in order]
+    above = lax.ppermute(own_head, "tensor", shifted("tensor", 1))
+    below = lax.ppermute(own_head, "tensor", shifted("tensor", -1))
+    split, block_rows = group * patch_count // 128, HEAD_VIT * d_vit // 128
+    payload = jax.ShapeDtypeStruct((split + block_rows, 128), BF16)
+    up, down = call(pack_kernel, (payload, payload), [vmem] * 3, 0)(context, above, below)
+    ups, downs = [up], [down]
+    for k in range(1, n // 2):
+        ups.append(lax.ppermute(ups[-1], "tensor", shifted("tensor", 1)))
+        away = downs[-1] if k < n // 2 - 1 else downs[-1][:split]
+        downs.append(lax.ppermute(away, "tensor", shifted("tensor", -1)))
+    ups.append(lax.ppermute(ups[-1][:split], "tensor", shifted("tensor", 1)))
+    contexts = [up]
+    tall = []
+    for k in range(1, n // 2 + 1):
+        contexts.append(ups[k])
+        if k < n // 2:
+            contexts.append(downs[k])
+            tall.append(ups[k])
+        if k < n // 2 - 1:
+            tall.append(downs[k])
     swap = [(i, i ^ 1) for i in range(owner_count)]
-    laid = call(stack_kernel, jax.ShapeDtypeStruct((n, *own_head.shape), BF16), [vmem] * n, 0)(*mine)
+    laid = call(
+        functools.partial(stack_kernel, 3),
+        jax.ShapeDtypeStruct((n - 1, block_rows, 128), BF16),
+        [vmem] * (n - 1),
+        0,
+    )(own_head, above, below, *tall[:-1])
     other = lax.ppermute(laid, "dp", swap)
+    last = lax.ppermute(tall[-1], "dp", swap)
 
     stacked = jnp.concatenate([gate_weight, up_weight, down_weight.T], axis=1)
     whole = lax.all_gather(stacked, "dp", axis=0, tiled=True)
-
-    context, laid = lax.optimization_barrier((context, laid))
-    got = ring_blocks(context, "tensor")
 
     video_rows = patch_count // 4
     seq_count = video_rows + audio.shape[0]
@@ -270,7 +327,7 @@
     outgoing = call(
         functools.partial(merge_kernel, n),
         jax.ShapeDtypeStruct((slots, width), BF16),
-        [vmem] * (2 * n + 3) + [hbm, vmem, vmem],
+        [vmem] * (2 * n + 4) + [hbm, vmem, vmem],
         2 * patch_count * d_vit * (d_vit + width),
         scratch=[
             pltpu.VMEM((d_vit, patch_count), BF16),
@@ -280,9 +337,13 @@
             pltpu.SemaphoreType.DMA,
         ],
     )(
-        *[got[k] for k in order],
-        *mine,
+        *contexts,
+        own_head,
+        above,
+        below,
+        *tall,
         other,
+        last,
         patches,
         merge_gain[None, :],
         merger_weight.T,
@@ -299,43 +360,48 @@
     target = jnp.where(
         slot_index[None, :] < taken_lengths[:, None], offsets[:, None] + slot_index[None, :], -1
     ).reshape(1, -1)
+    parts = 2
+    part_rows = seq_count // parts
     sequence = call(
-        pick_kernel,
-        jax.ShapeDtypeStruct((seq_count, width), BF16),
+        functools.partial(pick_kernel, n),
+        (jax.ShapeDtypeStruct((part_rows, width), BF16),) * parts,
         [vmem] * 2,
         2 * slots * seq_count * width,
     )(target, incoming)
 
-    got = ring_blocks(sequence, "tensor")
     features = n * width
     low = 2 * units // 256 * 256
     tail = (2 * units - low + 127) // 128 * 128
-    own_count = seq_count // n
-    terms, own_rows = call(
-        functools.partial(ffn_kernel, n, tuple(order), units),
-        (
-            jax.ShapeDtypeStruct((seq_count, features), BF16),
-            jax.ShapeDtypeStruct((n, own_count, width), BF16),
-        ),
-        [smem] + [vmem] * (n + 1) + [hbm],
-        6 * seq_count * features * units,
-        scratch=[
-            pltpu.VMEM((features, 3 * units), BF16),
-            pltpu.VMEM((n, seq_count, width), BF16),
-            pltpu.VMEM((seq_count, low + tail), F32),
-            pltpu.VMEM((seq_count, 3 * units - low), BF16),
-            pltpu.SemaphoreType.DMA((low // 256 + 1,)),
-        ],
-        mib=60,
-    )(
-        plane.reshape(1),
-        *[got[k] for k in order],
-        llm_gain.reshape(n, 1, width),
-        whole,
-    )
-    summed = lax.psum_scatter(terms, "tensor", scatter_dimension=0, tiled=True).astype(F32)
-    own_rows = jnp.moveaxis(own_rows, 0, 1).reshape(own_count, features)
-    return (own_rows.astype(F32) + summed).astype(BF16)
+    own_count = part_rows // n
+    results = []
+    waiting = list(sequence)
+    for k in range(parts):
+        got = ring_blocks(waiting[k], "tensor")
+        order = sorted(got)
+        blocks = [got[j] for j in order]
+        if k + 1 < parts:
+            waiting[k + 1], blocks = lax.optimization_barrier((waiting[k + 1], blocks))
+        terms, own_rows = call(
+            functools.partial(ffn_kernel, n, tuple(order), units),
+            (
+                jax.ShapeDtypeStruct((part_rows, features), BF16),
+                jax.ShapeDtypeStruct((n, own_count, width), BF16),
+            ),
+            [smem] + [vmem] * (n + 1) + [hbm],
+            6 * part_rows * features * units,
+            scratch=[
+                pltpu.VMEM((features, 3 * units), BF16),
+                pltpu.VMEM((n, part_rows, width), BF16),
+                pltpu.VMEM((part_rows, low + tail), F32),
+                pltpu.VMEM((part_rows, 3 * units - low), BF16),
+                pltpu.SemaphoreType.DMA((low // 256 + 1,)),
+            ],
+            mib=60,
+        )(plane.reshape(1), *blocks, llm_gain.reshape(n, 1, width), whole)
+        summed = lax.psum_scatter(terms, "tensor", scatter_dimension=0, tiled=True).astype(F32)
+        own_rows = jnp.moveaxis(own_rows, 0, 1).reshape(own_count, features)
+        results.append((own_rows.astype(F32) + summed).astype(BF16))
+    return jnp.concatenate(results, axis=0)
 
 
 def solution(mesh):

time: 265 us -> 285 us (1.075); the launches traced: 264 us -> 281 us
  local copies, waits for them, and re-layouts: 8.54 us -> 19.4 us
  Pallas kernels: 45.6 us -> 51.2 us
    ppermute x21 -> x24, waiting for transfers between devices: 64.4 us -> 79.2 us  [the longest x8 50.2 us: ring_blocks(): a = lax.ppermute(a, axis, shifted(axis, 1))]
    reduce_scatter x1 -> x2, waiting for transfers between devices: 58.5 us -> 44.7 us  [body(): lax.psum_scatter(terms, 'tensor', scatter_dimension=0, tiled=True)]
    unnamed x30 -> x70, local copies, waits for them, and re-layouts: 1.07 us -> 9.82 us
    pallas_call x5 -> x7, Pallas kernels: 45.6 us -> 51.2 us  [run(): pl.pallas_call(kernel, out_shape=out_shape, in_specs=specs, out_specs=jax...]
    ppermute x21 -> x24, starting transfers between devices: 29.2 us -> 31 us  [the longest x6 16 us: ring_blocks(): b = lax.ppermute(b, axis, shifted(axis, -1))]
  transfers between devices with their start and end apart: 25 -> 29, of which waited for: 14 -> 17; matrix products, arithmetic and copies ran while one was open for 3% -> 4% of each run, Pallas kernels for 7% -> 12%
where the time goes in v1:
time: 285 us; the launch traced here: 281 us
  waiting for transfers between devices  149 us (52%)
  Pallas kernels  51.2 us (18%)
  starting transfers between devices  42.4 us (15%)
  local copies, waits for them, and re-layouts  19.4 us (7%)
  between operations  13.6 us (5%)
  other arithmetic  3.28 us (1%)
    pallas_call x7, Pallas kernels, run(): pl.pallas_call(kernel, out_shape=out_shape, in_specs=specs, out_specs=jax...  51.2 us
    ppermute x8, waiting for transfers between devices, ring_blocks(): a = lax.ppermute(a, axis, shifted(axis, 1))  50.2 us
    reduce_scatter x2, waiting for transfers between devices, body(): lax.psum_scatter(terms, 'tensor', scatter_dimension=0, tiled=True)  44.7 us
    all_to_all x1, waiting for transfers between devices, body(): lax.all_to_all(outgoing.reshape(owner_count, capacity, width), 'dp', spli...  25.2 us
    ppermute x3, waiting for transfers between devices, body(): ups.append(lax.ppermute(ups[-1], 'tensor', shifted('tensor', 1)))  24.4 us
    ppermute x6, starting transfers between devices, ring_blocks(): b = lax.ppermute(b, axis, shifted(axis, -1))  16 us
    unnamed x70, local copies, waits for them, and re-layouts  9.82 us
    all_to_all x1, starting transfers between devices, body(): lax.all_to_all(outgoing.reshape(owner_count, capacity, width), 'dp', spli...  8.45 us
  transfers between devices with their start and end apart: 29, of which 17 were waited for; matrix products, arithmetic and copies ran while one was open for 4% of the time, Pallas kernels for 12%

profile of v1, /device:TPU:1, one launch (start us, length us, event | category | flops | bytes accessed | tf_op | source)
XLA Modules:
  0.0 280.9 jit_solution(7787774386562033456)
XLA Ops:
  6.6 2.4 concatenate.6
  9.1 2.5 collective-permute-start
  11.6 4.0 %collective-permute-start.1 = (bf16[80,1280]{1,0:T(8,128)(2,1)S(1)}, bf16[80,1280]{1,0:T(8,128)(2,1)S(1)}, u32[]{:S(2)}, u32[]{:S(2)}) collective-permute-start(bf16[80,1280]{1,0:T(8,128)(2,1)S(1)} %constant_dynamic-slice_fusion.1.refs_0_.refs_8_), channel_id=1, source_target_pairs={{0,7},{1,0},{2,1},{3,2},{4,3},{5,4},{6,5},{7,6},{8,15},{9,8},{10,9... | collective-permute-start | bytes 614408 | tf_op jit(solution)/shard_map/ppermute | solution.py:281
  15.8 1.3 copy-done.8
  17.1 2.9 %shard_map.136.context_ref = bf16[160,512]{1,0:T(8,128)(2,1)S(1)} custom-call(s32[1]{0:T(128)} %bitcast.2.core_ref, bf16[512,1280]{1,0:T(8,128)(2,1)S(1)} %copy-done.1, s32[512,1]{1,0:T(8,128)S(1)} %copy.24.column_ref, s32[1,512]{1,0:T(1,128)S(1)} %copy-done.13, f32[1,1280]{1,0:T(1,128)S(1)} %broadcast_in_dim.30.gain_ref, bf16[3,160,1280]{2,1,0:T(8,128)(2,1)S(1)} %bitcast.20), custom_call_target="tpu_custom_call" | custom-call | flops 796917760 | bytes 2548740 | tf_op jit(solution)/shard_map/pallas_call | solution.py:223
  21.1 0.7 copy-done.9
  21.8 2.7 collective-permute-start.3
  24.5 6.8 %collective-permute-done.2.refs_3_.refs_1_.refs_11_ = bf16[1440,128]{1,0:T(8,128)(2,1)S(1)} collective-permute-done((bf16[1440,128]{1,0:T(8,128)(2,1)S(1)}, bf16[1440,128]{1,0:T(8,128)(2,1)S(1)}, u32[]{:S(2)}, u32[]{:S(2)}) %collective-permute-start.2) | collective-permute-done | bytes 368672 | tf_op jit(solution)/shard_map/ppermute | solution.py:287
  31.3 3.1 %collective-permute-start.5 = (bf16[1440,128]{1,0:T(8,128)(2,1)S(1)}, bf16[1440,128]{1,0:T(8,128)(2,1)S(1)}, u32[]{:S(2)}, u32[]{:S(2)}) collective-permute-start(bf16[1440,128]{1,0:T(8,128)(2,1)S(1)} %collective-permute-done.3.refs_4_.refs_2_.refs_12_), channel_id=1, source_target_pairs={{0,7},{1,0},{2,1},{3,2},{4,3},{5,4},{6,5},{7,6},{8,15},{9,8},{10,9... | collective-permute-start | bytes 1105928 | tf_op jit(solution)/shard_map/ppermute | solution.py:289
  34.4 6.2 %collective-permute-done.4.refs_5_.refs_3_.refs_13_ = bf16[1440,128]{1,0:T(8,128)(2,1)S(1)} collective-permute-done((bf16[1440,128]{1,0:T(8,128)(2,1)S(1)}, bf16[1440,128]{1,0:T(8,128)(2,1)S(1)}, u32[]{:S(2)}, u32[]{:S(2)}) %collective-permute-start.4) | collective-permute-done | bytes 368672 | tf_op jit(solution)/shard_map/ppermute | solution.py:287
  40.6 0.9 copy-done.6
  41.5 1.3 shard_map.138
  42.8 2.9 %collective-permute-start.9 = (bf16[7,800,128]{2,1,0:T(8,128)(2,1)}, bf16[7,800,128]{2,1,0:T(8,128)(2,1)}, u32[]{:S(2)}, u32[]{:S(2)}) collective-permute-start(bf16[7,800,128]{2,1,0:T(8,128)(2,1)} %shard_map.138), channel_id=1, source_target_pairs={{0,8},{8,0},{16,24},{24,16},{32,40},{40,32},{48,56},{56,48},{64,72... | collective-permute-start | bytes 4300808 | tf_op jit(solution)/shard_map/ppermute | solution.py:307
  46.4 11.4 %collective-permute-done.6.refs_5_.refs_15_ = bf16[1440,128]{1,0:T(8,128)(2,1)S(1)} collective-permute-done((bf16[1440,128]{1,0:T(8,128)(2,1)S(1)}, bf16[1440,128]{1,0:T(8,128)(2,1)S(1)}, u32[]{:S(2)}, u32[]{:S(2)}) %collective-permute-start.6) | collective-permute-done | bytes 368672 | tf_op jit(solution)/shard_map/ppermute | solution.py:287
  58.5 1.3 select_n.51.refs_21_
  60.5 1.5 collective-permute-start.7
  62.7 1.8 fusion.2
  64.5 1.5 copy.27.refs_22_
  66.7 3.1 %collective-permute-done.8.refs_7_ = bf16[640,128]{1,0:T(8,128)(2,1)} collective-permute-done((bf16[640,128]{1,0:T(8,128)(2,1)}, bf16[640,128]{1,0:T(8,128)(2,1)}, u32[]{:S(2)}, u32[]{:S(2)}) %collective-permute-start.8) | collective-permute-done | bytes 163872 | tf_op jit(solution)/shard_map/ppermute | solution.py:290
  69.7 1.0 copy-done.2
  70.8 0.9 copy-done.4
  71.7 0.9 copy-done.7
  72.7 1.0 copy-done.10
  73.7 9.3 %shard_map.139 = bf16[1024,448]{1,0:T(8,128)(2,1)} custom-call(bf16[1440,128]{1,0:T(8,128)(2,1)S(1)} %copy-done.10, bf16[1440,128]{1,0:T(8,128)(2,1)S(1)} %collective-permute-done.2.refs_3_.refs_1_.refs_11_, bf16[1440,128]{1,0:T(8,128)(2,1)S(1)} %collective-permute-done.3.refs_4_.refs_2_.refs_12_, ...), custom_call_target="tpu_custom_call" | custom-call | flops 2264924160 | bytes 13624320 | tf_op jit(solution)/shard_map/pallas_call | solution.py:223
  83.0 8.4 %all-to-all-start = ((bf16[32,32,448]{2,1,0:T(8,128)(2,1)}), bf16[32,32,448]{2,1,0:T(8,128)(2,1)S(1)}, u32[]{:S(2)}, u32[]{:S(2)}) async-start(bf16[32,32,448]{2,1,0:T(8,128)(2,1)} %bitcast.8), calls=%async_computation | async-start | bytes 2097152 | tf_op jit(solution)/shard_map/all_to_all | solution.py:353
  92.6 25.2 %all-to-all-done = bf16[32,32,448]{2,1,0:T(8,128)(2,1)S(1)} async-done(((bf16[32,32,448]{2,1,0:T(8,128)(2,1)}), bf16[32,32,448]{2,1,0:T(8,128)(2,1)S(1)}, u32[]{:S(2)}, u32[]{:S(2)}) %all-to-all-start) | async-done | bytes 917536 | tf_op jit(solution)/shard_map/all_to_all | solution.py:353
  117.8 0.7 shard_map.140
  118.7 2.7 collective-permute-start.15
  121.3 3.8 %collective-permute-done.11.refs_3_ = bf16[256,448]{1,0:T(8,128)(2,1)S(1)} collective-permute-done((bf16[256,448]{1,0:T(8,128)(2,1)S(1)}, bf16[256,448]{1,0:T(8,128)(2,1)S(1)}, u32[]{:S(2)}, u32[]{:S(2)}) %collective-permute-start.11) | collective-permute-done | bytes 229408 | tf_op jit(solution)/shard_map/ppermute | solution.py:29
  125.1 2.7 collective-permute-start.16
  127.8 3.8 %collective-permute-done.12.refs_2_ = bf16[256,448]{1,0:T(8,128)(2,1)S(1)} collective-permute-done((bf16[256,448]{1,0:T(8,128)(2,1)S(1)}, bf16[256,448]{1,0:T(8,128)(2,1)S(1)}, u32[]{:S(2)}, u32[]{:S(2)}) %collective-permute-start.12) | collective-permute-done | bytes 229408 | tf_op jit(solution)/shard_map/ppermute | solution.py:29
  131.5 2.7 collective-permute-start.17
  134.2 4.4 %collective-permute-done.13.refs_1_ = bf16[256,448]{1,0:T(8,128)(2,1)S(1)} collective-permute-done((bf16[256,448]{1,0:T(8,128)(2,1)S(1)}, bf16[256,448]{1,0:T(8,128)(2,1)S(1)}, u32[]{:S(2)}, u32[]{:S(2)}) %collective-permute-start.13) | collective-permute-done | bytes 229408 | tf_op jit(solution)/shard_map/ppermute | solution.py:29
  139.3 7.5 %collective-permute-done.14.refs_0_ = bf16[256,448]{1,0:T(8,128)(2,1)S(1)} collective-permute-done((bf16[256,448]{1,0:T(8,128)(2,1)S(1)}, bf16[256,448]{1,0:T(8,128)(2,1)S(1)}, u32[]{:S(2)}, u32[]{:S(2)}) %collective-permute-start.14) | collective-permute-done | bytes 229408 | tf_op jit(solution)/shard_map/ppermute | solution.py:29
  147.5 18.3 %shard_map.141 = (bf16[256,3584]{1,0:T(8,128)(2,1)}, bf16[8,32,448]{2,1,0:T(8,128)(2,1)}) custom-call(s32[1]{0:T(128)} %bitcast.place_ref, bf16[256,448]{1,0:T(8,128)(2,1)} %copy-done.25, bf16[256,448]{1,0:T(8,128)(2,1)} %copy-done.21, bf16[256,448]{1,0:T(8,128)(2,1)} %copy-done.17, bf16[256,448]{1,0:T(8,128)(2,1)} %copy-done.14, ...), custom_call_target="tpu_custom_call" | custom-call | flops 6517948416 | bytes 27310084 | tf_op jit(solution)/shard_map/pallas_call | solution.py:223
  166.0 2.7 collective-permute-start.22
  168.6 3.8 %collective-permute-done.18.refs_3_ = bf16[256,448]{1,0:T(8,128)(2,1)S(1)} collective-permute-done((bf16[256,448]{1,0:T(8,128)(2,1)S(1)}, bf16[256,448]{1,0:T(8,128)(2,1)S(1)}, u32[]{:S(2)}, u32[]{:S(2)}) %collective-permute-start.18) | collective-permute-done | bytes 229408 | tf_op jit(solution)/shard_map/ppermute | solution.py:29
  172.4 2.7 collective-permute-start.23
  175.1 5.6 %collective-permute-done.19.refs_2_ = bf16[256,448]{1,0:T(8,128)(2,1)S(1)} collective-permute-done((bf16[256,448]{1,0:T(8,128)(2,1)S(1)}, bf16[256,448]{1,0:T(8,128)(2,1)S(1)}, u32[]{:S(2)}, u32[]{:S(2)}) %collective-permute-start.19) | collective-permute-done | bytes 229408 | tf_op jit(solution)/shard_map/ppermute | solution.py:29
  180.7 2.7 collective-permute-start.24
  183.3 8.7 %collective-permute-done.20.refs_1_ = bf16[256,448]{1,0:T(8,128)(2,1)S(1)} collective-permute-done((bf16[256,448]{1,0:T(8,128)(2,1)S(1)}, bf16[256,448]{1,0:T(8,128)(2,1)S(1)}, u32[]{:S(2)}, u32[]{:S(2)}) %collective-permute-start.20) | collective-permute-done | bytes 229408 | tf_op jit(solution)/shard_map/ppermute | solution.py:29
  192.7 12.7 %collective-permute-done.21.refs_0_ = bf16[256,448]{1,0:T(8,128)(2,1)S(1)} collective-permute-done((bf16[256,448]{1,0:T(8,128)(2,1)S(1)}, bf16[256,448]{1,0:T(8,128)(2,1)S(1)}, u32[]{:S(2)}, u32[]{:S(2)}) %collective-permute-start.21) | collective-permute-done | bytes 229408 | tf_op jit(solution)/shard_map/ppermute | solution.py:29
  206.2 18.6 %shard_map.142 = (bf16[256,3584]{1,0:T(8,128)(2,1)}, bf16[8,32,448]{2,1,0:T(8,128)(2,1)}) custom-call(s32[1]{0:T(128)} %bitcast.place_ref, bf16[256,448]{1,0:T(8,128)(2,1)} %copy-done.27, bf16[256,448]{1,0:T(8,128)(2,1)} %copy-done.24, bf16[256,448]{1,0:T(8,128)(2,1)} %copy-done.20, bf16[256,448]{1,0:T(8,128)(2,1)} %copy-done.16, ...), custom_call_target="tpu_custom_call" | custom-call | flops 6517948416 | bytes 27310084 | tf_op jit(solution)/shard_map/pallas_call | solution.py:223
  224.8 0.9 copy-done.28
  226.9 1.0 add_convert_fusion.1
  227.9 44.7 %reduce-scatter.5.cloned.1.call-done = bf16[32,3584]{1,0:T(8,128)(2,1)} async-done(((bf16[256,3584]{1,0:T(8,128)(2,1)}), bf16[32,3584]{1,0:T(8,128)(2,1)}) %reduce-scatter.5.cloned.1.call-update) | async-done | bytes 229392 | tf_op jit(solution)/shard_map/reduce_scatter | solution.py:401
  272.6 1.0 add_convert_fusion
  273.6 0.8 pad_maximum_fusion
  (124 shorter events, 10.0 us)
Async XLA Ops:
  6.5 9.1 %copy-start.13 = (s32[1,512]{1,0:T(1,128)S(1)}, s32[1,512]{1,0:T(1,128)}, u32[]{:S(2)}) copy-start(s32[1,512]{1,0:T(1,128)} %row_ref.1) | copy-start | bytes 6148
  6.5 140.2 %all-gather.2.cloned.1.call-start = ((), (), s32[]{:S(2)}) async-start(), calls=%async_computation.3 | async-start | bytes 26492928 | tf_op jit(solution)/shard_map/all_gather | solution.py:311
  6.5 9.2 %copy-start.32 = (f32[1280]{0:T(1024)S(1)}, f32[1280]{0:T(1024)}, u32[]{:S(2)}) copy-start(f32[1280]{0:T(1024)} %param.16) | copy-start | bytes 15364
  6.5 9.3 %copy-start.1 = (bf16[512,1280]{1,0:T(8,128)(2,1)S(1)}, bf16[512,1280]{1,0:T(8,128)(2,1)}, u32[]{:S(2)}) copy-start(bf16[512,1280]{1,0:T(8,128)(2,1)} %refs_18_.1) | copy-start | bytes 3932164
  9.1 11.3 %collective-permute-start = (bf16[80,1280]{1,0:T(8,128)(2,1)S(1)}, bf16[80,1280]{1,0:T(8,128)(2,1)S(1)}, u32[]{:S(2)}, u32[]{:S(2)}) collective-permute-start(bf16[80,1280]{1,0:T(8,128)(2,1)S(1)} %constant_dynamic-slice_fusion.1.refs_0_.refs_8_), channel_id=1, source_target_pairs={{0,1},{1,2},{2,3},{3,4},{4,5},{5,6},{6,7},{7,0},{8,9},{9,10},{10,1... | collective-permute-start | bytes 614408 | tf_op jit(solution)/shard_map/ppermute | solution.py:280
  11.6 8.7 %collective-permute-start.1 = (bf16[80,1280]{1,0:T(8,128)(2,1)S(1)}, bf16[80,1280]{1,0:T(8,128)(2,1)S(1)}, u32[]{:S(2)}, u32[]{:S(2)}) collective-permute-start(bf16[80,1280]{1,0:T(8,128)(2,1)S(1)} %constant_dynamic-slice_fusion.1.refs_0_.refs_8_), channel_id=1, source_target_pairs={{0,7},{1,0},{2,1},{3,2},{4,3},{5,4},{6,5},{7,6},{8,15},{9,8},{10,9... | collective-permute-start | bytes 614408 | tf_op jit(solution)/shard_map/ppermute | solution.py:281
  20.3 22.5 %copy-start.3 = (bf16[80,1280]{1,0:T(8,128)(2,1)}, bf16[80,1280]{1,0:T(8,128)(2,1)S(1)}, u32[]{:S(2)}) copy-start(bf16[80,1280]{1,0:T(8,128)(2,1)S(1)} %collective-permute-done.above_ref.refs_1_.refs_9_) | copy-start | bytes 614404
  20.3 25.7 %copy-start.30 = (s32[32,32]{1,0:T(8,128)S(1)}, s32[32,32]{1,0:T(8,128)}, u32[]{:S(2)}) copy-start(s32[32,32]{1,0:T(8,128)} %param.22) | copy-start | bytes 12292
  20.4 42.3 %copy-start.34 = (bf16[384,448]{0,1:T(8,128)(2,1)S(1)}, bf16[384,448]{0,1:T(8,128)(2,1)}, u32[]{:S(2)}) copy-start(bf16[384,448]{0,1:T(8,128)(2,1)} %param.21) | copy-start | bytes 1032196
  21.1 10.2 %collective-permute-start.2 = (bf16[1440,128]{1,0:T(8,128)(2,1)S(1)}, bf16[1440,128]{1,0:T(8,128)(2,1)S(1)}, u32[]{:S(2)}, u32[]{:S(2)}) collective-permute-start(bf16[1440,128]{1,0:T(8,128)(2,1)S(1)} %get-tuple-element.22.refs_0_), channel_id=1, source_target_pairs={{0,1},{1,2},{2,3},{3,4},{4,5},{5,6},{6,7},{7,0},{8,9},{9,10},{10,1... | collective-permute-start | bytes 1105928 | tf_op jit(solution)/shard_map/ppermute | solution.py:287
  21.8 9.4 %collective-permute-start.3 = (bf16[1440,128]{1,0:T(8,128)(2,1)S(1)}, bf16[1440,128]{1,0:T(8,128)(2,1)S(1)}, u32[]{:S(2)}, u32[]{:S(2)}) collective-permute-start(bf16[1440,128]{1,0:T(8,128)(2,1)S(1)} %get-tuple-element.23), channel_id=1, source_target_pairs={{0,7},{1,0},{2,1},{3,2},{4,3},{5,4},{6,5},{7,6},{8,15},{9,8},{10,9... | collective-permute-start | bytes 1105928 | tf_op jit(solution)/shard_map/ppermute | solution.py:289
  31.2 9.4 %collective-permute-start.4 = (bf16[1440,128]{1,0:T(8,128)(2,1)S(1)}, bf16[1440,128]{1,0:T(8,128)(2,1)S(1)}, u32[]{:S(2)}, u32[]{:S(2)}) collective-permute-start(bf16[1440,128]{1,0:T(8,128)(2,1)S(1)} %collective-permute-done.2.refs_3_.refs_1_.refs_11_), channel_id=1, source_target_pairs={{0,1},{1,2},{2,3},{3,4},{4,5},{5,6},{6,7},{7,0},{8,9},{9,10},{10,1... | collective-permute-start | bytes 1105928 | tf_op jit(solution)/shard_map/ppermute | solution.py:287
  31.3 9.3 %collective-permute-start.5 = (bf16[1440,128]{1,0:T(8,128)(2,1)S(1)}, bf16[1440,128]{1,0:T(8,128)(2,1)S(1)}, u32[]{:S(2)}, u32[]{:S(2)}) collective-permute-start(bf16[1440,128]{1,0:T(8,128)(2,1)S(1)} %collective-permute-done.3.refs_4_.refs_2_.refs_12_), channel_id=1, source_target_pairs={{0,7},{1,0},{2,1},{3,2},{4,3},{5,4},{6,5},{7,6},{8,15},{9,8},{10,9... | collective-permute-start | bytes 1105928 | tf_op jit(solution)/shard_map/ppermute | solution.py:289
  42.8 26.9 %collective-permute-start.9 = (bf16[7,800,128]{2,1,0:T(8,128)(2,1)}, bf16[7,800,128]{2,1,0:T(8,128)(2,1)}, u32[]{:S(2)}, u32[]{:S(2)}) collective-permute-start(bf16[7,800,128]{2,1,0:T(8,128)(2,1)} %shard_map.138), channel_id=1, source_target_pairs={{0,8},{8,0},{16,24},{24,16},{32,40},{40,32},{48,56},{56,48},{64,72... | collective-permute-start | bytes 4300808 | tf_op jit(solution)/shard_map/ppermute | solution.py:307
  45.7 12.1 %collective-permute-start.6 = (bf16[1440,128]{1,0:T(8,128)(2,1)S(1)}, bf16[1440,128]{1,0:T(8,128)(2,1)S(1)}, u32[]{:S(2)}, u32[]{:S(2)}) collective-permute-start(bf16[1440,128]{1,0:T(8,128)(2,1)S(1)} %collective-permute-done.4.refs_5_.refs_3_.refs_13_), channel_id=1, source_target_pairs={{0,1},{1,2},{2,3},{3,4},{4,5},{5,6},{6,7},{7,0},{8,9},{9,10},{10,1... | collective-permute-start | bytes 1105928 | tf_op jit(solution)/shard_map/ppermute | solution.py:287
  57.8 11.9 %collective-permute-start.10 = (bf16[1440,128]{1,0:T(8,128)(2,1)S(1)}, bf16[1440,128]{1,0:T(8,128)(2,1)}, u32[]{:S(2)}, u32[]{:S(2)}) collective-permute-start(bf16[1440,128]{1,0:T(8,128)(2,1)S(1)} %collective-permute-done.6.refs_5_.refs_15_), channel_id=1, source_target_pairs={{0,8},{8,0},{16,24},{24,16},{32,40},{40,32},{48,56},{56,48},{64,72... | collective-permute-start | bytes 1105928 | tf_op jit(solution)/shard_map/ppermute | solution.py:308
  60.5 6.1 %collective-permute-start.7 = (bf16[640,128]{1,0:T(8,128)(2,1)}, bf16[640,128]{1,0:T(8,128)(2,1)}, u32[]{:S(2)}, u32[]{:S(2)}) collective-permute-start(bf16[640,128]{1,0:T(8,128)(2,1)} %slice.12), channel_id=1, source_target_pairs={{0,7},{1,0},{2,1},{3,2},{4,3},{5,4},{6,5},{7,6},{8,15},{9,8},{10,9... | collective-permute-start | bytes 491528 | tf_op jit(solution)/shard_map/ppermute | solution.py:289
  62.7 7.0 %collective-permute-start.8 = (bf16[640,128]{1,0:T(8,128)(2,1)}, bf16[640,128]{1,0:T(8,128)(2,1)}, u32[]{:S(2)}, u32[]{:S(2)}) collective-permute-start(bf16[640,128]{1,0:T(8,128)(2,1)} %slice.13), channel_id=1, source_target_pairs={{0,1},{1,2},{2,3},{3,4},{4,5},{5,6},{6,7},{7,0},{8,9},{9,10},{10,1... | collective-permute-start | bytes 491528 | tf_op jit(solution)/shard_map/ppermute | solution.py:290
  83.0 55.6 %copy-start.31 = (f32[3584]{0:T(1024)S(1)}, f32[3584]{0:T(1024)}, u32[]{:S(2)}) copy-start(f32[3584]{0:T(1024)} %param.24) | copy-start | bytes 43012
  83.0 34.9 %all-to-all-start = ((bf16[32,32,448]{2,1,0:T(8,128)(2,1)}), bf16[32,32,448]{2,1,0:T(8,128)(2,1)S(1)}, u32[]{:S(2)}, u32[]{:S(2)}) async-start(bf16[32,32,448]{2,1,0:T(8,128)(2,1)} %bitcast.8), calls=%async_computation | async-start | bytes 2097152 | tf_op jit(solution)/shard_map/all_to_all | solution.py:353
  91.4 135.5 %reduce-scatter.3.cloned.1.call-start = ((), (), s32[]{:S(2)}) async-start(), calls=%async_computation.4 | async-start | bytes 2064384 | tf_op jit(solution)/shard_map/reduce_scatter | solution.py:401
  118.6 28.2 %copy-start.12 = (bf16[256,448]{1,0:T(8,128)(2,1)}, bf16[256,448]{1,0:T(8,128)(2,1)S(1)}, u32[]{:S(2)}) copy-start(bf16[256,448]{1,0:T(8,128)(2,1)S(1)} %get-tuple-element.30.refs_4_) | copy-start | bytes 688132
  118.6 47.4 %copy-start.11 = (bf16[256,448]{1,0:T(8,128)(2,1)}, bf16[256,448]{1,0:T(8,128)(2,1)S(1)}, u32[]{:S(2)}) copy-start(bf16[256,448]{1,0:T(8,128)(2,1)S(1)} %get-tuple-element.36.refs_4_) | copy-start | bytes 688132
  118.6 6.5 %collective-permute-start.11 = (bf16[256,448]{1,0:T(8,128)(2,1)S(1)}, bf16[256,448]{1,0:T(8,128)(2,1)S(1)}, u32[]{:S(2)}, u32[]{:S(2)}) collective-permute-start(bf16[256,448]{1,0:T(8,128)(2,1)S(1)} %get-tuple-element.30.refs_4_), channel_id=1, source_target_pairs={{0,1},{1,2},{2,3},{3,4},{4,5},{5,6},{6,7},{7,0},{8,9},{9,10},{10,1... | collective-permute-start | bytes 688136 | tf_op jit(solution)/shard_map/ppermute | solution.py:29
  118.7 6.4 %collective-permute-start.15 = (bf16[256,448]{1,0:T(8,128)(2,1)S(1)}, bf16[256,448]{1,0:T(8,128)(2,1)S(1)}, u32[]{:S(2)}, u32[]{:S(2)}) collective-permute-start(bf16[256,448]{1,0:T(8,128)(2,1)S(1)} %get-tuple-element.30.refs_4_), channel_id=1, source_target_pairs={{0,7},{1,0},{2,1},{3,2},{4,3},{5,4},{6,5},{7,6},{8,15},{9,8},{10,9... | collective-permute-start | bytes 688136 | tf_op jit(solution)/shard_map/ppermute | solution.py:32
  125.1 21.7 %copy-start.14 = (bf16[256,448]{1,0:T(8,128)(2,1)}, bf16[256,448]{1,0:T(8,128)(2,1)S(1)}, u32[]{:S(2)}) copy-start(bf16[256,448]{1,0:T(8,128)(2,1)S(1)} %collective-permute-done.11.refs_3_) | copy-start | bytes 688132
  125.1 6.4 %collective-permute-start.12 = (bf16[256,448]{1,0:T(8,128)(2,1)S(1)}, bf16[256,448]{1,0:T(8,128)(2,1)S(1)}, u32[]{:S(2)}, u32[]{:S(2)}) collective-permute-start(bf16[256,448]{1,0:T(8,128)(2,1)S(1)} %collective-permute-done.11.refs_3_), channel_id=1, source_target_pairs={{0,1},{1,2},{2,3},{3,4},{4,5},{5,6},{6,7},{7,0},{8,9},{9,10},{10,1... | collective-permute-start | bytes 688136 | tf_op jit(solution)/shard_map/ppermute | solution.py:29
  125.1 21.7 %copy-start.15 = (bf16[256,448]{1,0:T(8,128)(2,1)}, bf16[256,448]{1,0:T(8,128)(2,1)S(1)}, u32[]{:S(2)}) copy-start(bf16[256,448]{1,0:T(8,128)(2,1)S(1)} %collective-permute-done.15.refs_5_) | copy-start | bytes 688132
  125.1 6.4 %collective-permute-start.16 = (bf16[256,448]{1,0:T(8,128)(2,1)S(1)}, bf16[256,448]{1,0:T(8,128)(2,1)S(1)}, u32[]{:S(2)}, u32[]{:S(2)}) collective-permute-start(bf16[256,448]{1,0:T(8,128)(2,1)S(1)} %collective-permute-done.15.refs_5_), channel_id=1, source_target_pairs={{0,7},{1,0},{2,1},{3,2},{4,3},{5,4},{6,5},{7,6},{8,15},{9,8},{10,9... | collective-permute-start | bytes 688136 | tf_op jit(solution)/shard_map/ppermute | solution.py:32
  131.5 15.3 %copy-start.17 = (bf16[256,448]{1,0:T(8,128)(2,1)}, bf16[256,448]{1,0:T(8,128)(2,1)S(1)}, u32[]{:S(2)}) copy-start(bf16[256,448]{1,0:T(8,128)(2,1)S(1)} %collective-permute-done.12.refs_2_) | copy-start | bytes 688132
  131.5 7.1 %collective-permute-start.13 = (bf16[256,448]{1,0:T(8,128)(2,1)S(1)}, bf16[256,448]{1,0:T(8,128)(2,1)S(1)}, u32[]{:S(2)}, u32[]{:S(2)}) collective-permute-start(bf16[256,448]{1,0:T(8,128)(2,1)S(1)} %collective-permute-done.12.refs_2_), channel_id=1, source_target_pairs={{0,1},{1,2},{2,3},{3,4},{4,5},{5,6},{6,7},{7,0},{8,9},{9,10},{10,1... | collective-permute-start | bytes 688136 | tf_op jit(solution)/shard_map/ppermute | solution.py:29
  131.5 15.3 %copy-start.19 = (bf16[256,448]{1,0:T(8,128)(2,1)}, bf16[256,448]{1,0:T(8,128)(2,1)S(1)}, u32[]{:S(2)}) copy-start(bf16[256,448]{1,0:T(8,128)(2,1)S(1)} %collective-permute-done.16.refs_6_) | copy-start | bytes 688132
  131.5 7.8 %collective-permute-start.17 = (bf16[256,448]{1,0:T(8,128)(2,1)S(1)}, bf16[256,448]{1,0:T(8,128)(2,1)S(1)}, u32[]{:S(2)}, u32[]{:S(2)}) collective-permute-start(bf16[256,448]{1,0:T(8,128)(2,1)S(1)} %collective-permute-done.16.refs_6_), channel_id=1, source_target_pairs={{0,7},{1,0},{2,1},{3,2},{4,3},{5,4},{6,5},{7,6},{8,15},{9,8},{10,9... | collective-permute-start | bytes 688136 | tf_op jit(solution)/shard_map/ppermute | solution.py:32
  138.6 8.2 %collective-permute-start.14 = (bf16[256,448]{1,0:T(8,128)(2,1)S(1)}, bf16[256,448]{1,0:T(8,128)(2,1)S(1)}, u32[]{:S(2)}, u32[]{:S(2)}) collective-permute-start(bf16[256,448]{1,0:T(8,128)(2,1)S(1)} %collective-permute-done.13.refs_1_), channel_id=1, source_target_pairs={{0,1},{1,2},{2,3},{3,4},{4,5},{5,6},{6,7},{7,0},{8,9},{9,10},{10,1... | collective-permute-start | bytes 688136 | tf_op jit(solution)/shard_map/ppermute | solution.py:29
  165.8 106.8 %reduce-scatter.5.cloned.1.call-start = ((), (), s32[]{:S(2)}) async-start(), calls=%async_computation.5 | async-start | bytes 2064384 | tf_op jit(solution)/shard_map/reduce_scatter | solution.py:401
  165.9 6.5 %collective-permute-start.18 = (bf16[256,448]{1,0:T(8,128)(2,1)S(1)}, bf16[256,448]{1,0:T(8,128)(2,1)S(1)}, u32[]{:S(2)}, u32[]{:S(2)}) collective-permute-start(bf16[256,448]{1,0:T(8,128)(2,1)S(1)} %get-tuple-element.36.refs_4_), channel_id=1, source_target_pairs={{0,1},{1,2},{2,3},{3,4},{4,5},{5,6},{6,7},{7,0},{8,9},{9,10},{10,1... | collective-permute-start | bytes 688136 | tf_op jit(solution)/shard_map/ppermute | solution.py:29
  166.0 6.4 %collective-permute-start.22 = (bf16[256,448]{1,0:T(8,128)(2,1)S(1)}, bf16[256,448]{1,0:T(8,128)(2,1)S(1)}, u32[]{:S(2)}, u32[]{:S(2)}) collective-permute-start(bf16[256,448]{1,0:T(8,128)(2,1)S(1)} %get-tuple-element.36.refs_4_), channel_id=1, source_target_pairs={{0,7},{1,0},{2,1},{3,2},{4,3},{5,4},{6,5},{7,6},{8,15},{9,8},{10,9... | collective-permute-start | bytes 688136 | tf_op jit(solution)/shard_map/ppermute | solution.py:32
  172.4 33.1 %copy-start.16 = (bf16[256,448]{1,0:T(8,128)(2,1)}, bf16[256,448]{1,0:T(8,128)(2,1)S(1)}, u32[]{:S(2)}) copy-start(bf16[256,448]{1,0:T(8,128)(2,1)S(1)} %collective-permute-done.18.refs_3_) | copy-start | bytes 688132
  172.4 8.3 %collective-permute-start.19 = (bf16[256,448]{1,0:T(8,128)(2,1)S(1)}, bf16[256,448]{1,0:T(8,128)(2,1)S(1)}, u32[]{:S(2)}, u32[]{:S(2)}) collective-permute-start(bf16[256,448]{1,0:T(8,128)(2,1)S(1)} %collective-permute-done.18.refs_3_), channel_id=1, source_target_pairs={{0,1},{1,2},{2,3},{3,4},{4,5},{5,6},{6,7},{7,0},{8,9},{9,10},{10,1... | collective-permute-start | bytes 688136 | tf_op jit(solution)/shard_map/ppermute | solution.py:29
  172.4 33.1 %copy-start.18 = (bf16[256,448]{1,0:T(8,128)(2,1)}, bf16[256,448]{1,0:T(8,128)(2,1)S(1)}, u32[]{:S(2)}) copy-start(bf16[256,448]{1,0:T(8,128)(2,1)S(1)} %collective-permute-done.22.refs_5_) | copy-start | bytes 688132
  172.4 8.3 %collective-permute-start.23 = (bf16[256,448]{1,0:T(8,128)(2,1)S(1)}, bf16[256,448]{1,0:T(8,128)(2,1)S(1)}, u32[]{:S(2)}, u32[]{:S(2)}) collective-permute-start(bf16[256,448]{1,0:T(8,128)(2,1)S(1)} %collective-permute-done.22.refs_5_), channel_id=1, source_target_pairs={{0,7},{1,0},{2,1},{3,2},{4,3},{5,4},{6,5},{7,6},{8,15},{9,8},{10,9... | collective-permute-start | bytes 688136 | tf_op jit(solution)/shard_map/ppermute | solution.py:32
  180.7 24.8 %copy-start.20 = (bf16[256,448]{1,0:T(8,128)(2,1)}, bf16[256,448]{1,0:T(8,128)(2,1)S(1)}, u32[]{:S(2)}) copy-start(bf16[256,448]{1,0:T(8,128)(2,1)S(1)} %collective-permute-done.19.refs_2_) | copy-start | bytes 688132
  180.7 11.4 %collective-permute-start.20 = (bf16[256,448]{1,0:T(8,128)(2,1)S(1)}, bf16[256,448]{1,0:T(8,128)(2,1)S(1)}, u32[]{:S(2)}, u32[]{:S(2)}) collective-permute-start(bf16[256,448]{1,0:T(8,128)(2,1)S(1)} %collective-permute-done.19.refs_2_), channel_id=1, source_target_pairs={{0,1},{1,2},{2,3},{3,4},{4,5},{5,6},{6,7},{7,0},{8,9},{9,10},{10,1... | collective-permute-start | bytes 688136 | tf_op jit(solution)/shard_map/ppermute | solution.py:29
  180.7 24.8 %copy-start.22 = (bf16[256,448]{1,0:T(8,128)(2,1)}, bf16[256,448]{1,0:T(8,128)(2,1)S(1)}, u32[]{:S(2)}) copy-start(bf16[256,448]{1,0:T(8,128)(2,1)S(1)} %collective-permute-done.23.refs_6_) | copy-start | bytes 688132
  180.7 12.0 %collective-permute-start.24 = (bf16[256,448]{1,0:T(8,128)(2,1)S(1)}, bf16[256,448]{1,0:T(8,128)(2,1)S(1)}, u32[]{:S(2)}, u32[]{:S(2)}) collective-permute-start(bf16[256,448]{1,0:T(8,128)(2,1)S(1)} %collective-permute-done.23.refs_6_), channel_id=1, source_target_pairs={{0,7},{1,0},{2,1},{3,2},{4,3},{5,4},{6,5},{7,6},{8,15},{9,8},{10,9... | collective-permute-start | bytes 688136 | tf_op jit(solution)/shard_map/ppermute | solution.py:32
  192.1 13.4 %copy-start.24 = (bf16[256,448]{1,0:T(8,128)(2,1)}, bf16[256,448]{1,0:T(8,128)(2,1)S(1)}, u32[]{:S(2)}) copy-start(bf16[256,448]{1,0:T(8,128)(2,1)S(1)} %collective-permute-done.20.refs_1_) | copy-start | bytes 688132
  192.1 13.3 %collective-permute-start.21 = (bf16[256,448]{1,0:T(8,128)(2,1)S(1)}, bf16[256,448]{1,0:T(8,128)(2,1)S(1)}, u32[]{:S(2)}, u32[]{:S(2)}) collective-permute-start(bf16[256,448]{1,0:T(8,128)(2,1)S(1)} %collective-permute-done.20.refs_1_), channel_id=1, source_target_pairs={{0,1},{1,2},{2,3},{3,4},{4,5},{5,6},{6,7},{7,0},{8,9},{9,10},{10,1... | collective-permute-start | bytes 688136 | tf_op jit(solution)/shard_map/ppermute | solution.py:29
  192.7 12.8 %copy-start.26 = (bf16[256,448]{1,0:T(8,128)(2,1)}, bf16[256,448]{1,0:T(8,128)(2,1)S(1)}, u32[]{:S(2)}) copy-start(bf16[256,448]{1,0:T(8,128)(2,1)S(1)} %collective-permute-done.24.refs_7_) | copy-start | bytes 688132
  (16 other events, 33.0 us)
Sparse Core Ops, SparseCore 0:
  9.9 113.8 all-gather.1
  165.9 47.2 reduce-scatter.2
  224.9 47.6 reduce-scatter.4

commit v2 on v1

v2 whole, which is shorter than its diff:
```python
import functools
import math

import jax
import jax.numpy as jnp
from jax import lax
from jax.experimental import pallas as pl
from jax.experimental.pallas import tpu as pltpu
from jax.sharding import PartitionSpec as P

HEAD_VIT = 80
EPSILON = 1e-06
VMEM = pltpu.MemorySpace.VMEM
SMEM = pltpu.MemorySpace.SMEM
HBM = pltpu.MemorySpace.HBM
BF16 = jnp.bfloat16
F32 = jnp.float32


def shifted(axis, step):
    n = lax.axis_size(axis)
    return [(i, (i + step) % n) for i in range(n)]


def ring_blocks(x, axis):
    n = lax.axis_size(axis)
    blocks = {0: x}
    a = b = x
    for k in range(1, n // 2 + 1):
        a = lax.ppermute(a, axis, shifted(axis, 1))
        blocks[-k] = a
        if k < n - n // 2:
            b = lax.ppermute(b, axis, shifted(axis, -1))
            blocks[k] = b
    return blocks


def turned_dot(left, right):
    return lax.dot_general(left, right, (((1,), (1,)), ((), ())), preferred_element_type=F32)


def inverse_rms(wide):
    return lax.rsqrt(jnp.mean(wide * wide, axis=-1, keepdims=True) + EPSILON)


def vision_kernel(core_ref, patches_ref, column_ref, row_ref, gain_ref, weight_ref, out_ref):
    wide = patches_ref[...].astype(F32)
    normed = (wide * inverse_rms(wide) * gain_ref[...]).astype(BF16)
    query, keys, values = (
        turned_dot(normed, weight_ref[k]).astype(BF16) for k in range(3)
    )
    same = column_ref[...] == row_ref[...]
    for head in range(2):
        part = slice(head * HEAD_VIT, (head + 1) * HEAD_VIT)
        scores = turned_dot(query[:, part], keys[:, part])
        scores = jnp.where(same, scores * (1.0 / math.sqrt(HEAD_VIT)), -1e30)
        weights = jnp.exp(scores - jnp.max(scores, axis=-1, keepdims=True))
        probs = (weights / jnp.sum(weights, axis=-1, keepdims=True)).astype(BF16)
        context = lax.dot_general(
            values[:, part], probs, (((0,), (1,)), ((), ())), preferred_element_type=F32
        )
        place = pl.multiple_of(lax.rem(core_ref[0] + head, 2) * HEAD_VIT, 16)
        out_ref[pl.ds(place, HEAD_VIT), :] = context.astype(BF16)


def lay(into, at, wide):
    rows, columns = wide.shape
    for j in range(columns // 128):
        into[pl.ds(at + j * rows, rows), :] = wide[:, pl.ds(j * 128, 128)]


def spread(into, at, tall, start, rows):
    for j in range(into.shape[1] // 128):
        into[pl.ds(at, rows), pl.ds(j * 128, 128)] = tall[pl.ds(start + j * rows, rows), :]


def pack_kernel(context_ref, above_ref, below_ref, up_ref, down_ref):
    split = context_ref.size // 128
    for out_ref, block_ref in ((up_ref, above_ref), (down_ref, below_ref)):
        lay(out_ref, 0, context_ref)
        lay(out_ref, split, block_ref)


def stack_kernel(wide_count, *refs):
    blocks, out_ref = refs[:-1], refs[-1]
    rows = out_ref.shape[1]
    for k, ref in enumerate(blocks):
        if k < wide_count:
            lay(out_ref.at[k], 0, ref)
        else:
            out_ref[k] = ref[pl.ds(ref.shape[0] - rows, rows), :]


def project_kernel(n, *refs):
    count = n + 4
    sources, out_ref, sems = refs[:count], refs[count], refs[-1]
    places, (context, weight) = refs[count + 1 : 2 * count + 1], refs[2 * count + 1 : 2 * count + 3]
    fetch = [
        pltpu.make_async_copy(source, place, sems.at[k])
        for k, (source, place) in enumerate(zip(sources, places))
    ]
    for copy in fetch:
        copy.start()
    payloads, wide, (other, patches) = places[: n - 1], places[n - 1 : n + 2], places[n + 2 :]
    group = 2 * HEAD_VIT
    split = group * context.shape[1] // 128
    for k in range(n - 1):
        fetch[k].wait()
        spread(context, k * group, payloads[k], 0, group)
    for k in range(3):
        fetch[n - 1 + k].wait()
        weight[pl.ds(k * group, HEAD_VIT), :] = wide[k][...]
    for k in range(3, n - 1):
        spread(weight, k * group, payloads[k - 2], split, HEAD_VIT)
    turned = context[...].T
    fetch[n + 2].wait()
    for k in range(n - 1):
        spread(weight, k * group + HEAD_VIT, other.at[k], 0, HEAD_VIT)
    fetch[n + 3].wait()

    @pl.loop(0, out_ref.shape[1] // 256)
    def _(j):
        columns = pl.ds(pl.multiple_of(j * 256, 256), 256)
        attended = jnp.dot(turned, weight[:, columns], preferred_element_type=F32)
        out_ref[:, columns] = patches[:, columns].astype(F32) + attended


def merge_kernel(*refs):
    context_ref, mine_ref, last_ref, sofar_ref, gain_ref, merger_hbm, slot_ref, audio_hbm, out_ref = refs[:9]
    context, weight, normed, merger, audio, sems = refs[9:]
    fetch = [
        pltpu.make_async_copy(merger_hbm, merger, sems.at[0]),
        pltpu.make_async_copy(audio_hbm, audio, sems.at[1]),
    ]
    for copy in fetch:
        copy.start()
    rows, d_vit = sofar_ref.shape
    group = 2 * HEAD_VIT
    split = group * rows // 128
    spread(context, 0, context_ref, 0, group)
    spread(weight, 0, mine_ref, split, HEAD_VIT)
    spread(weight, HEAD_VIT, last_ref, split, HEAD_VIT)
    turned = context[...].T
    lanes = 128
    squares = jnp.zeros((rows, 1), F32)
    for j in range(d_vit // 256):
        columns = pl.ds(j * 256, 256)
        attended = jnp.dot(turned, weight[:, columns], preferred_element_type=F32)
        wide = (sofar_ref[:, columns] + attended).astype(BF16).astype(F32)
        squares += jnp.sum(wide * wide, axis=-1, keepdims=True)
        normed[2 * j] = wide[:, :lanes]
        normed[2 * j + 1] = wide[:, lanes:]
    scale = lax.rsqrt(squares / d_vit + EPSILON)
    for j in range(d_vit // lanes):
        normed[j] = normed[j] * scale * gain_ref[:, pl.ds(j * lanes, lanes)]

    fetch[0].wait()
    video = jnp.zeros((rows // 4, merger.shape[0]), F32)
    for j in range(4):
        part = [normed[k, pl.ds(j, rows // 4, stride=4), :] for k in range(d_vit // lanes)]
        part = jnp.concatenate(part, axis=1).astype(BF16)
        video += turned_dot(part, merger[:, pl.ds(j * d_vit, d_vit)])
    video = video.astype(BF16)
    index = lax.broadcasted_iota(jnp.int32, (slot_ref.shape[0], rows // 4), 1)
    select = (slot_ref[...] == index).astype(F32).astype(BF16)
    placed = jnp.dot(select, video, preferred_element_type=F32)
    fetch[1].wait()
    out_ref[...] = (placed + audio[...].astype(F32)).astype(BF16)


def pick_kernel(target_ref, incoming_ref, out_ref):
    row = lax.broadcasted_iota(jnp.int32, (out_ref.shape[0], incoming_ref.shape[0]), 0)
    pick = (row == target_ref[...]).astype(F32).astype(BF16)
    out_ref[...] = jnp.dot(pick, incoming_ref[...], preferred_element_type=F32).astype(BF16)


def gate_kernel(n, shifts, units, place_ref, *refs):
    sources, gain_ref, whole_hbm, hidden_ref, own_ref = refs[:n], refs[n], refs[n + 1], refs[n + 2], refs[n + 3]
    blocks, whole, normed, sems = refs[n + 4 :]
    features = whole.shape[0]
    rows, chunk = blocks.shape[1:]
    apart = whole.shape[1] - units
    bring, fetch, places = [], [], []
    for j, shift in enumerate(shifts):
        at = lax.rem(place_ref[0] + shift + n, n)
        places.append(at)
        bring.append(pltpu.make_async_copy(sources[j], blocks.at[j], sems.at[n + j]))
        source = whole_hbm.at[pl.ds(pl.multiple_of(at * chunk, 16), chunk), :]
        fetch.append(pltpu.make_async_copy(source, whole.at[pl.ds(j * chunk, chunk), :], sems.at[j]))
    for copy in bring + fetch:
        copy.start()
    squares = jnp.zeros((rows, 1), F32)
    for j in range(n):
        bring[j].wait()
        wide = blocks[j].astype(F32)
        squares += jnp.sum(wide * wide, axis=-1, keepdims=True)
    scale = lax.rsqrt(squares / features + EPSILON)
    own = own_ref.shape[1]
    first = pl.multiple_of(place_ref[0] * own, own)
    for j in range(n):
        gain = gain_ref[places[j]]
        normed[:, pl.ds(j * chunk, chunk)] = (blocks[j].astype(F32) * scale * gain).astype(BF16)
        own_ref[places[j]] = blocks[j, pl.ds(first, own), :]
    for copy in fetch:
        copy.wait()

    def step(start, width):
        gate = jnp.dot(normed[...], whole[:, pl.ds(start, width)], preferred_element_type=F32)
        upward = jnp.dot(normed[...], whole[:, pl.ds(apart + start, width)], preferred_element_type=F32)
        value = gate * (1.0 / (1.0 + jnp.exp(-gate))) * upward
        hidden_ref[:, pl.ds(start, width)] = value.astype(BF16)

    tile = 256

    @pl.loop(0, units // tile)
    def _(j):
        step(pl.multiple_of(j * tile, tile), tile)

    step(units // tile * tile, units % tile)


def down_kernel(hidden_ref, weight_hbm, out_hbm, weight, out, sems):
    tile = 256
    tiles = weight.shape[0] // tile

    def here(j):
        return pl.ds(pl.multiple_of(j * tile, tile), tile)

    def part(j):
        return pltpu.make_async_copy(weight_hbm.at[here(j), :], weight.at[here(j), :], sems.at[j])

    def result(j):
        return pltpu.make_async_copy(out.at[:, here(j)], out_hbm.at[:, here(j)], sems.at[tiles + j])

    @pl.loop(0, tiles)
    def _(j):
        part(j).start()

    @pl.loop(0, tiles)
    def _(j):
        part(j).wait()
        out[:, here(j)] = turned_dot(hidden_ref[...], weight[here(j), :]).astype(BF16)
        result(j).start()

    @pl.loop(0, tiles)
    def _(j):
        result(j).wait()


def call(kernel, out_shape, specs, flops, scratch=(), mib=16, out_space=VMEM):
    def run(*args):
        moved = sum(a.size * a.dtype.itemsize for a in args)
        return pl.pallas_call(
            kernel,
            out_shape=out_shape,
            in_specs=specs,
            out_specs=jax.tree.map(lambda _: pl.BlockSpec(memory_space=out_space), out_shape),
            scratch_shapes=scratch,
            compiler_params=pltpu.CompilerParams(vmem_limit_bytes=mib << 20),
            cost_estimate=pl.CostEstimate(flops=flops, bytes_accessed=moved, transcendentals=0),
        )(*args)

    return run


def body(
    patches,
    window_ids,
    vit_gain,
    qkv_weight,
    out_weight,
    merge_gain,
    merger_weight,
    audio,
    span_lengths,
    span_time,
    llm_gain,
    gate_weight,
    up_weight,
    down_weight,
):
    patch_count, d_vit = patches.shape
    n = lax.axis_size("tensor")
    owner_count = lax.axis_size("dp")
    owner = lax.axis_index("dp")
    plane = lax.axis_index("tensor")
    core = lax.rem(owner, 2)
    units = gate_weight.shape[1]
    vmem = pl.BlockSpec(memory_space=VMEM)
    smem = pl.BlockSpec(memory_space=SMEM)
    hbm = pl.BlockSpec(memory_space=HBM)

    windows = window_ids[0]
    context = call(
        vision_kernel,
        jax.ShapeDtypeStruct((2 * HEAD_VIT, patch_count), BF16),
        [smem] + [vmem] * 5,
        2 * patch_count * (3 * d_vit * 160 + 4 * patch_count * HEAD_VIT),
    )(
        core.reshape(1),
        patches,
        windows[:, None],
        windows[None, :],
        vit_gain[None, :],
        jnp.swapaxes(qkv_weight, 1, 2),
    )

    group = 2 * HEAD_VIT
    own_head = lax.dynamic_slice_in_dim(out_weight, core * HEAD_VIT, HEAD_VIT, 0)
    above = lax.ppermute(own_head, "tensor", shifted("tensor", 1))
    below = lax.ppermute(own_head, "tensor", shifted("tensor", -1))
    split, block_rows = group * patch_count // 128, HEAD_VIT * d_vit // 128
    payload = jax.ShapeDtypeStruct((split + block_rows, 128), BF16)
    up, down = call(pack_kernel, (payload, payload), [vmem] * 3, 0)(context, above, below)
    ups, downs = [up], [down]
    for k in range(1, n // 2):
        ups.append(lax.ppermute(ups[-1], "tensor", shifted("tensor", 1)))
        away = downs[-1] if k < n // 2 - 1 else downs[-1][:split]
        downs.append(lax.ppermute(away, "tensor", shifted("tensor", -1)))
    ups.append(lax.ppermute(ups[-1][:split], "tensor", shifted("tensor", 1)))
    contexts = [up]
    tall = []
    for k in range(1, n // 2 + 1):
        contexts.append(ups[k])
        if k < n // 2:
            contexts.append(downs[k])
            tall.append(ups[k])
        if k < n // 2 - 1:
            tall.append(downs[k])
    swap = [(i, i ^ 1) for i in range(owner_count)]
    laid = call(
        functools.partial(stack_kernel, 3),
        jax.ShapeDtypeStruct((n - 1, block_rows, 128), BF16),
        [vmem] * (n - 1),
        0,
    )(own_head, above, below, *tall[:-1])
    other = lax.ppermute(laid, "dp", swap)
    last = lax.ppermute(tall[-1], "dp", swap)

    gap = -units % 128
    stacked = jnp.concatenate(
        [gate_weight, jnp.zeros((gate_weight.shape[0], gap), BF16), up_weight], axis=1
    )
    whole = lax.all_gather(stacked, "dp", axis=0, tiled=True)

    video_rows = patch_count // 4
    seq_count = video_rows + audio.shape[0]
    capacity = 2 * seq_count // owner_count
    sent_lengths = span_lengths[owner]
    starts = jnp.cumsum(sent_lengths) - sent_lengths
    slot_index = jnp.arange(capacity, dtype=jnp.int32)
    row_of_slot = jnp.where(
        slot_index[None, :] < sent_lengths[:, None], starts[:, None] + slot_index[None, :], -1
    ).reshape(-1)
    row = jnp.arange(seq_count, dtype=jnp.int32)
    select = (row_of_slot[:, None] == row[None, video_rows:]).astype(BF16)
    from_audio = jnp.dot(select, audio, preferred_element_type=F32).astype(BF16)
    slots = owner_count * capacity
    width = audio.shape[1]
    operands = [*contexts[: n - 1], own_head, above, below, other, patches]
    sofar = call(
        functools.partial(project_kernel, n),
        jax.ShapeDtypeStruct((patch_count, d_vit), F32),
        [hbm] * len(operands),
        2 * patch_count * d_vit * d_vit,
        scratch=[pltpu.VMEM(a.shape, BF16) for a in operands]
        + [
            pltpu.VMEM(((n - 1) * group, patch_count), BF16),
            pltpu.VMEM(((n - 1) * group, d_vit), BF16),
            pltpu.SemaphoreType.DMA((len(operands),)),
        ],
        mib=62,
    )(*operands)
    outgoing = call(
        merge_kernel,
        jax.ShapeDtypeStruct((slots, width), BF16),
        [vmem] * 5 + [hbm, vmem, hbm],
        2 * patch_count * d_vit * width,
        scratch=[
            pltpu.VMEM((group, patch_count), BF16),
            pltpu.VMEM((group, d_vit), BF16),
            pltpu.VMEM((d_vit // 128, patch_count, 128), F32),
            pltpu.VMEM(merger_weight.shape[::-1], BF16),
            pltpu.VMEM((slots, width), BF16),
            pltpu.SemaphoreType.DMA((2,)),
        ],
        mib=62,
    )(
        contexts[n - 1],
        tall[-1],
        last,
        sofar,
        merge_gain[None, :],
        merger_weight.T,
        row_of_slot[:, None],
        from_audio,
    )
    incoming = lax.all_to_all(
        outgoing.reshape(owner_count, capacity, width), "dp", split_axis=0, concat_axis=0, tiled=True
    ).reshape(slots, width)
    taken_lengths = span_lengths[:, owner]
    arrival = span_time[owner]
    earlier = arrival[:, None] < arrival[None, :]
    offsets = jnp.sum(jnp.where(earlier, taken_lengths[:, None], 0), axis=0)
    target = jnp.where(
        slot_index[None, :] < taken_lengths[:, None], offsets[:, None] + slot_index[None, :], -1
    ).reshape(1, -1)
    sequence = call(
        pick_kernel,
        jax.ShapeDtypeStruct((seq_count, width), BF16),
        [vmem] * 2,
        2 * slots * seq_count * width,
        mib=16,
    )(target, incoming)

    down_turned, sequence = lax.optimization_barrier((down_weight.T, sequence))
    down_whole = lax.all_gather(down_turned, "dp", axis=0, tiled=True)

    features = n * width
    own_count = seq_count // n
    got = ring_blocks(sequence, "tensor")
    order = sorted(got)
    hidden, own_rows = call(
        functools.partial(gate_kernel, n, tuple(order), units),
        (
            jax.ShapeDtypeStruct((seq_count, units), BF16),
            jax.ShapeDtypeStruct((n, own_count, width), BF16),
        ),
        [smem] + [hbm] * n + [vmem, hbm],
        4 * seq_count * features * units,
        scratch=[
            pltpu.VMEM((n, seq_count, width), BF16),
            pltpu.VMEM((features, 2 * units + gap), BF16),
            pltpu.VMEM((seq_count, features), BF16),
            pltpu.SemaphoreType.DMA((2 * n,)),
        ],
        mib=62,
    )(plane.reshape(1), *[got[k] for k in order], llm_gain.reshape(n, 1, width), whole)
    terms = call(
        down_kernel,
        jax.ShapeDtypeStruct((seq_count, features), BF16),
        [vmem, hbm],
        2 * seq_count * features * units,
        scratch=[
            pltpu.VMEM((features, units), BF16),
            pltpu.VMEM((seq_count, features), BF16),
            pltpu.SemaphoreType.DMA((2 * (features // 256),)),
        ],
        mib=62,
        out_space=HBM,
    )(hidden, down_whole)
    summed = lax.psum_scatter(terms, "tensor", scatter_dimension=0, tiled=True).astype(F32)
    own_rows = jnp.moveaxis(own_rows, 0, 1).reshape(own_count, features)
    return (own_rows.astype(F32) + summed).astype(BF16)


def solution(mesh):
    return jax.shard_map(
        body,
        mesh=mesh,
        in_specs=(
            P("dp", None),
            P("dp", None),
            P(),
            P(None, None, "tensor"),
            P("tensor", None),
            P(),
            P(None, "tensor"),
            P("dp", "tensor"),
            P(),
            P(),
            P(),
            P("dp", "tensor"),
            P("dp", "tensor"),
            P("tensor", "dp"),
        ),
        out_specs=P(("dp", "tensor"), None),
        check_vma=False,
    )
```

time: 285 us -> 253 us (0.89); the launches traced: 281 us -> 253 us
  waiting for transfers between devices: 149 us -> 137 us
  starting transfers between devices: 42.4 us -> 34.4 us
  local copies, waits for them, and re-layouts: 19.4 us -> 13 us
    ppermute x8 -> x4, waiting for transfers between devices: 50.2 us -> 39.1 us  [ring_blocks(): a = lax.ppermute(a, axis, shifted(axis, 1))]
    reduce_scatter x2 -> x1, waiting for transfers between devices: 44.7 us -> 55.5 us  [body(): lax.psum_scatter(terms, 'tensor', scatter_dimension=0, tiled=True)]
    ppermute x6 -> x3, starting transfers between devices: 16 us -> 6.53 us  [ring_blocks(): b = lax.ppermute(b, axis, shifted(axis, -1))]
    all_to_all x1, waiting for transfers between devices: 25.2 us -> 19.5 us  [body(): lax.all_to_all(outgoing.reshape(owner_count, capacity, width), 'dp', spli...]
    unnamed x70 -> x56, local copies, waits for them, and re-layouts: 9.82 us -> 4.59 us
    ppermute x1, waiting for transfers between devices: 3.06 us -> 0.01 us  [body(): ups.append(lax.ppermute(ups[-1][:split], 'tensor', shifted('tensor', 1)))]
    pallas_call x7 -> x8, Pallas kernels: 51.2 us -> 51.8 us  [run(): pl.pallas_call(kernel, out_shape=out_shape, in_specs=specs, out_specs=jax...]
  transfers between devices with their start and end apart: 29 -> 22, of which waited for: 17 -> 10; matrix products, arithmetic and copies ran while one was open for 4% -> 3% of each run, Pallas kernels for 12% -> 16%
where the time goes in v2:
time: 253 us
  waiting for transfers between devices  137 us (54%)
  Pallas kernels  51.8 us (20%)
  starting transfers between devices  34.4 us (14%)
  between operations  13.5 us (5%)
  local copies, waits for them, and re-layouts  13 us (5%)
    reduce_scatter x1, waiting for transfers between devices, body(): lax.psum_scatter(terms, 'tensor', scatter_dimension=0, tiled=True)  55.5 us
    pallas_call x8, Pallas kernels, run(): pl.pallas_call(kernel, out_shape=out_shape, in_specs=specs, out_specs=jax...  51.8 us
    ppermute x4, waiting for transfers between devices, ring_blocks(): a = lax.ppermute(a, axis, shifted(axis, 1))  39.1 us
    ppermute x3, waiting for transfers between devices, body(): ups.append(lax.ppermute(ups[-1], 'tensor', shifted('tensor', 1)))  22.3 us
    all_to_all x1, waiting for transfers between devices, body(): lax.all_to_all(outgoing.reshape(owner_count, capacity, width), 'dp', spli...  19.5 us
    ppermute x3, starting transfers between devices, body(): downs.append(lax.ppermute(away, 'tensor', shifted('tensor', -1)))  8.14 us
    all_to_all x1, starting transfers between devices, body(): lax.all_to_all(outgoing.reshape(owner_count, capacity, width), 'dp', spli...  7.34 us
    ppermute x3, starting transfers between devices, ring_blocks(): b = lax.ppermute(b, axis, shifted(axis, -1))  6.53 us
  transfers between devices with their start and end apart: 22, of which 10 were waited for; matrix products, arithmetic and copies ran while one was open for 3% of the time, Pallas kernels for 16%

profile of v2, /device:TPU:1, one launch (start us, length us, event | category | flops | bytes accessed | tf_op | source)
XLA Modules:
  0.0 252.8 jit_solution(16454636300843031102)
XLA Ops:
  6.6 2.0 concatenate.3
  8.7 2.5 %collective-permute-start = (bf16[80,1280]{1,0:T(8,128)(2,1)S(1)}, bf16[80,1280]{1,0:T(8,128)(2,1)S(1)}, u32[]{:S(2)}, u32[]{:S(2)}) collective-permute-start(bf16[80,1280]{1,0:T(8,128)(2,1)S(1)} %constant_dynamic-slice_fusion.1.refs_0_.refs_7_), channel_id=1, source_target_pairs={{0,1},{1,2},{2,3},{3,4},{4,5},{5,6},{6,7},{7,0},{8,9},{9,10},{10,1... | collective-permute-start | bytes 614408 | tf_op jit(solution)/shard_map/ppermute | solution.py:310
  11.3 4.0 %collective-permute-start.1 = (bf16[80,1280]{1,0:T(8,128)(2,1)S(1)}, bf16[80,1280]{1,0:T(8,128)(2,1)S(1)}, u32[]{:S(2)}, u32[]{:S(2)}) collective-permute-start(bf16[80,1280]{1,0:T(8,128)(2,1)S(1)} %constant_dynamic-slice_fusion.1.refs_0_.refs_7_), channel_id=1, source_target_pairs={{0,7},{1,0},{2,1},{3,2},{4,3},{5,4},{6,5},{7,6},{8,15},{9,8},{10,9... | collective-permute-start | bytes 614408 | tf_op jit(solution)/shard_map/ppermute | solution.py:311
  15.3 0.1 copy.23.column_ref
  15.5 1.3 copy-done.9
  16.8 2.9 %shard_map.136.context_ref = bf16[160,512]{1,0:T(8,128)(2,1)S(1)} custom-call(s32[1]{0:T(128)} %bitcast.3.core_ref, bf16[512,1280]{1,0:T(8,128)(2,1)S(1)} %copy-done.1, s32[512,1]{1,0:T(8,128)S(1)} %copy.23.column_ref, s32[1,512]{1,0:T(1,128)S(1)} %copy-done.11, f32[1,1280]{1,0:T(1,128)S(1)} %broadcast_in_dim.33.gain_ref, bf16[3,160,1280]{2,1,0:T(8,128)(2,1)S(1)} %bitcast.18), custom_call_target="tpu_custom_call" | custom-call | flops 796917760 | bytes 2548740 | tf_op jit(solution)/shard_map/pallas_call | solution.py:253
  19.7 0.3 collective-permute-done.above_ref.refs_1_.refs_8_
  20.3 2.6 %collective-permute-start.7 = (bf16[1440,128]{1,0:T(8,128)(2,1)S(1)}, bf16[1440,128]{1,0:T(8,128)(2,1)S(1)}, u32[]{:S(2)}, u32[]{:S(2)}) collective-permute-start(bf16[1440,128]{1,0:T(8,128)(2,1)S(1)} %get-tuple-element.12), channel_id=1, source_target_pairs={{0,7},{1,0},{2,1},{3,2},{4,3},{5,4},{6,5},{7,6},{8,15},{9,8},{10,9... | collective-permute-start | bytes 1105928 | tf_op jit(solution)/shard_map/ppermute | solution.py:319
  22.9 7.4 %collective-permute-done.2.refs_3_.refs_1_ = bf16[1440,128]{1,0:T(8,128)(2,1)S(1)} collective-permute-done((bf16[1440,128]{1,0:T(8,128)(2,1)S(1)}, bf16[1440,128]{1,0:T(8,128)(2,1)S(1)}, u32[]{:S(2)}, u32[]{:S(2)}) %collective-permute-start.2) | collective-permute-done | bytes 368672 | tf_op jit(solution)/shard_map/ppermute | solution.py:317
  30.3 2.7 %collective-permute-start.8 = (bf16[1440,128]{1,0:T(8,128)(2,1)S(1)}, bf16[1440,128]{1,0:T(8,128)(2,1)S(1)}, u32[]{:S(2)}, u32[]{:S(2)}) collective-permute-start(bf16[1440,128]{1,0:T(8,128)(2,1)S(1)} %collective-permute-done.7.refs_4_.refs_2_), channel_id=1, source_target_pairs={{0,7},{1,0},{2,1},{3,2},{4,3},{5,4},{6,5},{7,6},{8,15},{9,8},{10,9... | collective-permute-start | bytes 1105928 | tf_op jit(solution)/shard_map/ppermute | solution.py:319
  33.0 6.5 %collective-permute-done.3.refs_5_.refs_3_ = bf16[1440,128]{1,0:T(8,128)(2,1)S(1)} collective-permute-done((bf16[1440,128]{1,0:T(8,128)(2,1)S(1)}, bf16[1440,128]{1,0:T(8,128)(2,1)S(1)}, u32[]{:S(2)}, u32[]{:S(2)}) %collective-permute-start.3) | collective-permute-done | bytes 368672 | tf_op jit(solution)/shard_map/ppermute | solution.py:317
  39.6 1.3 shard_map.138
  40.9 3.1 %collective-permute-start.10 = (bf16[7,800,128]{2,1,0:T(8,128)(2,1)}, bf16[7,800,128]{2,1,0:T(8,128)(2,1)}, u32[]{:S(2)}, u32[]{:S(2)}) collective-permute-start(bf16[7,800,128]{2,1,0:T(8,128)(2,1)} %shard_map.138), channel_id=1, source_target_pairs={{0,8},{8,0},{16,24},{24,16},{32,40},{40,32},{48,56},{56,48},{64,72... | collective-permute-start | bytes 4300808 | tf_op jit(solution)/shard_map/ppermute | solution.py:337
  44.5 2.8 %collective-permute-start.9 = (bf16[640,128]{1,0:T(8,128)(2,1)S(1)}, bf16[640,128]{1,0:T(8,128)(2,1)S(1)}, u32[]{:S(2)}, u32[]{:S(2)}) collective-permute-start(bf16[640,128]{1,0:T(8,128)(2,1)S(1)} %slice.13), channel_id=1, source_target_pairs={{0,7},{1,0},{2,1},{3,2},{4,3},{5,4},{6,5},{7,6},{8,15},{9,8},{10,9... | collective-permute-start | bytes 491528 | tf_op jit(solution)/shard_map/ppermute | solution.py:319
  47.3 8.5 %collective-permute-done.4.refs_5_.refs_1_ = bf16[1440,128]{1,0:T(8,128)(2,1)S(1)} collective-permute-done((bf16[1440,128]{1,0:T(8,128)(2,1)S(1)}, bf16[1440,128]{1,0:T(8,128)(2,1)S(1)}, u32[]{:S(2)}, u32[]{:S(2)}) %collective-permute-start.4) | collective-permute-done | bytes 368672 | tf_op jit(solution)/shard_map/ppermute | solution.py:317
  55.9 1.1 collective-permute-start.6
  56.9 0.8 fusion.2
  57.7 1.3 select_n.51.refs_6_
  59.0 1.3 copy.26.refs_7_
  60.3 0.6 broadcast_in_dim.34.refs_4_
  60.9 0.7 copy-done.17
  61.6 7.2 %shard_map.139.refs_3_ = f32[512,1280]{1,0:T(8,128)} custom-call(bf16[1440,128]{1,0:T(8,128)(2,1)} %copy-done.10, bf16[1440,128]{1,0:T(8,128)(2,1)} %copy-done.6, bf16[1440,128]{1,0:T(8,128)(2,1)} %copy-done.7, bf16[1440,128]{1,0:T(8,128)(2,1)} %copy-done.8, bf16[1440,128]{1,0:T(8,128)(2,1)} %copy-done.2, bf16[1440,128]{1,0:T(8,128)(2,1)} %copy-done.13, ...), custom_call_target="tpu_custom_call" | custom-call | flops 1677721600 | bytes 5734400 | tf_op jit(solution)/shard_map/pallas_call | solution.py:253
  68.8 0.6 copy-done.16
  69.5 0.1 copy-done.15
  69.6 7.8 %shard_map.140 = bf16[1024,448]{1,0:T(8,128)(2,1)} custom-call(bf16[640,128]{1,0:T(8,128)(2,1)} %copy-done.16, bf16[1440,128]{1,0:T(8,128)(2,1)} %copy-done.13, bf16[1440,128]{1,0:T(8,128)(2,1)} %copy-done.15, f32[512,1280]{1,0:T(8,128)} %shard_map.139.refs_3_, f32[1,1280]{1,0:T(1,128)} %broadcast_in_dim.34.refs_4_, bf16[448,5120]{1,0:T(8,128)(2,1)} %bitcast.21, ...), custom_call_target="tpu_custom_call" | custom-call | flops 587202560 | bytes 9036800 | tf_op jit(solution)/shard_map/pallas_call | solution.py:253
  77.4 7.3 %all-to-all-start = ((bf16[32,32,448]{2,1,0:T(8,128)(2,1)}), bf16[32,32,448]{2,1,0:T(8,128)(2,1)S(1)}, u32[]{:S(2)}, u32[]{:S(2)}) async-start(bf16[32,32,448]{2,1,0:T(8,128)(2,1)} %bitcast.22), calls=%async_computation | async-start | bytes 2097152 | tf_op jit(solution)/shard_map/all_to_all | solution.py:398
  84.8 0.2 dynamic-slice_reduce_fusion
  85.0 0.7 fusion.7
  85.9 19.5 %all-to-all-done = bf16[32,32,448]{2,1,0:T(8,128)(2,1)S(1)} async-done(((bf16[32,32,448]{2,1,0:T(8,128)(2,1)}), bf16[32,32,448]{2,1,0:T(8,128)(2,1)S(1)}, u32[]{:S(2)}, u32[]{:S(2)}) %all-to-all-start) | async-done | bytes 917536 | tf_op jit(solution)/shard_map/all_to_all | solution.py:398
  105.4 0.7 shard_map.141.refs_4_
  106.2 1.4 collective-permute-start.11
  107.6 1.8 collective-permute-start.15
  109.4 10.6 %collective-permute-done.11.refs_3_ = bf16[512,448]{1,0:T(8,128)(2,1)S(1)} collective-permute-done((bf16[512,448]{1,0:T(8,128)(2,1)S(1)}, bf16[512,448]{1,0:T(8,128)(2,1)S(1)}, u32[]{:S(2)}, u32[]{:S(2)}) %collective-permute-start.11) | collective-permute-done | bytes 458784 | tf_op jit(solution)/shard_map/ppermute | solution.py:30
  120.1 2.7 %collective-permute-start.16 = (bf16[512,448]{1,0:T(8,128)(2,1)S(1)}, bf16[512,448]{1,0:T(8,128)(2,1)S(1)}, u32[]{:S(2)}, u32[]{:S(2)}) collective-permute-start(bf16[512,448]{1,0:T(8,128)(2,1)S(1)} %collective-permute-done.15.refs_5_), channel_id=1, source_target_pairs={{0,7},{1,0},{2,1},{3,2},{4,3},{5,4},{6,5},{7,6},{8,15},{9,8},{10,9... | collective-permute-start | bytes 1376264 | tf_op jit(solution)/shard_map/ppermute | solution.py:33
  122.7 9.8 %collective-permute-done.12.refs_2_ = bf16[512,448]{1,0:T(8,128)(2,1)S(1)} collective-permute-done((bf16[512,448]{1,0:T(8,128)(2,1)S(1)}, bf16[512,448]{1,0:T(8,128)(2,1)S(1)}, u32[]{:S(2)}, u32[]{:S(2)}) %collective-permute-start.12) | collective-permute-done | bytes 458784 | tf_op jit(solution)/shard_map/ppermute | solution.py:30
  132.5 0.8 copy-done.24
  133.3 2.0 collective-permute-start.17
  135.4 8.7 %collective-permute-done.13.refs_1_ = bf16[512,448]{1,0:T(8,128)(2,1)S(1)} collective-permute-done((bf16[512,448]{1,0:T(8,128)(2,1)S(1)}, bf16[512,448]{1,0:T(8,128)(2,1)S(1)}, u32[]{:S(2)}, u32[]{:S(2)}) %collective-permute-start.13) | collective-permute-done | bytes 458784 | tf_op jit(solution)/shard_map/ppermute | solution.py:30
  144.1 0.8 reshape.164.refs_8_
  144.9 10.0 %collective-permute-done.14.refs_0_ = bf16[512,448]{1,0:T(8,128)(2,1)} collective-permute-done((bf16[512,448]{1,0:T(8,128)(2,1)S(1)}, bf16[512,448]{1,0:T(8,128)(2,1)}, u32[]{:S(2)}, u32[]{:S(2)}) %collective-permute-start.14) | collective-permute-done | bytes 458784 | tf_op jit(solution)/shard_map/ppermute | solution.py:30
  154.8 20.8 %shard_map.142 = (bf16[512,1184]{1,0:T(8,128)(2,1)}, bf16[8,64,448]{2,1,0:T(8,128)(2,1)}) custom-call(s32[1]{0:T(128)} %bitcast.place_ref, bf16[512,448]{1,0:T(8,128)(2,1)} %collective-permute-done.14.refs_0_, bf16[512,448]{1,0:T(8,128)(2,1)} %copy-done.26, bf16[512,448]{1,0:T(8,128)(2,1)} %copy-done.24, bf16[512,448]{1,0:T(8,128)(2,1)} %copy-done.22, ...), custom_call_target="tpu_custom_call" | custom-call | flops 8690597888 | bytes 21346308 | tf_op jit(solution)/shard_map/pallas_call | solution.py:253
  175.6 11.0 %shard_map.143 = bf16[512,3584]{1,0:T(8,128)(2,1)} custom-call(bf16[512,1184]{1,0:T(8,128)(2,1)} %get-tuple-element.15.hidden_ref, bf16[3584,1184]{1,0:T(8,128)(2,1)} %all-gather.5.cloned.1.call-done.weight_hbm), custom_call_target="tpu_custom_call" | custom-call | flops 4345298944 | bytes 9699328 | tf_op jit(solution)/shard_map/pallas_call | solution.py:253
  186.7 1.0 copy-done.14
  187.7 0.1 convert_bitcast_fusion
  187.8 0.6 copy.27
  188.4 0.4 reshape.165
  188.9 55.5 %reduce-scatter.2.cloned.1.call-done = bf16[64,3584]{1,0:T(8,128)(2,1)} async-done(((bf16[512,3584]{1,0:T(8,128)(2,1)}), bf16[64,3584]{1,0:T(8,128)(2,1)}) %reduce-scatter.2.cloned.1.call-update) | async-done | bytes 458768 | tf_op jit(solution)/shard_map/reduce_scatter | solution.py:452
  244.4 1.9 add_convert_fusion
  (93 shorter events, 1.4 us)
Async XLA Ops:
  6.5 2.1 copy-start
  6.5 8.8 %copy-start.11 = (s32[1,512]{1,0:T(1,128)S(1)}, s32[1,512]{1,0:T(1,128)}, u32[]{:S(2)}) copy-start(s32[1,512]{1,0:T(1,128)} %row_ref.1) | copy-start | bytes 6148
  6.5 8.9 %copy-start.20 = (f32[1280]{0:T(1024)S(1)}, f32[1280]{0:T(1024)}, u32[]{:S(2)}) copy-start(f32[1280]{0:T(1024)} %param.16) | copy-start | bytes 15364
  6.5 8.9 %copy-start.1 = (bf16[512,1280]{1,0:T(8,128)(2,1)S(1)}, bf16[512,1280]{1,0:T(8,128)(2,1)}, u32[]{:S(2)}) copy-start(bf16[512,1280]{1,0:T(8,128)(2,1)} %refs_11_.1) | copy-start | bytes 3932164
  6.5 148.3 %all-gather.3.cloned.1.call-start = ((), (), s32[]{:S(2)}) async-start(), calls=%async_computation.2 | async-start | bytes 18923520 | tf_op jit(solution)/shard_map/all_gather | solution.py:344
  8.7 30.8 %copy-start.3 = (bf16[80,1280]{1,0:T(8,128)(2,1)}, bf16[80,1280]{1,0:T(8,128)(2,1)S(1)}, u32[]{:S(2)}) copy-start(bf16[80,1280]{1,0:T(8,128)(2,1)S(1)} %constant_dynamic-slice_fusion.1.refs_0_.refs_7_) | copy-start | bytes 614404
  8.7 11.3 %collective-permute-start = (bf16[80,1280]{1,0:T(8,128)(2,1)S(1)}, bf16[80,1280]{1,0:T(8,128)(2,1)S(1)}, u32[]{:S(2)}, u32[]{:S(2)}) collective-permute-start(bf16[80,1280]{1,0:T(8,128)(2,1)S(1)} %constant_dynamic-slice_fusion.1.refs_0_.refs_7_), channel_id=1, source_target_pairs={{0,1},{1,2},{2,3},{3,4},{4,5},{5,6},{6,7},{7,0},{8,9},{9,10},{10,1... | collective-permute-start | bytes 614408 | tf_op jit(solution)/shard_map/ppermute | solution.py:310
  11.3 8.7 %collective-permute-start.1 = (bf16[80,1280]{1,0:T(8,128)(2,1)S(1)}, bf16[80,1280]{1,0:T(8,128)(2,1)S(1)}, u32[]{:S(2)}, u32[]{:S(2)}) collective-permute-start(bf16[80,1280]{1,0:T(8,128)(2,1)S(1)} %constant_dynamic-slice_fusion.1.refs_0_.refs_7_), channel_id=1, source_target_pairs={{0,7},{1,0},{2,1},{3,2},{4,3},{5,4},{6,5},{7,6},{8,15},{9,8},{10,9... | collective-permute-start | bytes 614408 | tf_op jit(solution)/shard_map/ppermute | solution.py:311
  15.5 1.3 copy-start.9
  20.0 20.9 %copy-start.4 = (bf16[80,1280]{1,0:T(8,128)(2,1)}, bf16[80,1280]{1,0:T(8,128)(2,1)S(1)}, u32[]{:S(2)}) copy-start(bf16[80,1280]{1,0:T(8,128)(2,1)S(1)} %collective-permute-done.above_ref.refs_1_.refs_8_) | copy-start | bytes 614404
  20.0 20.9 %copy-start.5 = (bf16[80,1280]{1,0:T(8,128)(2,1)}, bf16[80,1280]{1,0:T(8,128)(2,1)S(1)}, u32[]{:S(2)}) copy-start(bf16[80,1280]{1,0:T(8,128)(2,1)S(1)} %collective-permute-done.1.below_ref.refs_2_.refs_9_) | copy-start | bytes 614404
  20.1 10.2 %copy-start.10 = (bf16[1440,128]{1,0:T(8,128)(2,1)}, bf16[1440,128]{1,0:T(8,128)(2,1)S(1)}, u32[]{:S(2)}) copy-start(bf16[1440,128]{1,0:T(8,128)(2,1)S(1)} %get-tuple-element.11.refs_0_) | copy-start | bytes 1105924
  20.1 10.1 %collective-permute-start.2 = (bf16[1440,128]{1,0:T(8,128)(2,1)S(1)}, bf16[1440,128]{1,0:T(8,128)(2,1)S(1)}, u32[]{:S(2)}, u32[]{:S(2)}) collective-permute-start(bf16[1440,128]{1,0:T(8,128)(2,1)S(1)} %get-tuple-element.11.refs_0_), channel_id=1, source_target_pairs={{0,1},{1,2},{2,3},{3,4},{4,5},{5,6},{6,7},{7,0},{8,9},{9,10},{10,1... | collective-permute-start | bytes 1105928 | tf_op jit(solution)/shard_map/ppermute | solution.py:317
  20.2 23.7 %copy-start.18 = (s32[32,32]{1,0:T(8,128)S(1)}, s32[32,32]{1,0:T(8,128)}, u32[]{:S(2)}) copy-start(s32[32,32]{1,0:T(8,128)} %param.22) | copy-start | bytes 12292
  20.2 36.7 %copy-start.27 = (bf16[384,448]{0,1:T(8,128)(2,1)S(1)}, bf16[384,448]{0,1:T(8,128)(2,1)}, u32[]{:S(2)}) copy-start(bf16[384,448]{0,1:T(8,128)(2,1)} %param.21) | copy-start | bytes 1032196
  20.3 10.0 %collective-permute-start.7 = (bf16[1440,128]{1,0:T(8,128)(2,1)S(1)}, bf16[1440,128]{1,0:T(8,128)(2,1)S(1)}, u32[]{:S(2)}, u32[]{:S(2)}) collective-permute-start(bf16[1440,128]{1,0:T(8,128)(2,1)S(1)} %get-tuple-element.12), channel_id=1, source_target_pairs={{0,7},{1,0},{2,1},{3,2},{4,3},{5,4},{6,5},{7,6},{8,15},{9,8},{10,9... | collective-permute-start | bytes 1105928 | tf_op jit(solution)/shard_map/ppermute | solution.py:319
  30.3 10.6 %copy-start.6 = (bf16[1440,128]{1,0:T(8,128)(2,1)}, bf16[1440,128]{1,0:T(8,128)(2,1)S(1)}, u32[]{:S(2)}) copy-start(bf16[1440,128]{1,0:T(8,128)(2,1)S(1)} %collective-permute-done.2.refs_3_.refs_1_) | copy-start | bytes 1105924
  30.3 9.2 %collective-permute-start.3 = (bf16[1440,128]{1,0:T(8,128)(2,1)S(1)}, bf16[1440,128]{1,0:T(8,128)(2,1)S(1)}, u32[]{:S(2)}, u32[]{:S(2)}) collective-permute-start(bf16[1440,128]{1,0:T(8,128)(2,1)S(1)} %collective-permute-done.2.refs_3_.refs_1_), channel_id=1, source_target_pairs={{0,1},{1,2},{2,3},{3,4},{4,5},{5,6},{6,7},{7,0},{8,9},{9,10},{10,1... | collective-permute-start | bytes 1105928 | tf_op jit(solution)/shard_map/ppermute | solution.py:317
  30.3 10.6 %copy-start.7 = (bf16[1440,128]{1,0:T(8,128)(2,1)}, bf16[1440,128]{1,0:T(8,128)(2,1)S(1)}, u32[]{:S(2)}) copy-start(bf16[1440,128]{1,0:T(8,128)(2,1)S(1)} %collective-permute-done.7.refs_4_.refs_2_) | copy-start | bytes 1105924
  30.3 9.2 %collective-permute-start.8 = (bf16[1440,128]{1,0:T(8,128)(2,1)S(1)}, bf16[1440,128]{1,0:T(8,128)(2,1)S(1)}, u32[]{:S(2)}, u32[]{:S(2)}) collective-permute-start(bf16[1440,128]{1,0:T(8,128)(2,1)S(1)} %collective-permute-done.7.refs_4_.refs_2_), channel_id=1, source_target_pairs={{0,7},{1,0},{2,1},{3,2},{4,3},{5,4},{6,5},{7,6},{8,15},{9,8},{10,9... | collective-permute-start | bytes 1105928 | tf_op jit(solution)/shard_map/ppermute | solution.py:319
  39.5 4.7 %copy-start.8 = (bf16[1440,128]{1,0:T(8,128)(2,1)}, bf16[1440,128]{1,0:T(8,128)(2,1)S(1)}, u32[]{:S(2)}) copy-start(bf16[1440,128]{1,0:T(8,128)(2,1)S(1)} %collective-permute-done.3.refs_5_.refs_3_) | copy-start | bytes 1105924
  39.5 5.0 %copy-start.2 = (bf16[1440,128]{1,0:T(8,128)(2,1)}, bf16[1440,128]{1,0:T(8,128)(2,1)S(1)}, u32[]{:S(2)}) copy-start(bf16[1440,128]{1,0:T(8,128)(2,1)S(1)} %collective-permute-done.8.refs_6_.refs_4_) | copy-start | bytes 1105924
  40.9 20.0 %collective-permute-start.10 = (bf16[7,800,128]{2,1,0:T(8,128)(2,1)}, bf16[7,800,128]{2,1,0:T(8,128)(2,1)}, u32[]{:S(2)}, u32[]{:S(2)}) collective-permute-start(bf16[7,800,128]{2,1,0:T(8,128)(2,1)} %shard_map.138), channel_id=1, source_target_pairs={{0,8},{8,0},{16,24},{24,16},{32,40},{40,32},{48,56},{56,48},{64,72... | collective-permute-start | bytes 4300808 | tf_op jit(solution)/shard_map/ppermute | solution.py:337
  44.2 11.5 %collective-permute-start.4 = (bf16[1440,128]{1,0:T(8,128)(2,1)S(1)}, bf16[1440,128]{1,0:T(8,128)(2,1)S(1)}, u32[]{:S(2)}, u32[]{:S(2)}) collective-permute-start(bf16[1440,128]{1,0:T(8,128)(2,1)S(1)} %collective-permute-done.3.refs_5_.refs_3_), channel_id=1, source_target_pairs={{0,1},{1,2},{2,3},{3,4},{4,5},{5,6},{6,7},{7,0},{8,9},{9,10},{10,1... | collective-permute-start | bytes 1105928 | tf_op jit(solution)/shard_map/ppermute | solution.py:317
  44.5 16.4 %collective-permute-start.9 = (bf16[640,128]{1,0:T(8,128)(2,1)S(1)}, bf16[640,128]{1,0:T(8,128)(2,1)S(1)}, u32[]{:S(2)}, u32[]{:S(2)}) collective-permute-start(bf16[640,128]{1,0:T(8,128)(2,1)S(1)} %slice.13), channel_id=1, source_target_pairs={{0,7},{1,0},{2,1},{3,2},{4,3},{5,4},{6,5},{7,6},{8,15},{9,8},{10,9... | collective-permute-start | bytes 491528 | tf_op jit(solution)/shard_map/ppermute | solution.py:319
  55.8 4.6 %copy-start.13 = (bf16[1440,128]{1,0:T(8,128)(2,1)}, bf16[1440,128]{1,0:T(8,128)(2,1)S(1)}, u32[]{:S(2)}) copy-start(bf16[1440,128]{1,0:T(8,128)(2,1)S(1)} %collective-permute-done.4.refs_5_.refs_1_) | copy-start | bytes 1105924
  55.8 13.0 %collective-permute-start.5 = (bf16[640,128]{1,0:T(8,128)(2,1)S(1)}, bf16[640,128]{1,0:T(8,128)(2,1)S(1)}, u32[]{:S(2)}, u32[]{:S(2)}) collective-permute-start(bf16[640,128]{1,0:T(8,128)(2,1)S(1)} %slice.12), channel_id=1, source_target_pairs={{0,1},{1,2},{2,3},{3,4},{4,5},{5,6},{6,7},{7,0},{8,9},{9,10},{10,1... | collective-permute-start | bytes 491528 | tf_op jit(solution)/shard_map/ppermute | solution.py:320
  55.9 12.9 %collective-permute-start.6 = (bf16[1440,128]{1,0:T(8,128)(2,1)S(1)}, bf16[1440,128]{1,0:T(8,128)(2,1)S(1)}, u32[]{:S(2)}, u32[]{:S(2)}) collective-permute-start(bf16[1440,128]{1,0:T(8,128)(2,1)S(1)} %collective-permute-done.4.refs_5_.refs_1_), channel_id=1, source_target_pairs={{0,8},{8,0},{16,24},{24,16},{32,40},{40,32},{48,56},{56,48},{64,72... | collective-permute-start | bytes 1105928 | tf_op jit(solution)/shard_map/ppermute | solution.py:338
  57.7 2.6 %copy-start.21 = (f32[1280]{0:T(1024)S(1)}, f32[1280]{0:T(1024)}, u32[]{:S(2)}) copy-start(f32[1280]{0:T(1024)} %param.19) | copy-start | bytes 15364
  68.8 0.8 copy-start.15
  77.4 66.7 %copy-start.19 = (f32[3584]{0:T(1024)S(1)}, f32[3584]{0:T(1024)}, u32[]{:S(2)}) copy-start(f32[3584]{0:T(1024)} %param.24) | copy-start | bytes 43012
  77.4 28.0 %all-to-all-start = ((bf16[32,32,448]{2,1,0:T(8,128)(2,1)}), bf16[32,32,448]{2,1,0:T(8,128)(2,1)S(1)}, u32[]{:S(2)}, u32[]{:S(2)}) async-start(bf16[32,32,448]{2,1,0:T(8,128)(2,1)} %bitcast.22), calls=%async_computation | async-start | bytes 2097152 | tf_op jit(solution)/shard_map/all_to_all | solution.py:398
  84.8 90.9 %all-gather.5.cloned.1.call-start = ((), (), s32[]{:S(2)}) async-start(), calls=%async_computation.3 | async-start | bytes 9461760 | tf_op jit(solution)/shard_map/all_gather | solution.py:417
  106.1 48.7 %copy-start.12 = (bf16[512,448]{1,0:T(8,128)(2,1)}, bf16[512,448]{1,0:T(8,128)(2,1)S(1)}, u32[]{:S(2)}) copy-start(bf16[512,448]{1,0:T(8,128)(2,1)S(1)} %shard_map.141.refs_4_) | copy-start | bytes 1376260
  106.1 138.2 %reduce-scatter.2.cloned.1.call-start = ((), (), s32[]{:S(2)}) async-start(), calls=%async_computation.4 | async-start | bytes 4128768 | tf_op jit(solution)/shard_map/reduce_scatter | solution.py:452
  106.2 13.8 %collective-permute-start.11 = (bf16[512,448]{1,0:T(8,128)(2,1)S(1)}, bf16[512,448]{1,0:T(8,128)(2,1)S(1)}, u32[]{:S(2)}, u32[]{:S(2)}) collective-permute-start(bf16[512,448]{1,0:T(8,128)(2,1)S(1)} %shard_map.141.refs_4_), channel_id=1, source_target_pairs={{0,1},{1,2},{2,3},{3,4},{4,5},{5,6},{6,7},{7,0},{8,9},{9,10},{10,1... | collective-permute-start | bytes 1376264 | tf_op jit(solution)/shard_map/ppermute | solution.py:30
  107.6 12.5 %collective-permute-start.15 = (bf16[512,448]{1,0:T(8,128)(2,1)S(1)}, bf16[512,448]{1,0:T(8,128)(2,1)S(1)}, u32[]{:S(2)}, u32[]{:S(2)}) collective-permute-start(bf16[512,448]{1,0:T(8,128)(2,1)S(1)} %shard_map.141.refs_4_), channel_id=1, source_target_pairs={{0,7},{1,0},{2,1},{3,2},{4,3},{5,4},{6,5},{7,6},{8,15},{9,8},{10,9... | collective-permute-start | bytes 1376264 | tf_op jit(solution)/shard_map/ppermute | solution.py:33
  120.0 34.8 %copy-start.22 = (bf16[512,448]{1,0:T(8,128)(2,1)}, bf16[512,448]{1,0:T(8,128)(2,1)S(1)}, u32[]{:S(2)}) copy-start(bf16[512,448]{1,0:T(8,128)(2,1)S(1)} %collective-permute-done.11.refs_3_) | copy-start | bytes 1376260
  120.0 12.5 %collective-permute-start.12 = (bf16[512,448]{1,0:T(8,128)(2,1)S(1)}, bf16[512,448]{1,0:T(8,128)(2,1)S(1)}, u32[]{:S(2)}, u32[]{:S(2)}) collective-permute-start(bf16[512,448]{1,0:T(8,128)(2,1)S(1)} %collective-permute-done.11.refs_3_), channel_id=1, source_target_pairs={{0,1},{1,2},{2,3},{3,4},{4,5},{5,6},{6,7},{7,0},{8,9},{9,10},{10,1... | collective-permute-start | bytes 1376264 | tf_op jit(solution)/shard_map/ppermute | solution.py:30
  120.0 34.8 %copy-start.23 = (bf16[512,448]{1,0:T(8,128)(2,1)}, bf16[512,448]{1,0:T(8,128)(2,1)S(1)}, u32[]{:S(2)}) copy-start(bf16[512,448]{1,0:T(8,128)(2,1)S(1)} %collective-permute-done.15.refs_5_) | copy-start | bytes 1376260
  120.1 12.5 %collective-permute-start.16 = (bf16[512,448]{1,0:T(8,128)(2,1)S(1)}, bf16[512,448]{1,0:T(8,128)(2,1)S(1)}, u32[]{:S(2)}, u32[]{:S(2)}) collective-permute-start(bf16[512,448]{1,0:T(8,128)(2,1)S(1)} %collective-permute-done.15.refs_5_), channel_id=1, source_target_pairs={{0,7},{1,0},{2,1},{3,2},{4,3},{5,4},{6,5},{7,6},{8,15},{9,8},{10,9... | collective-permute-start | bytes 1376264 | tf_op jit(solution)/shard_map/ppermute | solution.py:33
  132.5 0.8 copy-start.24
  132.5 11.6 %collective-permute-start.13 = (bf16[512,448]{1,0:T(8,128)(2,1)S(1)}, bf16[512,448]{1,0:T(8,128)(2,1)S(1)}, u32[]{:S(2)}, u32[]{:S(2)}) collective-permute-start(bf16[512,448]{1,0:T(8,128)(2,1)S(1)} %collective-permute-done.12.refs_2_), channel_id=1, source_target_pairs={{0,1},{1,2},{2,3},{3,4},{4,5},{5,6},{6,7},{7,0},{8,9},{9,10},{10,1... | collective-permute-start | bytes 1376264 | tf_op jit(solution)/shard_map/ppermute | solution.py:30
  133.3 11.6 %copy-start.25 = (bf16[512,448]{1,0:T(8,128)(2,1)}, bf16[512,448]{1,0:T(8,128)(2,1)S(1)}, u32[]{:S(2)}) copy-start(bf16[512,448]{1,0:T(8,128)(2,1)S(1)} %collective-permute-done.16.refs_6_) | copy-start | bytes 1376260
  133.3 11.6 %collective-permute-start.17 = (bf16[512,448]{1,0:T(8,128)(2,1)S(1)}, bf16[512,448]{1,0:T(8,128)(2,1)}, u32[]{:S(2)}, u32[]{:S(2)}) collective-permute-start(bf16[512,448]{1,0:T(8,128)(2,1)S(1)} %collective-permute-done.16.refs_6_), channel_id=1, source_target_pairs={{0,7},{1,0},{2,1},{3,2},{4,3},{5,4},{6,5},{7,6},{8,15},{9,8},{10,9... | collective-permute-start | bytes 1376264 | tf_op jit(solution)/shard_map/ppermute | solution.py:33
  144.1 0.8 copy-start.26
  144.1 10.7 %collective-permute-start.14 = (bf16[512,448]{1,0:T(8,128)(2,1)S(1)}, bf16[512,448]{1,0:T(8,128)(2,1)}, u32[]{:S(2)}, u32[]{:S(2)}) collective-permute-start(bf16[512,448]{1,0:T(8,128)(2,1)S(1)} %collective-permute-done.13.refs_1_), channel_id=1, source_target_pairs={{0,1},{1,2},{2,3},{3,4},{4,5},{5,6},{6,7},{7,0},{8,9},{9,10},{10,1... | collective-permute-start | bytes 1376264 | tf_op jit(solution)/shard_map/ppermute | solution.py:30
  186.7 1.0 copy-start.14
  (2 other events, 1.3 us)
Sparse Core Ops, SparseCore 0:
  9.9 94.2 all-gather.2
  106.7 61.6 all-gather.4
  186.8 57.5 reduce-scatter.1

commit v3 on v2

--- a/solution.py
+++ b/solution.py
@@ -174,43 +174,83 @@
     out_ref[...] = jnp.dot(pick, incoming_ref[...], preferred_element_type=F32).astype(BF16)
 
 
-def gate_kernel(n, shifts, units, place_ref, *refs):
-    sources, gain_ref, whole_hbm, hidden_ref, own_ref = refs[:n], refs[n], refs[n + 1], refs[n + 2], refs[n + 3]
-    blocks, whole, normed, sems = refs[n + 4 :]
-    features = whole.shape[0]
-    rows, chunk = blocks.shape[1:]
-    apart = whole.shape[1] - units
-    bring, fetch, places = [], [], []
+def rows_fetch(place, shifts, n, whole_hbm, whole, sems):
+    chunk = whole.shape[0] // len(shifts)
+    fetch = []
     for j, shift in enumerate(shifts):
-        at = lax.rem(place_ref[0] + shift + n, n)
-        places.append(at)
-        bring.append(pltpu.make_async_copy(sources[j], blocks.at[j], sems.at[n + j]))
+        at = lax.rem(place + shift + n, n)
         source = whole_hbm.at[pl.ds(pl.multiple_of(at * chunk, 16), chunk), :]
         fetch.append(pltpu.make_async_copy(source, whole.at[pl.ds(j * chunk, chunk), :], sems.at[j]))
-    for copy in bring + fetch:
+    return fetch
+
+
+def scaled_blocks(blocks, gains, scaled, squares):
+    chunk = blocks[0].shape[1]
+    for j, block in enumerate(blocks):
+        wide = block[...].astype(F32)
+        squares += jnp.sum(wide * wide, axis=-1, keepdims=True)
+        scaled[:, pl.ds(j * chunk, chunk)] = (wide * gains[j]).astype(BF16)
+    return squares
+
+
+def early_kernel(shifts, place_ref, *refs):
+    count = len(shifts)
+    blocks, gain_ref, whole_hbm, sums_ref, squares_ref, scaled, whole, sems = refs[:count], *refs[count:]
+    n = gain_ref.shape[0]
+    fetch = rows_fetch(place_ref[0], shifts, n, whole_hbm, whole, sems)
+    for copy in fetch:
         copy.start()
-    squares = jnp.zeros((rows, 1), F32)
-    for j in range(n):
-        bring[j].wait()
-        wide = blocks[j].astype(F32)
-        squares += jnp.sum(wide * wide, axis=-1, keepdims=True)
-    scale = lax.rsqrt(squares / features + EPSILON)
+    gains = [gain_ref[lax.rem(place_ref[0] + shift + n, n)] for shift in shifts]
+    zero = jnp.zeros((blocks[0].shape[0], 1), F32)
+    squares_ref[...] = scaled_blocks(blocks, gains, scaled, zero)
+    for copy in fetch:
+        copy.wait()
+    tile = 256
+    width = sums_ref.shape[1]
+
+    def step(start, size):
+        sums_ref[:, pl.ds(start, size)] = jnp.dot(
+            scaled[...], whole[:, pl.ds(start, size)], preferred_element_type=F32
+        )
+
+    @pl.loop(0, width // tile)
+    def _(j):
+        step(pl.multiple_of(j * tile, tile), tile)
+
+    if width % tile:
+        step(width // tile * tile, width % tile)
+
+
+def late_kernel(shifts, early, units, place_ref, *refs):
+    n = len(shifts)
+    blocks, gain_ref, whole_hbm, sums_ref, squares_ref, hidden_ref, own_ref = refs[:n], *refs[n : n + 6]
+    scaled, whole, sems = refs[n + 6 :]
+    fetch = rows_fetch(place_ref[0], shifts[early:], n, whole_hbm, whole, sems)
+    for copy in fetch:
+        copy.start()
+    places = [lax.rem(place_ref[0] + shift + n, n) for shift in shifts]
+    gains = [gain_ref[at] for at in places[early:]]
+    squares = scaled_blocks(blocks[early:], gains, scaled, squares_ref[...])
+    scale = lax.rsqrt(squares / whole_hbm.shape[0] + EPSILON)
     own = own_ref.shape[1]
     first = pl.multiple_of(place_ref[0] * own, own)
-    for j in range(n):
-        gain = gain_ref[places[j]]
-        normed[:, pl.ds(j * chunk, chunk)] = (blocks[j].astype(F32) * scale * gain).astype(BF16)
-        own_ref[places[j]] = blocks[j, pl.ds(first, own), :]
+    for at, block in zip(places, blocks):
+        own_ref[at] = block[pl.ds(first, own), :]
     for copy in fetch:
         copy.wait()
-
-    def step(start, width):
-        gate = jnp.dot(normed[...], whole[:, pl.ds(start, width)], preferred_element_type=F32)
-        upward = jnp.dot(normed[...], whole[:, pl.ds(apart + start, width)], preferred_element_type=F32)
+    apart, tile = whole.shape[1] - units, 256
+
+    def step(start, size):
+        gate, upward = (
+            scale
+            * (
+                sums_ref[:, pl.ds(at, size)]
+                + jnp.dot(scaled[...], whole[:, pl.ds(at, size)], preferred_element_type=F32)
+            )
+            for at in (start, apart + start)
+        )
         value = gate * (1.0 / (1.0 + jnp.exp(-gate))) * upward
-        hidden_ref[:, pl.ds(start, width)] = value.astype(BF16)
-
-    tile = 256
+        hidden_ref[:, pl.ds(start, size)] = value.astype(BF16)
 
     @pl.loop(0, units // tile)
     def _(j):
@@ -219,8 +259,7 @@
     step(units // tile * tile, units % tile)
 
 
-def down_kernel(hidden_ref, weight_hbm, out_hbm, weight, out, sems):
-    tile = 256
+def down_kernel(tile, hidden_ref, weight_hbm, out_hbm, weight, out, sems):
     tiles = weight.shape[0] // tile
 
     def here(j):
@@ -395,6 +434,8 @@
         row_of_slot[:, None],
         from_audio,
     )
+    down_turned, outgoing = lax.optimization_barrier((down_weight.T, outgoing))
+    down_whole = lax.all_gather(down_turned, "dp", axis=0, tiled=True)
     incoming = lax.all_to_all(
         outgoing.reshape(owner_count, capacity, width), "dp", split_axis=0, concat_axis=0, tiled=True
     ).reshape(slots, width)
@@ -413,38 +454,67 @@
         mib=16,
     )(target, incoming)
 
-    down_turned, sequence = lax.optimization_barrier((down_weight.T, sequence))
-    down_whole = lax.all_gather(down_turned, "dp", axis=0, tiled=True)
-
     features = n * width
     own_count = seq_count // n
-    got = ring_blocks(sequence, "tensor")
-    order = sorted(got)
+    shifts = [0]
+    for k in range(1, n // 2):
+        shifts += [-k, k]
+    shifts.append(-(n // 2))
+    early = 5
+    here = plane.reshape(1)
+    padded = 2 * units + gap
+    gains = llm_gain.reshape(n, 1, width)
+    blocks = [sequence]
+    a = b = sequence
+    for k in range(1, n // 2 + 1):
+        a = lax.ppermute(a, "tensor", shifted("tensor", 1))
+        if k < n // 2:
+            b = lax.ppermute(b, "tensor", shifted("tensor", -1))
+        if k == 3:
+            sums, squares = call(
+                functools.partial(early_kernel, shifts[:early]),
+                (
+                    jax.ShapeDtypeStruct((seq_count, padded), F32),
+                    jax.ShapeDtypeStruct((seq_count, 1), F32),
+                ),
+                [smem] + [vmem] * (early + 1) + [hbm],
+                4 * seq_count * early * width * units,
+                scratch=[
+                    pltpu.VMEM((seq_count, early * width), BF16),
+                    pltpu.VMEM((early * width, padded), BF16),
+                    pltpu.SemaphoreType.DMA((early,)),
+                ],
+                mib=48,
+            )(here, *blocks, gains, whole)
+            a, b, sums = lax.optimization_barrier((a, b, sums))
+        blocks.append(a)
+        if k < n // 2:
+            blocks.append(b)
     hidden, own_rows = call(
-        functools.partial(gate_kernel, n, tuple(order), units),
+        functools.partial(late_kernel, shifts, early, units),
         (
             jax.ShapeDtypeStruct((seq_count, units), BF16),
             jax.ShapeDtypeStruct((n, own_count, width), BF16),
         ),
-        [smem] + [hbm] * n + [vmem, hbm],
-        4 * seq_count * features * units,
+        [smem] + [vmem] * (n + 1) + [hbm] + [vmem] * 2,
+        4 * seq_count * (n - early) * width * units,
         scratch=[
-            pltpu.VMEM((n, seq_count, width), BF16),
-            pltpu.VMEM((features, 2 * units + gap), BF16),
-            pltpu.VMEM((seq_count, features), BF16),
-            pltpu.SemaphoreType.DMA((2 * n,)),
+            pltpu.VMEM((seq_count, (n - early) * width), BF16),
+            pltpu.VMEM(((n - early) * width, padded), BF16),
+            pltpu.SemaphoreType.DMA((n - early,)),
         ],
-        mib=62,
-    )(plane.reshape(1), *[got[k] for k in order], llm_gain.reshape(n, 1, width), whole)
+        mib=48,
+    )(here, *blocks, gains, whole, sums, squares)
+    down_tile = 512
     terms = call(
-        down_kernel,
+        functools.partial(down_kernel, down_tile),
         jax.ShapeDtypeStruct((seq_count, features), BF16),
         [vmem, hbm],
         2 * seq_count * features * units,
         scratch=[
             pltpu.VMEM((features, units), BF16),
             pltpu.VMEM((seq_count, features), BF16),
-            pltpu.SemaphoreType.DMA((2 * (features // 256),)),
+            pltpu.SemaphoreType.DMA((2 * (features // down_tile),)),
         ],
         mib=62,
         out_space=HBM,

time: 253 us -> 250 us (0.988)
  waiting for transfers between devices: 137 us -> 127 us
  Pallas kernels: 51.8 us -> 57.7 us
    ppermute x7, waiting for transfers between devices: 39.1 us -> 31.5 us  [the longest x4 31.5 us: body(): a = lax.ppermute(a, 'tensor', shifted('tensor', 1))]
    pallas_call x8 -> x9, Pallas kernels: 51.8 us -> 57.7 us  [run(): pl.pallas_call(kernel, out_shape=out_shape, in_specs=specs, out_specs=jax...]
  transfers between devices with their start and end apart: 22 -> 22, of which waited for: 10 -> 9; matrix products, arithmetic and copies ran while one was open for 3% -> 3% of each run, Pallas kernels for 16% -> 19%
where the time goes in v3:
time: 250 us; the launch traced here: 249 us
  waiting for transfers between devices  127 us (51%)
  Pallas kernels  57.7 us (23%)
  starting transfers between devices  35 us (14%)
  between operations  13.5 us (5%)
  local copies, waits for them, and re-layouts  12.4 us (5%)
    pallas_call x9, Pallas kernels, run(): pl.pallas_call(kernel, out_shape=out_shape, in_specs=specs, out_specs=jax...  57.7 us
    reduce_scatter x1, waiting for transfers between devices, body(): lax.psum_scatter(terms, 'tensor', scatter_dimension=0, tiled=True)  53.6 us
    ppermute x4, waiting for transfers between devices, body(): a = lax.ppermute(a, 'tensor', shifted('tensor', 1))  31.5 us
    ppermute x3, waiting for transfers between devices, body(): ups.append(lax.ppermute(ups[-1], 'tensor', shifted('tensor', 1)))  22.4 us
    all_to_all x1, waiting for transfers between devices, body(): lax.all_to_all(outgoing.reshape(owner_count, capacity, width), 'dp', spli...  19.4 us
    ppermute x3, starting transfers between devices, body(): downs.append(lax.ppermute(away, 'tensor', shifted('tensor', -1)))  8.04 us
    all_to_all x1, starting transfers between devices, body(): lax.all_to_all(outgoing.reshape(owner_count, capacity, width), 'dp', spli...  7.37 us
    ppermute x3, starting transfers between devices, body(): b = lax.ppermute(b, 'tensor', shifted('tensor', -1))  5.21 us
  transfers between devices with their start and end apart: 22, of which 9 were waited for; matrix products, arithmetic and copies ran while one was open for 3% of the time, Pallas kernels for 19%

profile of v3, /device:TPU:1, one launch (start us, length us, event | category | flops | bytes accessed | tf_op | source)
XLA Modules:
  0.0 249.1 jit_solution(8535413513077373847)
XLA Ops:
  6.6 2.0 concatenate.3
  8.8 2.5 %collective-permute-start = (bf16[80,1280]{1,0:T(8,128)(2,1)S(1)}, bf16[80,1280]{1,0:T(8,128)(2,1)S(1)}, u32[]{:S(2)}, u32[]{:S(2)}) collective-permute-start(bf16[80,1280]{1,0:T(8,128)(2,1)S(1)} %constant_dynamic-slice_fusion.1.refs_0_.refs_7_), channel_id=1, source_target_pairs={{0,1},{1,2},{2,3},{3,4},{4,5},{5,6},{6,7},{7,0},{8,9},{9,10},{10,1... | collective-permute-start | bytes 614408 | tf_op jit(solution)/shard_map/ppermute | solution.py:349
  11.3 4.0 %collective-permute-start.1 = (bf16[80,1280]{1,0:T(8,128)(2,1)S(1)}, bf16[80,1280]{1,0:T(8,128)(2,1)S(1)}, u32[]{:S(2)}, u32[]{:S(2)}) collective-permute-start(bf16[80,1280]{1,0:T(8,128)(2,1)S(1)} %constant_dynamic-slice_fusion.1.refs_0_.refs_7_), channel_id=1, source_target_pairs={{0,7},{1,0},{2,1},{3,2},{4,3},{5,4},{6,5},{7,6},{8,15},{9,8},{10,9... | collective-permute-start | bytes 614408 | tf_op jit(solution)/shard_map/ppermute | solution.py:350
  15.4 0.1 copy.23.column_ref
  15.6 1.3 copy-done.10
  16.8 2.9 %shard_map.136.context_ref = bf16[160,512]{1,0:T(8,128)(2,1)S(1)} custom-call(s32[1]{0:T(128)} %bitcast.3.core_ref, bf16[512,1280]{1,0:T(8,128)(2,1)S(1)} %copy-done.2, s32[512,1]{1,0:T(8,128)S(1)} %copy.23.column_ref, s32[1,512]{1,0:T(1,128)S(1)} %copy-done.14, f32[1,1280]{1,0:T(1,128)S(1)} %broadcast_in_dim.33.gain_ref, bf16[3,160,1280]{2,1,0:T(8,128)(2,1)S(1)} %bitcast.18), custom_call_target="tpu_custom_call" | custom-call | flops 796917760 | bytes 2548740 | tf_op jit(solution)/shard_map/pallas_call | solution.py:292
  19.8 0.3 collective-permute-done.above_ref.refs_1_.refs_8_
  20.3 2.7 %collective-permute-start.7 = (bf16[1440,128]{1,0:T(8,128)(2,1)S(1)}, bf16[1440,128]{1,0:T(8,128)(2,1)S(1)}, u32[]{:S(2)}, u32[]{:S(2)}) collective-permute-start(bf16[1440,128]{1,0:T(8,128)(2,1)S(1)} %get-tuple-element.17), channel_id=1, source_target_pairs={{0,7},{1,0},{2,1},{3,2},{4,3},{5,4},{6,5},{7,6},{8,15},{9,8},{10,9... | collective-permute-start | bytes 1105928 | tf_op jit(solution)/shard_map/ppermute | solution.py:358
  23.0 7.4 %collective-permute-done.2.refs_3_.refs_1_ = bf16[1440,128]{1,0:T(8,128)(2,1)S(1)} collective-permute-done((bf16[1440,128]{1,0:T(8,128)(2,1)S(1)}, bf16[1440,128]{1,0:T(8,128)(2,1)S(1)}, u32[]{:S(2)}, u32[]{:S(2)}) %collective-permute-start.2) | collective-permute-done | bytes 368672 | tf_op jit(solution)/shard_map/ppermute | solution.py:356
  30.4 2.7 %collective-permute-start.8 = (bf16[1440,128]{1,0:T(8,128)(2,1)S(1)}, bf16[1440,128]{1,0:T(8,128)(2,1)S(1)}, u32[]{:S(2)}, u32[]{:S(2)}) collective-permute-start(bf16[1440,128]{1,0:T(8,128)(2,1)S(1)} %collective-permute-done.7.refs_4_.refs_2_), channel_id=1, source_target_pairs={{0,7},{1,0},{2,1},{3,2},{4,3},{5,4},{6,5},{7,6},{8,15},{9,8},{10,9... | collective-permute-start | bytes 1105928 | tf_op jit(solution)/shard_map/ppermute | solution.py:358
  33.0 6.6 %collective-permute-done.3.refs_5_.refs_3_ = bf16[1440,128]{1,0:T(8,128)(2,1)S(1)} collective-permute-done((bf16[1440,128]{1,0:T(8,128)(2,1)S(1)}, bf16[1440,128]{1,0:T(8,128)(2,1)S(1)}, u32[]{:S(2)}, u32[]{:S(2)}) %collective-permute-start.3) | collective-permute-done | bytes 368672 | tf_op jit(solution)/shard_map/ppermute | solution.py:356
  39.6 1.4 shard_map.138
  41.0 3.0 %collective-permute-start.10 = (bf16[7,800,128]{2,1,0:T(8,128)(2,1)}, bf16[7,800,128]{2,1,0:T(8,128)(2,1)}, u32[]{:S(2)}, u32[]{:S(2)}) collective-permute-start(bf16[7,800,128]{2,1,0:T(8,128)(2,1)} %shard_map.138), channel_id=1, source_target_pairs={{0,8},{8,0},{16,24},{24,16},{32,40},{40,32},{48,56},{56,48},{64,72... | collective-permute-start | bytes 4300808 | tf_op jit(solution)/shard_map/ppermute | solution.py:376
  44.6 2.7 %collective-permute-start.9 = (bf16[640,128]{1,0:T(8,128)(2,1)S(1)}, bf16[640,128]{1,0:T(8,128)(2,1)S(1)}, u32[]{:S(2)}, u32[]{:S(2)}) collective-permute-start(bf16[640,128]{1,0:T(8,128)(2,1)S(1)} %slice.13), channel_id=1, source_target_pairs={{0,7},{1,0},{2,1},{3,2},{4,3},{5,4},{6,5},{7,6},{8,15},{9,8},{10,9... | collective-permute-start | bytes 491528 | tf_op jit(solution)/shard_map/ppermute | solution.py:358
  47.3 8.4 %collective-permute-done.4.refs_5_.refs_1_ = bf16[1440,128]{1,0:T(8,128)(2,1)S(1)} collective-permute-done((bf16[1440,128]{1,0:T(8,128)(2,1)S(1)}, bf16[1440,128]{1,0:T(8,128)(2,1)S(1)}, u32[]{:S(2)}, u32[]{:S(2)}) %collective-permute-start.4) | collective-permute-done | bytes 368672 | tf_op jit(solution)/shard_map/ppermute | solution.py:356
  55.8 1.1 collective-permute-start.6
  56.9 0.8 fusion.2
  57.7 1.3 select_n.51.refs_6_
  59.0 1.3 copy.26.refs_7_
  60.3 0.6 broadcast_in_dim.34.refs_4_
  60.9 0.7 copy-done.18
  61.6 7.2 %shard_map.139.refs_3_ = f32[512,1280]{1,0:T(8,128)} custom-call(bf16[1440,128]{1,0:T(8,128)(2,1)} %copy-done.13, bf16[1440,128]{1,0:T(8,128)(2,1)} %copy-done.7, bf16[1440,128]{1,0:T(8,128)(2,1)} %copy-done.8, bf16[1440,128]{1,0:T(8,128)(2,1)} %copy-done.9, bf16[1440,128]{1,0:T(8,128)(2,1)} %copy-done.3, bf16[1440,128]{1,0:T(8,128)(2,1)} %copy-done.15, ...), custom_call_target="tpu_custom_call" | custom-call | flops 1677721600 | bytes 5734400 | tf_op jit(solution)/shard_map/pallas_call | solution.py:292
  68.8 0.6 copy-done.17
  69.5 0.2 copy-done.16
  69.7 7.7 %shard_map.140 = bf16[1024,448]{1,0:T(8,128)(2,1)} custom-call(bf16[640,128]{1,0:T(8,128)(2,1)} %copy-done.17, bf16[1440,128]{1,0:T(8,128)(2,1)} %copy-done.15, bf16[1440,128]{1,0:T(8,128)(2,1)} %copy-done.16, f32[512,1280]{1,0:T(8,128)} %shard_map.139.refs_3_, f32[1,1280]{1,0:T(1,128)} %broadcast_in_dim.34.refs_4_, bf16[448,5120]{1,0:T(8,128)(2,1)} %bitcast.21, ...), custom_call_target="tpu_custom_call" | custom-call | flops 587202560 | bytes 9036800 | tf_op jit(solution)/shard_map/pallas_call | solution.py:292
  77.4 7.4 %all-to-all-start = ((bf16[32,32,448]{2,1,0:T(8,128)(2,1)}), bf16[32,32,448]{2,1,0:T(8,128)(2,1)S(1)}, u32[]{:S(2)}, u32[]{:S(2)}) async-start(bf16[32,32,448]{2,1,0:T(8,128)(2,1)} %bitcast.22), calls=%async_computation | async-start | bytes 2097152 | tf_op jit(solution)/shard_map/all_to_all | solution.py:439
  84.8 0.2 dynamic-slice_reduce_fusion
  85.0 0.7 fusion.7
  86.0 19.4 %all-to-all-done = bf16[32,32,448]{2,1,0:T(8,128)(2,1)S(1)} async-done(((bf16[32,32,448]{2,1,0:T(8,128)(2,1)}), bf16[32,32,448]{2,1,0:T(8,128)(2,1)S(1)}, u32[]{:S(2)}, u32[]{:S(2)}) %all-to-all-start) | async-done | bytes 917536 | tf_op jit(solution)/shard_map/all_to_all | solution.py:439
  105.4 0.7 shard_map.141.refs_0_
  106.1 2.0 collective-permute-start.11
  108.2 1.2 collective-permute-start.12
  109.3 10.6 %collective-permute-done.11.refs_1_ = bf16[512,448]{1,0:T(8,128)(2,1)S(1)} collective-permute-done((bf16[512,448]{1,0:T(8,128)(2,1)S(1)}, bf16[512,448]{1,0:T(8,128)(2,1)S(1)}, u32[]{:S(2)}, u32[]{:S(2)}) %collective-permute-start.11) | collective-permute-done | bytes 458784 | tf_op jit(solution)/shard_map/ppermute | solution.py:470
  120.0 0.9 collective-permute-start.13
  120.9 1.7 collective-permute-start.14
  122.7 9.7 %collective-permute-done.13.refs_3_ = bf16[512,448]{1,0:T(8,128)(2,1)S(1)} collective-permute-done((bf16[512,448]{1,0:T(8,128)(2,1)S(1)}, bf16[512,448]{1,0:T(8,128)(2,1)S(1)}, u32[]{:S(2)}, u32[]{:S(2)}) %collective-permute-start.13) | collective-permute-done | bytes 458784 | tf_op jit(solution)/shard_map/ppermute | solution.py:470
  132.4 0.4 collective-permute-start.15
  132.8 2.3 collective-permute-start.16
  135.1 15.3 %shard_map.142 = (f32[512,2464]{1,0:T(8,128)}, f32[512,1]{1,0:T(8,128)S(1)}) custom-call(s32[1]{0:T(128)} %bitcast.place_ref, bf16[512,448]{1,0:T(8,128)(2,1)S(1)} %shard_map.141.refs_0_, bf16[512,448]{1,0:T(8,128)(2,1)S(1)} %collective-permute-done.11.refs_1_, bf16[512,448]{1,0:T(8,128)(2,1)S(1)} %collective-permute-done.12.refs_2_, ...), custom_call_target="tpu_custom_call" | custom-call | flops 5431623680 | bytes 19970052 | tf_op jit(solution)/shard_map/pallas_call | solution.py:292
  150.6 11.1 %collective-permute-done.17.refs_7_ = bf16[512,448]{1,0:T(8,128)(2,1)S(1)} collective-permute-done((bf16[512,448]{1,0:T(8,128)(2,1)S(1)}, bf16[512,448]{1,0:T(8,128)(2,1)S(1)}, u32[]{:S(2)}, u32[]{:S(2)}) %collective-permute-start.17) | collective-permute-done | bytes 458784 | tf_op jit(solution)/shard_map/ppermute | solution.py:470
  161.7 12.7 %shard_map.143 = (bf16[512,1184]{1,0:T(8,128)(2,1)}, bf16[8,64,448]{2,1,0:T(8,128)(2,1)S(1)}) custom-call(s32[1]{0:T(128)} %bitcast.place_ref, bf16[512,448]{1,0:T(8,128)(2,1)S(1)} %shard_map.141.refs_0_, bf16[512,448]{1,0:T(8,128)(2,1)S(1)} %collective-permute-done.11.refs_1_, bf16[512,448]{1,0:T(8,128)(2,1)S(1)} %collective-permute-done.12.refs_2_, ...), custom_call_target="tpu_custom_call" | custom-call | flops 3258974208 | bytes 26394628 | tf_op jit(solution)/shard_map/pallas_call | solution.py:292
  174.4 0.8 copy-done.11
  175.1 9.7 %shard_map.144 = bf16[512,3584]{1,0:T(8,128)(2,1)} custom-call(bf16[512,1184]{1,0:T(8,128)(2,1)} %get-tuple-element.25.hidden_ref, bf16[3584,1184]{1,0:T(8,128)(2,1)} %all-gather.5.cloned.1.call-done.weight_hbm), custom_call_target="tpu_custom_call" | custom-call | flops 4345298944 | bytes 9699328 | tf_op jit(solution)/shard_map/pallas_call | solution.py:292
  184.9 1.0 copy-done.12
  186.0 0.6 copy.27
  186.7 0.4 reshape.165
  187.1 53.6 %reduce-scatter.2.cloned.1.call-done = bf16[64,3584]{1,0:T(8,128)(2,1)} async-done(((bf16[512,3584]{1,0:T(8,128)(2,1)}), bf16[64,3584]{1,0:T(8,128)(2,1)}) %reduce-scatter.2.cloned.1.call-update) | async-done | bytes 458768 | tf_op jit(solution)/shard_map/reduce_scatter | solution.py:522
  240.7 1.9 add_convert_fusion
  (86 shorter events, 1.7 us)
Async XLA Ops:
  6.5 2.2 copy-start
  6.5 8.8 %copy-start.14 = (s32[1,512]{1,0:T(1,128)S(1)}, s32[1,512]{1,0:T(1,128)}, u32[]{:S(2)}) copy-start(s32[1,512]{1,0:T(1,128)} %row_ref.1) | copy-start | bytes 6148
  6.5 9.0 %copy-start.21 = (f32[1280]{0:T(1024)S(1)}, f32[1280]{0:T(1024)}, u32[]{:S(2)}) copy-start(f32[1280]{0:T(1024)} %param.16) | copy-start | bytes 15364
  6.5 9.0 %copy-start.2 = (bf16[512,1280]{1,0:T(8,128)(2,1)S(1)}, bf16[512,1280]{1,0:T(8,128)(2,1)}, u32[]{:S(2)}) copy-start(bf16[512,1280]{1,0:T(8,128)(2,1)} %refs_11_.1) | copy-start | bytes 3932164
  6.5 128.6 %all-gather.3.cloned.1.call-start = ((), (), s32[]{:S(2)}) async-start(), calls=%async_computation.2 | async-start | bytes 18923520 | tf_op jit(solution)/shard_map/all_gather | solution.py:383
  8.7 166.5 %all-gather.5.cloned.1.call-start = ((), (), s32[]{:S(2)}) async-start(), calls=%async_computation.3 | async-start | bytes 9461760 | tf_op jit(solution)/shard_map/all_gather | solution.py:438
  8.8 30.8 %copy-start.4 = (bf16[80,1280]{1,0:T(8,128)(2,1)}, bf16[80,1280]{1,0:T(8,128)(2,1)S(1)}, u32[]{:S(2)}) copy-start(bf16[80,1280]{1,0:T(8,128)(2,1)S(1)} %constant_dynamic-slice_fusion.1.refs_0_.refs_7_) | copy-start | bytes 614404
  8.8 11.3 %collective-permute-start = (bf16[80,1280]{1,0:T(8,128)(2,1)S(1)}, bf16[80,1280]{1,0:T(8,128)(2,1)S(1)}, u32[]{:S(2)}, u32[]{:S(2)}) collective-permute-start(bf16[80,1280]{1,0:T(8,128)(2,1)S(1)} %constant_dynamic-slice_fusion.1.refs_0_.refs_7_), channel_id=1, source_target_pairs={{0,1},{1,2},{2,3},{3,4},{4,5},{5,6},{6,7},{7,0},{8,9},{9,10},{10,1... | collective-permute-start | bytes 614408 | tf_op jit(solution)/shard_map/ppermute | solution.py:349
  11.3 8.7 %collective-permute-start.1 = (bf16[80,1280]{1,0:T(8,128)(2,1)S(1)}, bf16[80,1280]{1,0:T(8,128)(2,1)S(1)}, u32[]{:S(2)}, u32[]{:S(2)}) collective-permute-start(bf16[80,1280]{1,0:T(8,128)(2,1)S(1)} %constant_dynamic-slice_fusion.1.refs_0_.refs_7_), channel_id=1, source_target_pairs={{0,7},{1,0},{2,1},{3,2},{4,3},{5,4},{6,5},{7,6},{8,15},{9,8},{10,9... | collective-permute-start | bytes 614408 | tf_op jit(solution)/shard_map/ppermute | solution.py:350
  15.5 1.3 copy-start.10
  20.1 20.9 %copy-start.5 = (bf16[80,1280]{1,0:T(8,128)(2,1)}, bf16[80,1280]{1,0:T(8,128)(2,1)S(1)}, u32[]{:S(2)}) copy-start(bf16[80,1280]{1,0:T(8,128)(2,1)S(1)} %collective-permute-done.above_ref.refs_1_.refs_8_) | copy-start | bytes 614404
  20.1 20.9 %copy-start.6 = (bf16[80,1280]{1,0:T(8,128)(2,1)}, bf16[80,1280]{1,0:T(8,128)(2,1)S(1)}, u32[]{:S(2)}) copy-start(bf16[80,1280]{1,0:T(8,128)(2,1)S(1)} %collective-permute-done.1.below_ref.refs_2_.refs_9_) | copy-start | bytes 614404
  20.2 2.8 %copy-start.13 = (bf16[1440,128]{1,0:T(8,128)(2,1)}, bf16[1440,128]{1,0:T(8,128)(2,1)S(1)}, u32[]{:S(2)}) copy-start(bf16[1440,128]{1,0:T(8,128)(2,1)S(1)} %get-tuple-element.16.refs_0_) | copy-start | bytes 1105924
  20.2 23.8 %copy-start.19 = (s32[32,32]{1,0:T(8,128)S(1)}, s32[32,32]{1,0:T(8,128)}, u32[]{:S(2)}) copy-start(s32[32,32]{1,0:T(8,128)} %param.22) | copy-start | bytes 12292
  20.2 10.1 %collective-permute-start.2 = (bf16[1440,128]{1,0:T(8,128)(2,1)S(1)}, bf16[1440,128]{1,0:T(8,128)(2,1)S(1)}, u32[]{:S(2)}, u32[]{:S(2)}) collective-permute-start(bf16[1440,128]{1,0:T(8,128)(2,1)S(1)} %get-tuple-element.16.refs_0_), channel_id=1, source_target_pairs={{0,1},{1,2},{2,3},{3,4},{4,5},{5,6},{6,7},{7,0},{8,9},{9,10},{10,1... | collective-permute-start | bytes 1105928 | tf_op jit(solution)/shard_map/ppermute | solution.py:356
  20.3 36.6 %copy-start.23 = (bf16[384,448]{0,1:T(8,128)(2,1)S(1)}, bf16[384,448]{0,1:T(8,128)(2,1)}, u32[]{:S(2)}) copy-start(bf16[384,448]{0,1:T(8,128)(2,1)} %param.21) | copy-start | bytes 1032196
  20.3 10.0 %collective-permute-start.7 = (bf16[1440,128]{1,0:T(8,128)(2,1)S(1)}, bf16[1440,128]{1,0:T(8,128)(2,1)S(1)}, u32[]{:S(2)}, u32[]{:S(2)}) collective-permute-start(bf16[1440,128]{1,0:T(8,128)(2,1)S(1)} %get-tuple-element.17), channel_id=1, source_target_pairs={{0,7},{1,0},{2,1},{3,2},{4,3},{5,4},{6,5},{7,6},{8,15},{9,8},{10,9... | collective-permute-start | bytes 1105928 | tf_op jit(solution)/shard_map/ppermute | solution.py:358
  30.4 14.2 %copy-start.7 = (bf16[1440,128]{1,0:T(8,128)(2,1)}, bf16[1440,128]{1,0:T(8,128)(2,1)S(1)}, u32[]{:S(2)}) copy-start(bf16[1440,128]{1,0:T(8,128)(2,1)S(1)} %collective-permute-done.2.refs_3_.refs_1_) | copy-start | bytes 1105924
  30.4 9.2 %collective-permute-start.3 = (bf16[1440,128]{1,0:T(8,128)(2,1)S(1)}, bf16[1440,128]{1,0:T(8,128)(2,1)S(1)}, u32[]{:S(2)}, u32[]{:S(2)}) collective-permute-start(bf16[1440,128]{1,0:T(8,128)(2,1)S(1)} %collective-permute-done.2.refs_3_.refs_1_), channel_id=1, source_target_pairs={{0,1},{1,2},{2,3},{3,4},{4,5},{5,6},{6,7},{7,0},{8,9},{9,10},{10,1... | collective-permute-start | bytes 1105928 | tf_op jit(solution)/shard_map/ppermute | solution.py:356
  30.4 14.2 %copy-start.8 = (bf16[1440,128]{1,0:T(8,128)(2,1)}, bf16[1440,128]{1,0:T(8,128)(2,1)S(1)}, u32[]{:S(2)}) copy-start(bf16[1440,128]{1,0:T(8,128)(2,1)S(1)} %collective-permute-done.7.refs_4_.refs_2_) | copy-start | bytes 1105924
  30.4 9.2 %collective-permute-start.8 = (bf16[1440,128]{1,0:T(8,128)(2,1)S(1)}, bf16[1440,128]{1,0:T(8,128)(2,1)S(1)}, u32[]{:S(2)}, u32[]{:S(2)}) collective-permute-start(bf16[1440,128]{1,0:T(8,128)(2,1)S(1)} %collective-permute-done.7.refs_4_.refs_2_), channel_id=1, source_target_pairs={{0,7},{1,0},{2,1},{3,2},{4,3},{5,4},{6,5},{7,6},{8,15},{9,8},{10,9... | collective-permute-start | bytes 1105928 | tf_op jit(solution)/shard_map/ppermute | solution.py:358
  39.6 4.9 %copy-start.9 = (bf16[1440,128]{1,0:T(8,128)(2,1)}, bf16[1440,128]{1,0:T(8,128)(2,1)S(1)}, u32[]{:S(2)}) copy-start(bf16[1440,128]{1,0:T(8,128)(2,1)S(1)} %collective-permute-done.3.refs_5_.refs_3_) | copy-start | bytes 1105924
  39.6 4.9 %copy-start.3 = (bf16[1440,128]{1,0:T(8,128)(2,1)}, bf16[1440,128]{1,0:T(8,128)(2,1)S(1)}, u32[]{:S(2)}) copy-start(bf16[1440,128]{1,0:T(8,128)(2,1)S(1)} %collective-permute-done.8.refs_6_.refs_4_) | copy-start | bytes 1105924
  41.0 19.9 %collective-permute-start.10 = (bf16[7,800,128]{2,1,0:T(8,128)(2,1)}, bf16[7,800,128]{2,1,0:T(8,128)(2,1)}, u32[]{:S(2)}, u32[]{:S(2)}) collective-permute-start(bf16[7,800,128]{2,1,0:T(8,128)(2,1)} %shard_map.138), channel_id=1, source_target_pairs={{0,8},{8,0},{16,24},{24,16},{32,40},{40,32},{48,56},{56,48},{64,72... | collective-permute-start | bytes 4300808 | tf_op jit(solution)/shard_map/ppermute | solution.py:376
  44.2 11.5 %collective-permute-start.4 = (bf16[1440,128]{1,0:T(8,128)(2,1)S(1)}, bf16[1440,128]{1,0:T(8,128)(2,1)S(1)}, u32[]{:S(2)}, u32[]{:S(2)}) collective-permute-start(bf16[1440,128]{1,0:T(8,128)(2,1)S(1)} %collective-permute-done.3.refs_5_.refs_3_), channel_id=1, source_target_pairs={{0,1},{1,2},{2,3},{3,4},{4,5},{5,6},{6,7},{7,0},{8,9},{9,10},{10,1... | collective-permute-start | bytes 1105928 | tf_op jit(solution)/shard_map/ppermute | solution.py:356
  44.6 16.4 %collective-permute-start.9 = (bf16[640,128]{1,0:T(8,128)(2,1)S(1)}, bf16[640,128]{1,0:T(8,128)(2,1)S(1)}, u32[]{:S(2)}, u32[]{:S(2)}) collective-permute-start(bf16[640,128]{1,0:T(8,128)(2,1)S(1)} %slice.13), channel_id=1, source_target_pairs={{0,7},{1,0},{2,1},{3,2},{4,3},{5,4},{6,5},{7,6},{8,15},{9,8},{10,9... | collective-permute-start | bytes 491528 | tf_op jit(solution)/shard_map/ppermute | solution.py:358
  55.7 4.6 %copy-start.15 = (bf16[1440,128]{1,0:T(8,128)(2,1)}, bf16[1440,128]{1,0:T(8,128)(2,1)S(1)}, u32[]{:S(2)}) copy-start(bf16[1440,128]{1,0:T(8,128)(2,1)S(1)} %collective-permute-done.4.refs_5_.refs_1_) | copy-start | bytes 1105924
  55.7 4.6 %copy-start.22 = (f32[1280]{0:T(1024)S(1)}, f32[1280]{0:T(1024)}, u32[]{:S(2)}) copy-start(f32[1280]{0:T(1024)} %param.19) | copy-start | bytes 15364
  55.7 13.1 %collective-permute-start.5 = (bf16[640,128]{1,0:T(8,128)(2,1)S(1)}, bf16[640,128]{1,0:T(8,128)(2,1)S(1)}, u32[]{:S(2)}, u32[]{:S(2)}) collective-permute-start(bf16[640,128]{1,0:T(8,128)(2,1)S(1)} %slice.12), channel_id=1, source_target_pairs={{0,1},{1,2},{2,3},{3,4},{4,5},{5,6},{6,7},{7,0},{8,9},{9,10},{10,1... | collective-permute-start | bytes 491528 | tf_op jit(solution)/shard_map/ppermute | solution.py:359
  55.8 13.0 %collective-permute-start.6 = (bf16[1440,128]{1,0:T(8,128)(2,1)S(1)}, bf16[1440,128]{1,0:T(8,128)(2,1)S(1)}, u32[]{:S(2)}, u32[]{:S(2)}) collective-permute-start(bf16[1440,128]{1,0:T(8,128)(2,1)S(1)} %collective-permute-done.4.refs_5_.refs_1_), channel_id=1, source_target_pairs={{0,8},{8,0},{16,24},{24,16},{32,40},{40,32},{48,56},{56,48},{64,72... | collective-permute-start | bytes 1105928 | tf_op jit(solution)/shard_map/ppermute | solution.py:377
  60.9 0.7 copy-start.18
  68.8 0.7 copy-start.17
  68.8 0.8 copy-start.16
  77.4 45.2 %copy-start.20 = (f32[3584]{0:T(1024)S(1)}, f32[3584]{0:T(1024)}, u32[]{:S(2)}) copy-start(f32[3584]{0:T(1024)} %param.24) | copy-start | bytes 43012
  77.4 28.0 %all-to-all-start = ((bf16[32,32,448]{2,1,0:T(8,128)(2,1)}), bf16[32,32,448]{2,1,0:T(8,128)(2,1)S(1)}, u32[]{:S(2)}, u32[]{:S(2)}) async-start(bf16[32,32,448]{2,1,0:T(8,128)(2,1)} %bitcast.22), calls=%async_computation | async-start | bytes 2097152 | tf_op jit(solution)/shard_map/all_to_all | solution.py:439
  84.8 155.9 %reduce-scatter.2.cloned.1.call-start = ((), (), s32[]{:S(2)}) async-start(), calls=%async_computation.4 | async-start | bytes 4128768 | tf_op jit(solution)/shard_map/reduce_scatter | solution.py:522
  106.1 13.8 %collective-permute-start.11 = (bf16[512,448]{1,0:T(8,128)(2,1)S(1)}, bf16[512,448]{1,0:T(8,128)(2,1)S(1)}, u32[]{:S(2)}, u32[]{:S(2)}) collective-permute-start(bf16[512,448]{1,0:T(8,128)(2,1)S(1)} %shard_map.141.refs_0_), channel_id=1, source_target_pairs={{0,1},{1,2},{2,3},{3,4},{4,5},{5,6},{6,7},{7,0},{8,9},{9,10},{10,1... | collective-permute-start | bytes 1376264 | tf_op jit(solution)/shard_map/ppermute | solution.py:470
  108.2 12.7 %collective-permute-start.12 = (bf16[512,448]{1,0:T(8,128)(2,1)S(1)}, bf16[512,448]{1,0:T(8,128)(2,1)S(1)}, u32[]{:S(2)}, u32[]{:S(2)}) collective-permute-start(bf16[512,448]{1,0:T(8,128)(2,1)S(1)} %shard_map.141.refs_0_), channel_id=1, source_target_pairs={{0,7},{1,0},{2,1},{3,2},{4,3},{5,4},{6,5},{7,6},{8,15},{9,8},{10,9... | collective-permute-start | bytes 1376264 | tf_op jit(solution)/shard_map/ppermute | solution.py:472
  120.0 12.5 %collective-permute-start.13 = (bf16[512,448]{1,0:T(8,128)(2,1)S(1)}, bf16[512,448]{1,0:T(8,128)(2,1)S(1)}, u32[]{:S(2)}, u32[]{:S(2)}) collective-permute-start(bf16[512,448]{1,0:T(8,128)(2,1)S(1)} %collective-permute-done.11.refs_1_), channel_id=1, source_target_pairs={{0,1},{1,2},{2,3},{3,4},{4,5},{5,6},{6,7},{7,0},{8,9},{9,10},{10,1... | collective-permute-start | bytes 1376264 | tf_op jit(solution)/shard_map/ppermute | solution.py:470
  120.9 11.9 %collective-permute-start.14 = (bf16[512,448]{1,0:T(8,128)(2,1)S(1)}, bf16[512,448]{1,0:T(8,128)(2,1)S(1)}, u32[]{:S(2)}, u32[]{:S(2)}) collective-permute-start(bf16[512,448]{1,0:T(8,128)(2,1)S(1)} %collective-permute-done.12.refs_2_), channel_id=1, source_target_pairs={{0,7},{1,0},{2,1},{3,2},{4,3},{5,4},{6,5},{7,6},{8,15},{9,8},{10,9... | collective-permute-start | bytes 1376264 | tf_op jit(solution)/shard_map/ppermute | solution.py:472
  132.4 18.0 %collective-permute-start.15 = (bf16[512,448]{1,0:T(8,128)(2,1)S(1)}, bf16[512,448]{1,0:T(8,128)(2,1)S(1)}, u32[]{:S(2)}, u32[]{:S(2)}) collective-permute-start(bf16[512,448]{1,0:T(8,128)(2,1)S(1)} %collective-permute-done.13.refs_3_), channel_id=1, source_target_pairs={{0,1},{1,2},{2,3},{3,4},{4,5},{5,6},{6,7},{7,0},{8,9},{9,10},{10,1... | collective-permute-start | bytes 1376264 | tf_op jit(solution)/shard_map/ppermute | solution.py:470
  132.8 17.7 %collective-permute-start.16 = (bf16[512,448]{1,0:T(8,128)(2,1)S(1)}, bf16[512,448]{1,0:T(8,128)(2,1)}, u32[]{:S(2)}, u32[]{:S(2)}) collective-permute-start(bf16[512,448]{1,0:T(8,128)(2,1)S(1)} %collective-permute-done.14.refs_4_), channel_id=1, source_target_pairs={{0,7},{1,0},{2,1},{3,2},{4,3},{5,4},{6,5},{7,6},{8,15},{9,8},{10,9... | collective-permute-start | bytes 1376264 | tf_op jit(solution)/shard_map/ppermute | solution.py:472
  150.5 11.2 %collective-permute-start.17 = (bf16[512,448]{1,0:T(8,128)(2,1)S(1)}, bf16[512,448]{1,0:T(8,128)(2,1)S(1)}, u32[]{:S(2)}, u32[]{:S(2)}) collective-permute-start(bf16[512,448]{1,0:T(8,128)(2,1)S(1)} %collective-permute-done.15.refs_5_), channel_id=1, source_target_pairs={{0,1},{1,2},{2,3},{3,4},{4,5},{5,6},{6,7},{7,0},{8,9},{9,10},{10,1... | collective-permute-start | bytes 1376264 | tf_op jit(solution)/shard_map/ppermute | solution.py:470
  174.3 0.8 copy-start.11
  184.9 1.0 copy-start.12
  186.0 56.5 %copy-start.1 = (bf16[160,1280]{1,0:T(8,128)(2,1)S(1)}, bf16[160,1280]{1,0:T(8,128)(2,1)}, u32[]{:S(2)}) copy-start(bf16[160,1280]{1,0:T(8,128)(2,1)} %param.18) | copy-start | bytes 1228804
Sparse Core Ops, SparseCore 0:
  9.9 94.1 all-gather.2
  106.7 61.7 all-gather.4
  185.0 55.6 reduce-scatter.1

commit v4 on v3

--- a/solution.py
+++ b/solution.py
@@ -195,7 +195,8 @@
 
 def early_kernel(shifts, place_ref, *refs):
     count = len(shifts)
-    blocks, gain_ref, whole_hbm, sums_ref, squares_ref, scaled, whole, sems = refs[:count], *refs[count:]
+    blocks, gain_ref, whole_hbm, sums_hbm, squares_ref = refs[:count], *refs[count : count + 4]
+    scaled, whole, sums, sems = refs[count + 4 :]
     n = gain_ref.shape[0]
     fetch = rows_fetch(place_ref[0], shifts, n, whole_hbm, whole, sems)
     for copy in fetch:
@@ -205,29 +206,43 @@
     squares_ref[...] = scaled_blocks(blocks, gains, scaled, zero)
     for copy in fetch:
         copy.wait()
+    width = sums.shape[1]
     tile = 256
-    width = sums_ref.shape[1]
-
-    def step(start, size):
-        sums_ref[:, pl.ds(start, size)] = jnp.dot(
-            scaled[...], whole[:, pl.ds(start, size)], preferred_element_type=F32
-        )
-
-    @pl.loop(0, width // tile)
+    full = width // tile
+
+    def result(columns, j):
+        return pltpu.make_async_copy(sums.at[:, columns], sums_hbm.at[:, columns], sems.at[count + j])
+
+    def step(start, size, j):
+        columns = pl.ds(start, size)
+        sums[:, columns] = jnp.dot(scaled[...], whole[:, columns], preferred_element_type=F32)
+
+    @pl.loop(0, full)
     def _(j):
-        step(pl.multiple_of(j * tile, tile), tile)
-
-    if width % tile:
-        step(width // tile * tile, width % tile)
+        start = pl.multiple_of(j * tile, tile)
+        step(start, tile, j)
+        result(pl.ds(start, tile), j).start()
+
+    rest = result(pl.ds(full * tile, width - full * tile), full)
+    step(full * tile, width - full * tile, full)
+    rest.start()
+
+    @pl.loop(0, full)
+    def _(j):
+        result(pl.ds(pl.multiple_of(j * tile, tile), tile), j).wait()
+
+    rest.wait()
 
 
 def late_kernel(shifts, early, units, place_ref, *refs):
     n = len(shifts)
-    blocks, gain_ref, whole_hbm, sums_ref, squares_ref, hidden_ref, own_ref = refs[:n], *refs[n : n + 6]
-    scaled, whole, sems = refs[n + 6 :]
+    blocks, gain_ref, whole_hbm, sums_hbm, squares_ref, hidden_ref, own_ref = refs[:n], *refs[n : n + 6]
+    scaled, whole, sums, sems = refs[n + 6 :]
     fetch = rows_fetch(place_ref[0], shifts[early:], n, whole_hbm, whole, sems)
     for copy in fetch:
         copy.start()
+    bring = pltpu.make_async_copy(sums_hbm, sums, sems.at[n - early])
+    bring.start()
     places = [lax.rem(place_ref[0] + shift + n, n) for shift in shifts]
     gains = [gain_ref[at] for at in places[early:]]
     squares = scaled_blocks(blocks[early:], gains, scaled, squares_ref[...])
@@ -240,27 +255,30 @@
         copy.wait()
     apart, tile = whole.shape[1] - units, 256
 
-    def step(start, size):
-        gate, upward = (
-            scale
-            * (
-                sums_ref[:, pl.ds(at, size)]
-                + jnp.dot(scaled[...], whole[:, pl.ds(at, size)], preferred_element_type=F32)
-            )
-            for at in (start, apart + start)
-        )
+    def product(at, size):
+        return jnp.dot(scaled[...], whole[:, pl.ds(at, size)], preferred_element_type=F32)
+
+    def finish(start, size, gate, upward):
+        gate = scale * (sums[:, pl.ds(start, size)] + gate)
+        upward = scale * (sums[:, pl.ds(apart + start, size)] + upward)
         value = gate * (1.0 / (1.0 + jnp.exp(-gate))) * upward
         hidden_ref[:, pl.ds(start, size)] = value.astype(BF16)
 
+    bring.wait()
+
     @pl.loop(0, units // tile)
     def _(j):
-        step(pl.multiple_of(j * tile, tile), tile)
-
-    step(units // tile * tile, units % tile)
-
-
-def down_kernel(tile, hidden_ref, weight_hbm, out_hbm, weight, out, sems):
+        start = pl.multiple_of(j * tile, tile)
+        finish(start, tile, product(start, tile), product(apart + start, tile))
+
+    start, size = units // tile * tile, units % tile
+    finish(start, size, product(start, size), product(apart + start, size))
+
+
+def down_kernel(tile, n, hidden_ref, weight_hbm, *refs):
+    outs_hbm, weight, outs, sems = refs[:2], refs[2], refs[3:5], refs[5]
     tiles = weight.shape[0] // tile
+    run = hidden_ref.shape[0] // n
 
     def here(j):
         return pl.ds(pl.multiple_of(j * tile, tile), tile)
@@ -268,8 +286,9 @@
     def part(j):
         return pltpu.make_async_copy(weight_hbm.at[here(j), :], weight.at[here(j), :], sems.at[j])
 
-    def result(j):
-        return pltpu.make_async_copy(out.at[:, here(j)], out_hbm.at[:, here(j)], sems.at[tiles + j])
+    def result(j, k):
+        place = sems.at[(k + 1) * tiles + j]
+        return pltpu.make_async_copy(outs[k].at[:, here(j)], outs_hbm[k].at[:, here(j)], place)
 
     @pl.loop(0, tiles)
     def _(j):
@@ -278,22 +297,31 @@
     @pl.loop(0, tiles)
     def _(j):
         part(j).wait()
-        out[:, here(j)] = turned_dot(hidden_ref[...], weight[here(j), :]).astype(BF16)
-        result(j).start()
+        value = turned_dot(hidden_ref[...], weight[here(j), :]).astype(BF16).reshape(n, run, tile)
+        for k in range(2):
+            half = value[:, k * run // 2 : (k + 1) * run // 2]
+            outs[k][:, here(j)] = half.reshape(n * run // 2, tile)
+            result(j, k).start()
 
     @pl.loop(0, tiles)
     def _(j):
-        result(j).wait()
+        for k in range(2):
+            result(j, k).wait()
 
 
 def call(kernel, out_shape, specs, flops, scratch=(), mib=16, out_space=VMEM):
     def run(*args):
         moved = sum(a.size * a.dtype.itemsize for a in args)
+        if isinstance(out_shape, tuple):
+            spaces = out_space if isinstance(out_space, tuple) else (out_space,) * len(out_shape)
+            outs = tuple(pl.BlockSpec(memory_space=space) for space in spaces)
+        else:
+            outs = pl.BlockSpec(memory_space=out_space)
         return pl.pallas_call(
             kernel,
             out_shape=out_shape,
             in_specs=specs,
-            out_specs=jax.tree.map(lambda _: pl.BlockSpec(memory_space=out_space), out_shape),
+            out_specs=outs,
             scratch_shapes=scratch,
             compiler_params=pltpu.CompilerParams(vmem_limit_bytes=mib << 20),
             cost_estimate=pl.CostEstimate(flops=flops, bytes_accessed=moved, transcendentals=0),
@@ -344,6 +372,18 @@
         jnp.swapaxes(qkv_weight, 1, 2),
     )
 
+    video_rows = patch_count // 4
+    seq_count = video_rows + audio.shape[0]
+    capacity = 2 * seq_count // owner_count
+    sent_lengths = span_lengths[owner]
+    starts = jnp.cumsum(sent_lengths) - sent_lengths
+    slot_index = jnp.arange(capacity, dtype=jnp.int32)
+    row_of_slot = jnp.where(
+        slot_index[None, :] < sent_lengths[:, None], starts[:, None] + slot_index[None, :], -1
+    ).reshape(-1)
+    row = jnp.arange(seq_count, dtype=jnp.int32)
+    select = (row_of_slot[:, None] == row[None, video_rows:]).astype(BF16)
+    from_audio = jnp.dot(select, audio, preferred_element_type=F32).astype(BF16)
     group = 2 * HEAD_VIT
     own_head = lax.dynamic_slice_in_dim(out_weight, core * HEAD_VIT, HEAD_VIT, 0)
     above = lax.ppermute(own_head, "tensor", shifted("tensor", 1))
@@ -353,11 +393,16 @@
     up, down = call(pack_kernel, (payload, payload), [vmem] * 3, 0)(context, above, below)
     ups, downs = [up], [down]
     for k in range(1, n // 2):
+        if k == n // 2 - 1:
+            up, from_audio, slot_column = lax.optimization_barrier(
+                (ups[-1], from_audio, row_of_slot[:, None])
+            )
+            ups[-1] = up
         ups.append(lax.ppermute(ups[-1], "tensor", shifted("tensor", 1)))
         away = downs[-1] if k < n // 2 - 1 else downs[-1][:split]
         downs.append(lax.ppermute(away, "tensor", shifted("tensor", -1)))
     ups.append(lax.ppermute(ups[-1][:split], "tensor", shifted("tensor", 1)))
-    contexts = [up]
+    contexts = [ups[0]]
     tall = []
     for k in range(1, n // 2 + 1):
         contexts.append(ups[k])
@@ -382,18 +427,6 @@
     )
     whole = lax.all_gather(stacked, "dp", axis=0, tiled=True)
 
-    video_rows = patch_count // 4
-    seq_count = video_rows + audio.shape[0]
-    capacity = 2 * seq_count // owner_count
-    sent_lengths = span_lengths[owner]
-    starts = jnp.cumsum(sent_lengths) - sent_lengths
-    slot_index = jnp.arange(capacity, dtype=jnp.int32)
-    row_of_slot = jnp.where(
-        slot_index[None, :] < sent_lengths[:, None], starts[:, None] + slot_index[None, :], -1
-    ).reshape(-1)
-    row = jnp.arange(seq_count, dtype=jnp.int32)
-    select = (row_of_slot[:, None] == row[None, video_rows:]).astype(BF16)
-    from_audio = jnp.dot(select, audio, preferred_element_type=F32).astype(BF16)
     slots = owner_count * capacity
     width = audio.shape[1]
     operands = [*contexts[: n - 1], own_head, above, below, other, patches]
@@ -431,7 +464,7 @@
         sofar,
         merge_gain[None, :],
         merger_weight.T,
-        row_of_slot[:, None],
+        slot_column,
         from_audio,
     )
     down_turned, outgoing = lax.optimization_barrier((down_weight.T, outgoing))
@@ -464,13 +497,22 @@
     here = plane.reshape(1)
     padded = 2 * units + gap
     gains = llm_gain.reshape(n, 1, width)
+
+    def scratch(count, sems):
+        return [
+            pltpu.VMEM((seq_count, count * width), BF16),
+            pltpu.VMEM((count * width, padded), BF16),
+            pltpu.VMEM((seq_count, padded), F32),
+            pltpu.SemaphoreType.DMA((count + sems,)),
+        ]
+
     blocks = [sequence]
     a = b = sequence
     for k in range(1, n // 2 + 1):
         a = lax.ppermute(a, "tensor", shifted("tensor", 1))
         if k < n // 2:
             b = lax.ppermute(b, "tensor", shifted("tensor", -1))
-        if k == 3:
+        if k == n // 2 - 1:
             sums, squares = call(
                 functools.partial(early_kernel, shifts[:early]),
                 (
@@ -479,12 +521,9 @@
                 ),
                 [smem] + [vmem] * (early + 1) + [hbm],
                 4 * seq_count * early * width * units,
-                scratch=[
-                    pltpu.VMEM((seq_count, early * width), BF16),
-                    pltpu.VMEM((early * width, padded), BF16),
-                    pltpu.SemaphoreType.DMA((early,)),
-                ],
-                mib=48,
+                scratch=scratch(early, padded // 256 + 1),
+                mib=57,
+                out_space=(HBM, VMEM),
             )(here, *blocks, gains, whole)
             a, b, sums = lax.optimization_barrier((a, b, sums))
         blocks.append(a)
@@ -496,32 +535,45 @@
             jax.ShapeDtypeStruct((seq_count, units), BF16),
             jax.ShapeDtypeStruct((n, own_count, width), BF16),
         ),
-        [smem] + [vmem] * (n + 1) + [hbm] + [vmem] * 2,
+        [smem] + [vmem] * (n + 1) + [hbm] * 2 + [vmem],
         4 * seq_count * (n - early) * width * units,
-        scratch=[
-            pltpu.VMEM((seq_count, (n - early) * width), BF16),
-            pltpu.VMEM(((n - early) * width, padded), BF16),
-            pltpu.SemaphoreType.DMA((n - early,)),
-        ],
-        mib=48,
+        scratch=scratch(n - early, 1),
+        mib=57,
     )(here, *blocks, gains, whole, sums, squares)
-    down_tile = 512
-    terms = call(
-        functools.partial(down_kernel, down_tile),
-        jax.ShapeDtypeStruct((seq_count, features), BF16),
+    tile = 512
+    half = jax.ShapeDtypeStruct((seq_count // 2, features), BF16)
+    scattered, ringed = call(
+        functools.partial(down_kernel, tile, n),
+        (half, half),
         [vmem, hbm],
         2 * seq_count * features * units,
         scratch=[
             pltpu.VMEM((features, units), BF16),
-            pltpu.VMEM((seq_count, features), BF16),
-            pltpu.SemaphoreType.DMA((2 * (features // down_tile),)),
+            pltpu.VMEM(half.shape, BF16),
+            pltpu.VMEM(half.shape, BF16),
+            pltpu.SemaphoreType.DMA((3 * (features // tile),)),
         ],
-        mib=62,
+        mib=57,
         out_space=HBM,
     )(hidden, down_whole)
-    summed = lax.psum_scatter(terms, "tensor", scatter_dimension=0, tiled=True).astype(F32)
-    own_rows = jnp.moveaxis(own_rows, 0, 1).reshape(own_count, features)
-    return (own_rows.astype(F32) + summed).astype(BF16)
+    by_scatter = lax.psum_scatter(scattered, "tensor", scatter_dimension=0, tiled=True).astype(F32)
+
+    ringed = ringed.reshape(n, own_count // 2, features)
+
+    def term(shift):
+        return lax.dynamic_index_in_dim(ringed, lax.rem(plane + shift + n, n), 0, keepdims=False)
+
+    def running(step, count):
+        total = term(step * count)
+        for k in range(count - 1, -1, -1):
+            total = lax.ppermute(total, "tensor", shifted("tensor", step))
+            if k > 0:
+                total = (total.astype(F32) + term(step * k).astype(F32)).astype(BF16)
+        return total.astype(F32)
+
+    by_ring = term(0).astype(F32) + running(1, n // 2) + running(-1, n - n // 2 - 1)
+    own_rows = jnp.moveaxis(own_rows, 0, 1).reshape(own_count, features).astype(F32)
+    return (own_rows + jnp.concatenate([by_scatter, by_ring], axis=0)).astype(BF16)
 
 
 def solution(mesh):

time: 250 us -> 250 us (level)
  waiting for transfers between devices: 127 us -> 114 us
  starting transfers between devices: 35 us -> 42.8 us
    reduce_scatter x1, waiting for transfers between devices: 53.6 us -> 14.1 us  [body(): lax.psum_scatter(scattered, 'tensor', scatter_dimension=0, tiled=True)]
    ppermute x0 -> x7, waiting for transfers between devices: none -> 25.6 us  [running(): total = lax.ppermute(total, 'tensor', shifted('tensor', step))]
    ppermute x0 -> x7, starting transfers between devices: none -> 8.25 us  [running(): total = lax.ppermute(total, 'tensor', shifted('tensor', step))]
    ppermute x3, waiting for transfers between devices: 0.01 us -> 2.56 us  [body(): downs.append(lax.ppermute(away, 'tensor', shifted('tensor', -1)))]
  transfers between devices with their start and end apart: 22 -> 29, of which waited for: 9 -> 14; matrix products, arithmetic and copies ran while one was open for 3% -> 4% of each run, Pallas kernels for 19% -> 20%
where the time goes in v4:
time: 250 us; the launch traced here: 248 us
  waiting for transfers between devices  114 us (46%)
  Pallas kernels  59.6 us (24%)
  starting transfers between devices  42.8 us (17%)
  between operations  13.7 us (5%)
  local copies, waits for them, and re-layouts  11.7 us (5%)
  other arithmetic  4.38 us (2%)
    pallas_call x9, Pallas kernels, run(): pl.pallas_call(kernel, out_shape=out_shape, in_specs=specs, out_specs=out...  59.6 us
    ppermute x4, waiting for transfers between devices, body(): a = lax.ppermute(a, 'tensor', shifted('tensor', 1))  30.6 us
    ppermute x7, waiting for transfers between devices, running(): total = lax.ppermute(total, 'tensor', shifted('tensor', step))  25.6 us
    ppermute x3, waiting for transfers between devices, body(): ups.append(lax.ppermute(ups[-1], 'tensor', shifted('tensor', 1)))  23 us
    all_to_all x1, waiting for transfers between devices, body(): lax.all_to_all(outgoing.reshape(owner_count, capacity, width), 'dp', spli...  17.6 us
    reduce_scatter x1, waiting for transfers between devices, body(): lax.psum_scatter(scattered, 'tensor', scatter_dimension=0, tiled=True)  14.1 us
    ppermute x7, starting transfers between devices, running(): total = lax.ppermute(total, 'tensor', shifted('tensor', step))  8.25 us
    all_to_all x1, starting transfers between devices, body(): lax.all_to_all(outgoing.reshape(owner_count, capacity, width), 'dp', spli...  7.88 us
  transfers between devices with their start and end apart: 29, of which 14 were waited for; matrix products, arithmetic and copies ran while one was open for 4% of the time, Pallas kernels for 20%

profile of v4, /device:TPU:1, one launch (start us, length us, event | category | flops | bytes accessed | tf_op | source)
XLA Modules:
  0.0 247.6 jit_solution(4155089842284066527)
XLA Ops:
  6.6 2.1 concatenate.6
  8.8 2.5 %collective-permute-start = (bf16[80,1280]{1,0:T(8,128)(2,1)S(1)}, bf16[80,1280]{1,0:T(8,128)(2,1)S(1)}, u32[]{:S(2)}, u32[]{:S(2)}) collective-permute-start(bf16[80,1280]{1,0:T(8,128)(2,1)S(1)} %constant_dynamic-slice_fusion.1.refs_0_.refs_7_), channel_id=1, source_target_pairs={{0,1},{1,2},{2,3},{3,4},{4,5},{5,6},{6,7},{7,0},{8,9},{9,10},{10,1... | collective-permute-start | bytes 614408 | tf_op jit(solution)/shard_map/ppermute | solution.py:389
  11.3 4.0 %collective-permute-start.1 = (bf16[80,1280]{1,0:T(8,128)(2,1)S(1)}, bf16[80,1280]{1,0:T(8,128)(2,1)S(1)}, u32[]{:S(2)}, u32[]{:S(2)}) collective-permute-start(bf16[80,1280]{1,0:T(8,128)(2,1)S(1)} %constant_dynamic-slice_fusion.1.refs_0_.refs_7_), channel_id=1, source_target_pairs={{0,7},{1,0},{2,1},{3,2},{4,3},{5,4},{6,5},{7,6},{8,15},{9,8},{10,9... | collective-permute-start | bytes 614408 | tf_op jit(solution)/shard_map/ppermute | solution.py:390
  15.6 1.3 copy-done.11
  16.9 2.9 %shard_map.136.context_ref = bf16[160,512]{1,0:T(8,128)(2,1)S(1)} custom-call(s32[1]{0:T(128)} %bitcast.3.core_ref, bf16[512,1280]{1,0:T(8,128)(2,1)S(1)} %copy-done.2, s32[512,1]{1,0:T(8,128)S(1)} %copy.18.column_ref, s32[1,512]{1,0:T(1,128)S(1)} %copy-done.13, f32[1,1280]{1,0:T(1,128)S(1)} %broadcast_in_dim.33.gain_ref, bf16[3,160,1280]{2,1,0:T(8,128)(2,1)S(1)} %bitcast.41), custom_call_target="tpu_custom_call" | custom-call | flops 796917760 | bytes 2548740 | tf_op jit(solution)/shard_map/pallas_call | solution.py:320
  20.3 2.7 %collective-permute-start.7 = (bf16[1440,128]{1,0:T(8,128)(2,1)S(1)}, bf16[1440,128]{1,0:T(8,128)(2,1)S(1)}, u32[]{:S(2)}, u32[]{:S(2)}) collective-permute-start(bf16[1440,128]{1,0:T(8,128)(2,1)S(1)} %get-tuple-element.23), channel_id=1, source_target_pairs={{0,7},{1,0},{2,1},{3,2},{4,3},{5,4},{6,5},{7,6},{8,15},{9,8},{10,9... | collective-permute-start | bytes 1105928 | tf_op jit(solution)/shard_map/ppermute | solution.py:403
  23.3 7.1 %collective-permute-done.2.refs_3_.refs_1_ = bf16[1440,128]{1,0:T(8,128)(2,1)S(1)} collective-permute-done((bf16[1440,128]{1,0:T(8,128)(2,1)S(1)}, bf16[1440,128]{1,0:T(8,128)(2,1)S(1)}, u32[]{:S(2)}, u32[]{:S(2)}) %collective-permute-start.2) | collective-permute-done | bytes 368672 | tf_op jit(solution)/shard_map/ppermute | solution.py:401
  30.4 2.7 %collective-permute-start.8 = (bf16[1440,128]{1,0:T(8,128)(2,1)S(1)}, bf16[1440,128]{1,0:T(8,128)(2,1)S(1)}, u32[]{:S(2)}, u32[]{:S(2)}) collective-permute-start(bf16[1440,128]{1,0:T(8,128)(2,1)S(1)} %collective-permute-done.7.refs_4_.refs_2_), channel_id=1, source_target_pairs={{0,7},{1,0},{2,1},{3,2},{4,3},{5,4},{6,5},{7,6},{8,15},{9,8},{10,9... | collective-permute-start | bytes 1105928 | tf_op jit(solution)/shard_map/ppermute | solution.py:403
  33.3 1.7 fusion.2.refs_7_
  35.0 4.6 %collective-permute-done.3.refs_5_.refs_3_ = bf16[1440,128]{1,0:T(8,128)(2,1)S(1)} collective-permute-done((bf16[1440,128]{1,0:T(8,128)(2,1)S(1)}, bf16[1440,128]{1,0:T(8,128)(2,1)S(1)}, u32[]{:S(2)}, u32[]{:S(2)}) %collective-permute-start.3) | collective-permute-done | bytes 368672 | tf_op jit(solution)/shard_map/ppermute | solution.py:401
  39.6 1.3 shard_map.138
  41.0 3.1 %collective-permute-start.10 = (bf16[7,800,128]{2,1,0:T(8,128)(2,1)}, bf16[7,800,128]{2,1,0:T(8,128)(2,1)}, u32[]{:S(2)}, u32[]{:S(2)}) collective-permute-start(bf16[7,800,128]{2,1,0:T(8,128)(2,1)} %shard_map.138), channel_id=1, source_target_pairs={{0,8},{8,0},{16,24},{24,16},{32,40},{40,32},{48,56},{56,48},{64,72... | collective-permute-start | bytes 4300808 | tf_op jit(solution)/shard_map/ppermute | solution.py:421
  44.0 11.4 %collective-permute-done.4.refs_5_.refs_1_ = bf16[1440,128]{1,0:T(8,128)(2,1)S(1)} collective-permute-done((bf16[1440,128]{1,0:T(8,128)(2,1)S(1)}, bf16[1440,128]{1,0:T(8,128)(2,1)S(1)}, u32[]{:S(2)}, u32[]{:S(2)}) %collective-permute-start.4) | collective-permute-done | bytes 368672 | tf_op jit(solution)/shard_map/ppermute | solution.py:401
  55.4 0.9 collective-permute-start.6
  56.3 1.5 collective-permute-start.9
  58.7 1.0 copy.21.refs_6_
  59.8 2.6 %collective-permute-done.9.refs_6_ = bf16[640,128]{1,0:T(8,128)(2,1)S(1)} collective-permute-done((bf16[640,128]{1,0:T(8,128)(2,1)S(1)}, bf16[640,128]{1,0:T(8,128)(2,1)S(1)}, u32[]{:S(2)}, u32[]{:S(2)}) %collective-permute-start.9) | collective-permute-done | bytes 163872 | tf_op jit(solution)/shard_map/ppermute | solution.py:403
  63.0 7.0 %shard_map.139.refs_3_ = f32[512,1280]{1,0:T(8,128)} custom-call(bf16[1440,128]{1,0:T(8,128)(2,1)} %copy-done.12, bf16[1440,128]{1,0:T(8,128)(2,1)} %copy-done.8, bf16[1440,128]{1,0:T(8,128)(2,1)} %copy-done.9, bf16[1440,128]{1,0:T(8,128)(2,1)} %copy-done.10, bf16[1440,128]{1,0:T(8,128)(2,1)} %copy-done.3, bf16[1440,128]{1,0:T(8,128)(2,1)} %copy-done.14, ...), custom_call_target="tpu_custom_call" | custom-call | flops 1677721600 | bytes 5734400 | tf_op jit(solution)/shard_map/pallas_call | solution.py:320
  70.8 7.9 %shard_map.140 = bf16[1024,448]{1,0:T(8,128)(2,1)} custom-call(bf16[640,128]{1,0:T(8,128)(2,1)} %copy-done.24, bf16[1440,128]{1,0:T(8,128)(2,1)} %copy-done.14, bf16[1440,128]{1,0:T(8,128)(2,1)} %copy-done.23, f32[512,1280]{1,0:T(8,128)} %shard_map.139.refs_3_, f32[1,1280]{1,0:T(1,128)} %broadcast_in_dim.34.refs_4_, bf16[448,5120]{1,0:T(8,128)(2,1)} %bitcast.44, ...), custom_call_target="tpu_custom_call" | custom-call | flops 587202560 | bytes 9036800 | tf_op jit(solution)/shard_map/pallas_call | solution.py:320
  78.7 7.9 %all-to-all-start = ((bf16[32,32,448]{2,1,0:T(8,128)(2,1)}), bf16[32,32,448]{2,1,0:T(8,128)(2,1)S(1)}, u32[]{:S(2)}, u32[]{:S(2)}) async-start(bf16[32,32,448]{2,1,0:T(8,128)(2,1)} %bitcast.45), calls=%async_computation | async-start | bytes 2097152 | tf_op jit(solution)/shard_map/all_to_all | solution.py:472
  86.8 0.7 fusion.14
  87.8 17.6 %all-to-all-done = bf16[32,32,448]{2,1,0:T(8,128)(2,1)S(1)} async-done(((bf16[32,32,448]{2,1,0:T(8,128)(2,1)}), bf16[32,32,448]{2,1,0:T(8,128)(2,1)S(1)}, u32[]{:S(2)}, u32[]{:S(2)}) %all-to-all-start) | async-done | bytes 917536 | tf_op jit(solution)/shard_map/all_to_all | solution.py:472
  105.4 0.7 shard_map.141.refs_0_
  106.1 1.4 collective-permute-start.11
  107.5 1.8 collective-permute-start.12
  109.3 10.6 %collective-permute-done.11.refs_1_ = bf16[512,448]{1,0:T(8,128)(2,1)S(1)} collective-permute-done((bf16[512,448]{1,0:T(8,128)(2,1)S(1)}, bf16[512,448]{1,0:T(8,128)(2,1)S(1)}, u32[]{:S(2)}, u32[]{:S(2)}) %collective-permute-start.11) | collective-permute-done | bytes 458784 | tf_op jit(solution)/shard_map/ppermute | solution.py:512
  120.0 2.7 %collective-permute-start.14 = (bf16[512,448]{1,0:T(8,128)(2,1)S(1)}, bf16[512,448]{1,0:T(8,128)(2,1)S(1)}, u32[]{:S(2)}, u32[]{:S(2)}) collective-permute-start(bf16[512,448]{1,0:T(8,128)(2,1)S(1)} %collective-permute-done.12.refs_2_), channel_id=1, source_target_pairs={{0,7},{1,0},{2,1},{3,2},{4,3},{5,4},{6,5},{7,6},{8,15},{9,8},{10,9... | collective-permute-start | bytes 1376264 | tf_op jit(solution)/shard_map/ppermute | solution.py:514
  122.6 0.7 reshape.179.refs_5_.refs_8_
  123.3 9.1 %collective-permute-done.13.refs_3_ = bf16[512,448]{1,0:T(8,128)(2,1)S(1)} collective-permute-done((bf16[512,448]{1,0:T(8,128)(2,1)S(1)}, bf16[512,448]{1,0:T(8,128)(2,1)S(1)}, u32[]{:S(2)}, u32[]{:S(2)}) %collective-permute-start.13) | collective-permute-done | bytes 458784 | tf_op jit(solution)/shard_map/ppermute | solution.py:512
  132.5 2.7 %collective-permute-start.16 = (bf16[512,448]{1,0:T(8,128)(2,1)S(1)}, bf16[512,448]{1,0:T(8,128)(2,1)}, u32[]{:S(2)}, u32[]{:S(2)}) collective-permute-start(bf16[512,448]{1,0:T(8,128)(2,1)S(1)} %collective-permute-done.14.refs_4_), channel_id=1, source_target_pairs={{0,7},{1,0},{2,1},{3,2},{4,3},{5,4},{6,5},{7,6},{8,15},{9,8},{10,9... | collective-permute-start | bytes 1376264 | tf_op jit(solution)/shard_map/ppermute | solution.py:514
  135.2 16.3 %shard_map.142 = (f32[512,2464]{1,0:T(8,128)}, f32[512,1]{1,0:T(8,128)}) custom-call(s32[1]{0:T(128)} %bitcast.place_ref, bf16[512,448]{1,0:T(8,128)(2,1)} %copy-done.4, bf16[512,448]{1,0:T(8,128)(2,1)} %copy-done.15, bf16[512,448]{1,0:T(8,128)(2,1)} %copy-done.16, bf16[512,448]{1,0:T(8,128)(2,1)} %copy-done.17, bf16[512,448]{1,0:T(8,128)(2,1)} %copy-done.18, ...), custom_call_target="tpu_custom_call" | custom-call | flops 5431623680 | bytes 19970052 | tf_op jit(solution)/shard_map/pallas_call | solution.py:320
  151.9 10.9 %collective-permute-done.17.refs_7_ = bf16[512,448]{1,0:T(8,128)(2,1)S(1)} collective-permute-done((bf16[512,448]{1,0:T(8,128)(2,1)S(1)}, bf16[512,448]{1,0:T(8,128)(2,1)S(1)}, u32[]{:S(2)}, u32[]{:S(2)}) %collective-permute-start.17) | collective-permute-done | bytes 458784 | tf_op jit(solution)/shard_map/ppermute | solution.py:512
  162.8 0.8 copy-done.22
  163.5 13.5 %shard_map.143 = (bf16[512,1184]{1,0:T(8,128)(2,1)}, bf16[8,64,448]{2,1,0:T(8,128)(2,1)}) custom-call(s32[1]{0:T(128)} %bitcast.place_ref, bf16[512,448]{1,0:T(8,128)(2,1)} %copy-done.4, bf16[512,448]{1,0:T(8,128)(2,1)} %copy-done.15, bf16[512,448]{1,0:T(8,128)(2,1)} %copy-done.16, bf16[512,448]{1,0:T(8,128)(2,1)} %copy-done.17, ...), custom_call_target="tpu_custom_call" | custom-call | flops 3258974208 | bytes 26394628 | tf_op jit(solution)/shard_map/pallas_call | solution.py:320
  177.1 9.8 %shard_map.144 = (bf16[256,3584]{1,0:T(8,128)(2,1)}, bf16[256,3584]{1,0:T(8,128)(2,1)}) custom-call(bf16[512,1184]{1,0:T(8,128)(2,1)} %get-tuple-element.33.hidden_ref, bf16[3584,1184]{1,0:T(8,128)(2,1)} %all-gather.5.cloned.1.call-done.weight_hbm), custom_call_target="tpu_custom_call" | custom-call | flops 4345298944 | bytes 9699328 | tf_op jit(solution)/shard_map/pallas_call | solution.py:320
  186.9 1.2 dynamic-slice_bitcast_fusion.1
  188.2 2.7 %collective-permute-start.22 = (bf16[32,3584]{1,0:T(8,128)(2,1)S(1)}, bf16[32,3584]{1,0:T(8,128)(2,1)S(1)}, u32[]{:S(2)}, u32[]{:S(2)}) collective-permute-start(bf16[32,3584]{1,0:T(8,128)(2,1)S(1)} %get-tuple-element.44), channel_id=1, source_target_pairs={{0,7},{1,0},{2,1},{3,2},{4,3},{5,4},{6,5},{7,6},{8,15},{9,8},{10,9... | collective-permute-start | bytes 688136 | tf_op jit(solution)/shard_map/ppermute | solution.py:569
  190.9 3.4 %collective-permute-done.18 = bf16[32,3584]{1,0:T(8,128)(2,1)S(1)} collective-permute-done((bf16[32,3584]{1,0:T(8,128)(2,1)S(1)}, bf16[32,3584]{1,0:T(8,128)(2,1)S(1)}, u32[]{:S(2)}, u32[]{:S(2)}) %collective-permute-start.18) | collective-permute-done | bytes 229408 | tf_op jit(solution)/shard_map/ppermute | solution.py:569
  194.4 7.2 %collective-permute-done.19 = bf16[32,3584]{1,0:T(8,128)(2,1)S(1)} collective-permute-done((bf16[32,3584]{1,0:T(8,128)(2,1)S(1)}, bf16[32,3584]{1,0:T(8,128)(2,1)S(1)}, u32[]{:S(2)}, u32[]{:S(2)}) %collective-permute-start.19) | collective-permute-done | bytes 229408 | tf_op jit(solution)/shard_map/ppermute | solution.py:569
  201.8 2.7 %collective-permute-start.23 = (bf16[32,3584]{1,0:T(8,128)(2,1)S(1)}, bf16[32,3584]{1,0:T(8,128)(2,1)S(1)}, u32[]{:S(2)}, u32[]{:S(2)}) collective-permute-start(bf16[32,3584]{1,0:T(8,128)(2,1)S(1)} %get-tuple-element.42), channel_id=1, source_target_pairs={{0,7},{1,0},{2,1},{3,2},{4,3},{5,4},{6,5},{7,6},{8,15},{9,8},{10,9... | collective-permute-start | bytes 688136 | tf_op jit(solution)/shard_map/ppermute | solution.py:569
  204.5 5.7 %collective-permute-done.20 = bf16[32,3584]{1,0:T(8,128)(2,1)S(1)} collective-permute-done((bf16[32,3584]{1,0:T(8,128)(2,1)S(1)}, bf16[32,3584]{1,0:T(8,128)(2,1)S(1)}, u32[]{:S(2)}, u32[]{:S(2)}) %collective-permute-start.20) | collective-permute-done | bytes 229408 | tf_op jit(solution)/shard_map/ppermute | solution.py:569
  210.2 0.8 fusion.10
  211.0 2.7 %collective-permute-start.24 = (bf16[32,3584]{1,0:T(8,128)(2,1)S(1)}, bf16[32,3584]{1,0:T(8,128)(2,1)S(1)}, u32[]{:S(2)}, u32[]{:S(2)}) collective-permute-start(bf16[32,3584]{1,0:T(8,128)(2,1)S(1)} %get-tuple-element.40), channel_id=1, source_target_pairs={{0,7},{1,0},{2,1},{3,2},{4,3},{5,4},{6,5},{7,6},{8,15},{9,8},{10,9... | collective-permute-start | bytes 688136 | tf_op jit(solution)/shard_map/ppermute | solution.py:569
  214.8 9.3 %collective-permute-done.21 = bf16[32,3584]{1,0:T(8,128)(2,1)S(1)} collective-permute-done((bf16[32,3584]{1,0:T(8,128)(2,1)}, bf16[32,3584]{1,0:T(8,128)(2,1)S(1)}, u32[]{:S(2)}, u32[]{:S(2)}) %collective-permute-start.21) | collective-permute-done | bytes 229408 | tf_op jit(solution)/shard_map/ppermute | solution.py:569
  224.1 1.0 fusion.13
  225.2 14.1 %reduce-scatter.2.cloned.1.call-done = bf16[32,3584]{1,0:T(8,128)(2,1)} async-done(((bf16[256,3584]{1,0:T(8,128)(2,1)}), bf16[32,3584]{1,0:T(8,128)(2,1)}) %reduce-scatter.2.cloned.1.call-update) | async-done | bytes 229392 | tf_op jit(solution)/shard_map/reduce_scatter | solution.py:559
  239.2 1.0 convert_element_type.95
  240.2 0.9 fusion.5
  (120 shorter events, 6.2 us)
Async XLA Ops:
  6.5 8.8 %copy-start.13 = (s32[1,512]{1,0:T(1,128)S(1)}, s32[1,512]{1,0:T(1,128)}, u32[]{:S(2)}) copy-start(s32[1,512]{1,0:T(1,128)} %row_ref.1) | copy-start | bytes 6148
  6.5 9.0 %copy-start.28 = (f32[1280]{0:T(1024)S(1)}, f32[1280]{0:T(1024)}, u32[]{:S(2)}) copy-start(f32[1280]{0:T(1024)} %param.16) | copy-start | bytes 15364
  6.5 9.0 %copy-start.2 = (bf16[512,1280]{1,0:T(8,128)(2,1)S(1)}, bf16[512,1280]{1,0:T(8,128)(2,1)}, u32[]{:S(2)}) copy-start(bf16[512,1280]{1,0:T(8,128)(2,1)} %refs_11_.1) | copy-start | bytes 3932164
  6.5 128.6 %all-gather.3.cloned.1.call-start = ((), (), s32[]{:S(2)}) async-start(), calls=%async_computation.2 | async-start | bytes 18923520 | tf_op jit(solution)/shard_map/all_gather | solution.py:428
  8.7 168.4 %all-gather.5.cloned.1.call-start = ((), (), s32[]{:S(2)}) async-start(), calls=%async_computation.3 | async-start | bytes 9461760 | tf_op jit(solution)/shard_map/all_gather | solution.py:471
  8.8 30.8 %copy-start.5 = (bf16[80,1280]{1,0:T(8,128)(2,1)}, bf16[80,1280]{1,0:T(8,128)(2,1)S(1)}, u32[]{:S(2)}) copy-start(bf16[80,1280]{1,0:T(8,128)(2,1)S(1)} %constant_dynamic-slice_fusion.1.refs_0_.refs_7_) | copy-start | bytes 614404
  8.8 11.3 %collective-permute-start = (bf16[80,1280]{1,0:T(8,128)(2,1)S(1)}, bf16[80,1280]{1,0:T(8,128)(2,1)S(1)}, u32[]{:S(2)}, u32[]{:S(2)}) collective-permute-start(bf16[80,1280]{1,0:T(8,128)(2,1)S(1)} %constant_dynamic-slice_fusion.1.refs_0_.refs_7_), channel_id=1, source_target_pairs={{0,1},{1,2},{2,3},{3,4},{4,5},{5,6},{6,7},{7,0},{8,9},{9,10},{10,1... | collective-permute-start | bytes 614408 | tf_op jit(solution)/shard_map/ppermute | solution.py:389
  11.3 8.7 %collective-permute-start.1 = (bf16[80,1280]{1,0:T(8,128)(2,1)S(1)}, bf16[80,1280]{1,0:T(8,128)(2,1)S(1)}, u32[]{:S(2)}, u32[]{:S(2)}) collective-permute-start(bf16[80,1280]{1,0:T(8,128)(2,1)S(1)} %constant_dynamic-slice_fusion.1.refs_0_.refs_7_), channel_id=1, source_target_pairs={{0,7},{1,0},{2,1},{3,2},{4,3},{5,4},{6,5},{7,6},{8,15},{9,8},{10,9... | collective-permute-start | bytes 614408 | tf_op jit(solution)/shard_map/ppermute | solution.py:390
  16.9 16.4 %copy-start.30 = (bf16[384,448]{0,1:T(8,128)(2,1)S(1)}, bf16[384,448]{0,1:T(8,128)(2,1)}, u32[]{:S(2)}) copy-start(bf16[384,448]{0,1:T(8,128)(2,1)} %param.21) | copy-start | bytes 1032196
  20.1 20.9 %copy-start.6 = (bf16[80,1280]{1,0:T(8,128)(2,1)}, bf16[80,1280]{1,0:T(8,128)(2,1)S(1)}, u32[]{:S(2)}) copy-start(bf16[80,1280]{1,0:T(8,128)(2,1)S(1)} %collective-permute-done.above_ref.refs_1_.refs_8_) | copy-start | bytes 614404
  20.1 20.9 %copy-start.7 = (bf16[80,1280]{1,0:T(8,128)(2,1)}, bf16[80,1280]{1,0:T(8,128)(2,1)S(1)}, u32[]{:S(2)}) copy-start(bf16[80,1280]{1,0:T(8,128)(2,1)S(1)} %collective-permute-done.1.below_ref.refs_2_.refs_9_) | copy-start | bytes 614404
  20.2 10.1 %collective-permute-start.2 = (bf16[1440,128]{1,0:T(8,128)(2,1)S(1)}, bf16[1440,128]{1,0:T(8,128)(2,1)S(1)}, u32[]{:S(2)}, u32[]{:S(2)}) collective-permute-start(bf16[1440,128]{1,0:T(8,128)(2,1)S(1)} %get-tuple-element.21.refs_0_), channel_id=1, source_target_pairs={{0,1},{1,2},{2,3},{3,4},{4,5},{5,6},{6,7},{7,0},{8,9},{9,10},{10,1... | collective-permute-start | bytes 1105928 | tf_op jit(solution)/shard_map/ppermute | solution.py:401
  20.3 10.1 %collective-permute-start.7 = (bf16[1440,128]{1,0:T(8,128)(2,1)S(1)}, bf16[1440,128]{1,0:T(8,128)(2,1)S(1)}, u32[]{:S(2)}, u32[]{:S(2)}) collective-permute-start(bf16[1440,128]{1,0:T(8,128)(2,1)S(1)} %get-tuple-element.23), channel_id=1, source_target_pairs={{0,7},{1,0},{2,1},{3,2},{4,3},{5,4},{6,5},{7,6},{8,15},{9,8},{10,9... | collective-permute-start | bytes 1105928 | tf_op jit(solution)/shard_map/ppermute | solution.py:403
  30.4 10.6 %copy-start.8 = (bf16[1440,128]{1,0:T(8,128)(2,1)}, bf16[1440,128]{1,0:T(8,128)(2,1)S(1)}, u32[]{:S(2)}) copy-start(bf16[1440,128]{1,0:T(8,128)(2,1)S(1)} %collective-permute-done.2.refs_3_.refs_1_) | copy-start | bytes 1105924
  30.4 9.2 %collective-permute-start.3 = (bf16[1440,128]{1,0:T(8,128)(2,1)S(1)}, bf16[1440,128]{1,0:T(8,128)(2,1)S(1)}, u32[]{:S(2)}, u32[]{:S(2)}) collective-permute-start(bf16[1440,128]{1,0:T(8,128)(2,1)S(1)} %collective-permute-done.2.refs_3_.refs_1_), channel_id=1, source_target_pairs={{0,1},{1,2},{2,3},{3,4},{4,5},{5,6},{6,7},{7,0},{8,9},{9,10},{10,1... | collective-permute-start | bytes 1105928 | tf_op jit(solution)/shard_map/ppermute | solution.py:401
  30.4 10.6 %copy-start.9 = (bf16[1440,128]{1,0:T(8,128)(2,1)}, bf16[1440,128]{1,0:T(8,128)(2,1)S(1)}, u32[]{:S(2)}) copy-start(bf16[1440,128]{1,0:T(8,128)(2,1)S(1)} %collective-permute-done.7.refs_4_.refs_2_) | copy-start | bytes 1105924
  30.4 9.2 %collective-permute-start.8 = (bf16[1440,128]{1,0:T(8,128)(2,1)S(1)}, bf16[1440,128]{1,0:T(8,128)(2,1)S(1)}, u32[]{:S(2)}, u32[]{:S(2)}) collective-permute-start(bf16[1440,128]{1,0:T(8,128)(2,1)S(1)} %collective-permute-done.7.refs_4_.refs_2_), channel_id=1, source_target_pairs={{0,7},{1,0},{2,1},{3,2},{4,3},{5,4},{6,5},{7,6},{8,15},{9,8},{10,9... | collective-permute-start | bytes 1105928 | tf_op jit(solution)/shard_map/ppermute | solution.py:403
  35.0 23.1 %copy-start.29 = (f32[1280]{0:T(1024)S(1)}, f32[1280]{0:T(1024)}, u32[]{:S(2)}) copy-start(f32[1280]{0:T(1024)} %param.19) | copy-start | bytes 15364
  39.6 16.7 %copy-start.10 = (bf16[1440,128]{1,0:T(8,128)(2,1)}, bf16[1440,128]{1,0:T(8,128)(2,1)S(1)}, u32[]{:S(2)}) copy-start(bf16[1440,128]{1,0:T(8,128)(2,1)S(1)} %collective-permute-done.3.refs_5_.refs_3_) | copy-start | bytes 1105924
  39.6 16.7 %copy-start.3 = (bf16[1440,128]{1,0:T(8,128)(2,1)}, bf16[1440,128]{1,0:T(8,128)(2,1)S(1)}, u32[]{:S(2)}) copy-start(bf16[1440,128]{1,0:T(8,128)(2,1)S(1)} %collective-permute-done.8.refs_6_.refs_4_) | copy-start | bytes 1105924
  41.0 21.3 %collective-permute-start.10 = (bf16[7,800,128]{2,1,0:T(8,128)(2,1)}, bf16[7,800,128]{2,1,0:T(8,128)(2,1)}, u32[]{:S(2)}, u32[]{:S(2)}) collective-permute-start(bf16[7,800,128]{2,1,0:T(8,128)(2,1)} %shard_map.138), channel_id=1, source_target_pairs={{0,8},{8,0},{16,24},{24,16},{32,40},{40,32},{48,56},{56,48},{64,72... | collective-permute-start | bytes 4300808 | tf_op jit(solution)/shard_map/ppermute | solution.py:421
  44.0 11.4 %collective-permute-start.4 = (bf16[1440,128]{1,0:T(8,128)(2,1)S(1)}, bf16[1440,128]{1,0:T(8,128)(2,1)S(1)}, u32[]{:S(2)}, u32[]{:S(2)}) collective-permute-start(bf16[1440,128]{1,0:T(8,128)(2,1)S(1)} %collective-permute-done.3.refs_5_.refs_3_), channel_id=1, source_target_pairs={{0,1},{1,2},{2,3},{3,4},{4,5},{5,6},{6,7},{7,0},{8,9},{9,10},{10,1... | collective-permute-start | bytes 1105928 | tf_op jit(solution)/shard_map/ppermute | solution.py:401
  55.4 14.6 %collective-permute-start.6 = (bf16[1440,128]{1,0:T(8,128)(2,1)S(1)}, bf16[1440,128]{1,0:T(8,128)(2,1)S(1)}, u32[]{:S(2)}, u32[]{:S(2)}) collective-permute-start(bf16[1440,128]{1,0:T(8,128)(2,1)S(1)} %collective-permute-done.4.refs_5_.refs_1_), channel_id=1, source_target_pairs={{0,8},{8,0},{16,24},{24,16},{32,40},{40,32},{48,56},{56,48},{64,72... | collective-permute-start | bytes 1105928 | tf_op jit(solution)/shard_map/ppermute | solution.py:422
  56.3 6.0 %collective-permute-start.9 = (bf16[640,128]{1,0:T(8,128)(2,1)S(1)}, bf16[640,128]{1,0:T(8,128)(2,1)S(1)}, u32[]{:S(2)}, u32[]{:S(2)}) collective-permute-start(bf16[640,128]{1,0:T(8,128)(2,1)S(1)} %slice.13), channel_id=1, source_target_pairs={{0,7},{1,0},{2,1},{3,2},{4,3},{5,4},{6,5},{7,6},{8,15},{9,8},{10,9... | collective-permute-start | bytes 491528 | tf_op jit(solution)/shard_map/ppermute | solution.py:403
  57.8 12.2 %collective-permute-start.5 = (bf16[640,128]{1,0:T(8,128)(2,1)S(1)}, bf16[640,128]{1,0:T(8,128)(2,1)S(1)}, u32[]{:S(2)}, u32[]{:S(2)}) collective-permute-start(bf16[640,128]{1,0:T(8,128)(2,1)S(1)} %slice.12), channel_id=1, source_target_pairs={{0,1},{1,2},{2,3},{3,4},{4,5},{5,6},{6,7},{7,0},{8,9},{9,10},{10,1... | collective-permute-start | bytes 491528 | tf_op jit(solution)/shard_map/ppermute | solution.py:404
  78.7 43.9 %copy-start.27 = (f32[3584]{0:T(1024)S(1)}, f32[3584]{0:T(1024)}, u32[]{:S(2)}) copy-start(f32[3584]{0:T(1024)} %param.24) | copy-start | bytes 43012
  78.7 26.7 %all-to-all-start = ((bf16[32,32,448]{2,1,0:T(8,128)(2,1)}), bf16[32,32,448]{2,1,0:T(8,128)(2,1)S(1)}, u32[]{:S(2)}, u32[]{:S(2)}) async-start(bf16[32,32,448]{2,1,0:T(8,128)(2,1)} %bitcast.45), calls=%async_computation | async-start | bytes 2097152 | tf_op jit(solution)/shard_map/all_to_all | solution.py:472
  86.6 152.6 %reduce-scatter.2.cloned.1.call-start = ((), (), s32[]{:S(2)}) async-start(), calls=%async_computation.4 | async-start | bytes 2064384 | tf_op jit(solution)/shard_map/reduce_scatter | solution.py:559
  106.1 29.0 %copy-start.4 = (bf16[512,448]{1,0:T(8,128)(2,1)}, bf16[512,448]{1,0:T(8,128)(2,1)S(1)}, u32[]{:S(2)}) copy-start(bf16[512,448]{1,0:T(8,128)(2,1)S(1)} %shard_map.141.refs_0_) | copy-start | bytes 1376260
  106.1 13.8 %collective-permute-start.11 = (bf16[512,448]{1,0:T(8,128)(2,1)S(1)}, bf16[512,448]{1,0:T(8,128)(2,1)S(1)}, u32[]{:S(2)}, u32[]{:S(2)}) collective-permute-start(bf16[512,448]{1,0:T(8,128)(2,1)S(1)} %shard_map.141.refs_0_), channel_id=1, source_target_pairs={{0,1},{1,2},{2,3},{3,4},{4,5},{5,6},{6,7},{7,0},{8,9},{9,10},{10,1... | collective-permute-start | bytes 1376264 | tf_op jit(solution)/shard_map/ppermute | solution.py:512
  107.5 12.5 %collective-permute-start.12 = (bf16[512,448]{1,0:T(8,128)(2,1)S(1)}, bf16[512,448]{1,0:T(8,128)(2,1)S(1)}, u32[]{:S(2)}, u32[]{:S(2)}) collective-permute-start(bf16[512,448]{1,0:T(8,128)(2,1)S(1)} %shard_map.141.refs_0_), channel_id=1, source_target_pairs={{0,7},{1,0},{2,1},{3,2},{4,3},{5,4},{6,5},{7,6},{8,15},{9,8},{10,9... | collective-permute-start | bytes 1376264 | tf_op jit(solution)/shard_map/ppermute | solution.py:514
  120.0 15.2 %copy-start.15 = (bf16[512,448]{1,0:T(8,128)(2,1)}, bf16[512,448]{1,0:T(8,128)(2,1)S(1)}, u32[]{:S(2)}) copy-start(bf16[512,448]{1,0:T(8,128)(2,1)S(1)} %collective-permute-done.11.refs_1_) | copy-start | bytes 1376260
  120.0 12.5 %collective-permute-start.13 = (bf16[512,448]{1,0:T(8,128)(2,1)S(1)}, bf16[512,448]{1,0:T(8,128)(2,1)S(1)}, u32[]{:S(2)}, u32[]{:S(2)}) collective-permute-start(bf16[512,448]{1,0:T(8,128)(2,1)S(1)} %collective-permute-done.11.refs_1_), channel_id=1, source_target_pairs={{0,1},{1,2},{2,3},{3,4},{4,5},{5,6},{6,7},{7,0},{8,9},{9,10},{10,1... | collective-permute-start | bytes 1376264 | tf_op jit(solution)/shard_map/ppermute | solution.py:512
  120.0 15.2 %copy-start.16 = (bf16[512,448]{1,0:T(8,128)(2,1)}, bf16[512,448]{1,0:T(8,128)(2,1)S(1)}, u32[]{:S(2)}) copy-start(bf16[512,448]{1,0:T(8,128)(2,1)S(1)} %collective-permute-done.12.refs_2_) | copy-start | bytes 1376260
  120.0 12.5 %collective-permute-start.14 = (bf16[512,448]{1,0:T(8,128)(2,1)S(1)}, bf16[512,448]{1,0:T(8,128)(2,1)S(1)}, u32[]{:S(2)}, u32[]{:S(2)}) collective-permute-start(bf16[512,448]{1,0:T(8,128)(2,1)S(1)} %collective-permute-done.12.refs_2_), channel_id=1, source_target_pairs={{0,7},{1,0},{2,1},{3,2},{4,3},{5,4},{6,5},{7,6},{8,15},{9,8},{10,9... | collective-permute-start | bytes 1376264 | tf_op jit(solution)/shard_map/ppermute | solution.py:514
  132.4 19.1 %collective-permute-start.15 = (bf16[512,448]{1,0:T(8,128)(2,1)S(1)}, bf16[512,448]{1,0:T(8,128)(2,1)S(1)}, u32[]{:S(2)}, u32[]{:S(2)}) collective-permute-start(bf16[512,448]{1,0:T(8,128)(2,1)S(1)} %collective-permute-done.13.refs_3_), channel_id=1, source_target_pairs={{0,1},{1,2},{2,3},{3,4},{4,5},{5,6},{6,7},{7,0},{8,9},{9,10},{10,1... | collective-permute-start | bytes 1376264 | tf_op jit(solution)/shard_map/ppermute | solution.py:512
  132.5 19.1 %collective-permute-start.16 = (bf16[512,448]{1,0:T(8,128)(2,1)S(1)}, bf16[512,448]{1,0:T(8,128)(2,1)}, u32[]{:S(2)}, u32[]{:S(2)}) collective-permute-start(bf16[512,448]{1,0:T(8,128)(2,1)S(1)} %collective-permute-done.14.refs_4_), channel_id=1, source_target_pairs={{0,7},{1,0},{2,1},{3,2},{4,3},{5,4},{6,5},{7,6},{8,15},{9,8},{10,9... | collective-permute-start | bytes 1376264 | tf_op jit(solution)/shard_map/ppermute | solution.py:514
  151.5 11.2 %copy-start.21 = (bf16[512,448]{1,0:T(8,128)(2,1)}, bf16[512,448]{1,0:T(8,128)(2,1)S(1)}, u32[]{:S(2)}) copy-start(bf16[512,448]{1,0:T(8,128)(2,1)S(1)} %collective-permute-done.15.refs_5_) | copy-start | bytes 1376260
  151.5 11.2 %collective-permute-start.17 = (bf16[512,448]{1,0:T(8,128)(2,1)S(1)}, bf16[512,448]{1,0:T(8,128)(2,1)S(1)}, u32[]{:S(2)}, u32[]{:S(2)}) collective-permute-start(bf16[512,448]{1,0:T(8,128)(2,1)S(1)} %collective-permute-done.15.refs_5_), channel_id=1, source_target_pairs={{0,1},{1,2},{2,3},{3,4},{4,5},{5,6},{6,7},{7,0},{8,9},{9,10},{10,1... | collective-permute-start | bytes 1376264 | tf_op jit(solution)/shard_map/ppermute | solution.py:512
  188.1 6.2 %collective-permute-start.18 = (bf16[32,3584]{1,0:T(8,128)(2,1)S(1)}, bf16[32,3584]{1,0:T(8,128)(2,1)S(1)}, u32[]{:S(2)}, u32[]{:S(2)}) collective-permute-start(bf16[32,3584]{1,0:T(8,128)(2,1)S(1)} %get-tuple-element.43), channel_id=1, source_target_pairs={{0,1},{1,2},{2,3},{3,4},{4,5},{5,6},{6,7},{7,0},{8,9},{9,10},{10,1... | collective-permute-start | bytes 688136 | tf_op jit(solution)/shard_map/ppermute | solution.py:569
  188.2 6.2 %collective-permute-start.22 = (bf16[32,3584]{1,0:T(8,128)(2,1)S(1)}, bf16[32,3584]{1,0:T(8,128)(2,1)S(1)}, u32[]{:S(2)}, u32[]{:S(2)}) collective-permute-start(bf16[32,3584]{1,0:T(8,128)(2,1)S(1)} %get-tuple-element.44), channel_id=1, source_target_pairs={{0,7},{1,0},{2,1},{3,2},{4,3},{5,4},{6,5},{7,6},{8,15},{9,8},{10,9... | collective-permute-start | bytes 688136 | tf_op jit(solution)/shard_map/ppermute | solution.py:569
  190.9 22.8 %copy-start.20 = (bf16[8,64,448]{2,1,0:T(8,128)(2,1)S(1)}, bf16[8,64,448]{2,1,0:T(8,128)(2,1)}, u32[]{:S(2)}) copy-start(bf16[8,64,448]{2,1,0:T(8,128)(2,1)} %get-tuple-element.32) | copy-start | bytes 1376260
  194.3 7.3 %collective-permute-start.19 = (bf16[32,3584]{1,0:T(8,128)(2,1)S(1)}, bf16[32,3584]{1,0:T(8,128)(2,1)S(1)}, u32[]{:S(2)}, u32[]{:S(2)}) collective-permute-start(bf16[32,3584]{1,0:T(8,128)(2,1)S(1)} %fusion.12), channel_id=1, source_target_pairs={{0,1},{1,2},{2,3},{3,4},{4,5},{5,6},{6,7},{7,0},{8,9},{9,10},{10,1... | collective-permute-start | bytes 688136 | tf_op jit(solution)/shard_map/ppermute | solution.py:569
  201.7 8.4 %collective-permute-start.20 = (bf16[32,3584]{1,0:T(8,128)(2,1)S(1)}, bf16[32,3584]{1,0:T(8,128)(2,1)S(1)}, u32[]{:S(2)}, u32[]{:S(2)}) collective-permute-start(bf16[32,3584]{1,0:T(8,128)(2,1)S(1)} %get-tuple-element.41), channel_id=1, source_target_pairs={{0,1},{1,2},{2,3},{3,4},{4,5},{5,6},{6,7},{7,0},{8,9},{9,10},{10,1... | collective-permute-start | bytes 688136 | tf_op jit(solution)/shard_map/ppermute | solution.py:569
  201.8 8.4 %collective-permute-start.23 = (bf16[32,3584]{1,0:T(8,128)(2,1)S(1)}, bf16[32,3584]{1,0:T(8,128)(2,1)S(1)}, u32[]{:S(2)}, u32[]{:S(2)}) collective-permute-start(bf16[32,3584]{1,0:T(8,128)(2,1)S(1)} %get-tuple-element.42), channel_id=1, source_target_pairs={{0,7},{1,0},{2,1},{3,2},{4,3},{5,4},{6,5},{7,6},{8,15},{9,8},{10,9... | collective-permute-start | bytes 688136 | tf_op jit(solution)/shard_map/ppermute | solution.py:569
  211.0 13.2 %collective-permute-start.21 = (bf16[32,3584]{1,0:T(8,128)(2,1)}, bf16[32,3584]{1,0:T(8,128)(2,1)S(1)}, u32[]{:S(2)}, u32[]{:S(2)}) collective-permute-start(bf16[32,3584]{1,0:T(8,128)(2,1)} %get-tuple-element.39), channel_id=1, source_target_pairs={{0,1},{1,2},{2,3},{3,4},{4,5},{5,6},{6,7},{7,0},{8,9},{9,10},{10,1... | collective-permute-start | bytes 688136 | tf_op jit(solution)/shard_map/ppermute | solution.py:569
  211.0 13.2 %collective-permute-start.24 = (bf16[32,3584]{1,0:T(8,128)(2,1)S(1)}, bf16[32,3584]{1,0:T(8,128)(2,1)S(1)}, u32[]{:S(2)}, u32[]{:S(2)}) collective-permute-start(bf16[32,3584]{1,0:T(8,128)(2,1)S(1)} %get-tuple-element.40), channel_id=1, source_target_pairs={{0,7},{1,0},{2,1},{3,2},{4,3},{5,4},{6,5},{7,6},{8,15},{9,8},{10,9... | collective-permute-start | bytes 688136 | tf_op jit(solution)/shard_map/ppermute | solution.py:569
  214.4 26.7 %copy-start.1 = (bf16[160,1280]{1,0:T(8,128)(2,1)S(1)}, bf16[160,1280]{1,0:T(8,128)(2,1)}, u32[]{:S(2)}) copy-start(bf16[160,1280]{1,0:T(8,128)(2,1)} %param.18) | copy-start | bytes 1228804
  (12 other events, 36.6 us)
Sparse Core Ops, SparseCore 0:
  9.9 90.3 all-gather.2
  102.9 65.1 all-gather.4
  191.0 48.1 reduce-scatter.1

commit v5 on v3

--- a/solution.py
+++ b/solution.py
@@ -174,14 +174,25 @@
     out_ref[...] = jnp.dot(pick, incoming_ref[...], preferred_element_type=F32).astype(BF16)
 
 
-def rows_fetch(place, shifts, n, whole_hbm, whole, sems):
-    chunk = whole.shape[0] // len(shifts)
-    fetch = []
-    for j, shift in enumerate(shifts):
-        at = lax.rem(place + shift + n, n)
-        source = whole_hbm.at[pl.ds(pl.multiple_of(at * chunk, 16), chunk), :]
-        fetch.append(pltpu.make_async_copy(source, whole.at[pl.ds(j * chunk, chunk), :], sems.at[j]))
+def tile_fetch(places, whole_hbm, whole, sems, tile):
+    chunk = whole.shape[0] // len(places)
+    tiles = pl.cdiv(whole.shape[1], tile)
+
+    def fetch(j, start, size):
+        columns = pl.ds(start, size)
+        copies = []
+        for k, at in enumerate(places):
+            source = whole_hbm.at[pl.ds(pl.multiple_of(at * chunk, 16), chunk), columns]
+            place = whole.at[pl.ds(k * chunk, chunk), columns]
+            copies.append(pltpu.make_async_copy(source, place, sems.at[k * tiles + j]))
+        return copies
+
     return fetch
+
+
+def run(copies, what):
+    for copy in copies:
+        getattr(copy, what)()
 
 
 def scaled_blocks(blocks, gains, scaled, squares):
@@ -195,40 +206,81 @@
 
 def early_kernel(shifts, place_ref, *refs):
     count = len(shifts)
-    blocks, gain_ref, whole_hbm, sums_ref, squares_ref, scaled, whole, sems = refs[:count], *refs[count:]
-    n = gain_ref.shape[0]
-    fetch = rows_fetch(place_ref[0], shifts, n, whole_hbm, whole, sems)
-    for copy in fetch:
-        copy.start()
-    gains = [gain_ref[lax.rem(place_ref[0] + shift + n, n)] for shift in shifts]
+    blocks, gain_ref, whole_hbm, sums_hbm, squares_ref = refs[:count], *refs[count : count + 4]
+    scaled, whole, sums, sems = refs[count + 4 :]
+    n, tile, width = gain_ref.shape[0], 256, sums.shape[1]
+    places = [lax.rem(place_ref[0] + shift + n, n) for shift in shifts]
+    fetch = tile_fetch(places, whole_hbm, whole, sems, tile)
+    full, rest = width // tile, width % tile
+    last = (full, full * tile, rest)
+
+    def part(j):
+        return j, pl.multiple_of(j * tile, tile), tile
+
+    @pl.loop(0, full)
+    def _(j):
+        run(fetch(*part(j)), "start")
+
+    run(fetch(*last), "start")
     zero = jnp.zeros((blocks[0].shape[0], 1), F32)
-    squares_ref[...] = scaled_blocks(blocks, gains, scaled, zero)
-    for copy in fetch:
-        copy.wait()
-    tile = 256
-    width = sums_ref.shape[1]
-
-    def step(start, size):
-        sums_ref[:, pl.ds(start, size)] = jnp.dot(
-            scaled[...], whole[:, pl.ds(start, size)], preferred_element_type=F32
-        )
-
-    @pl.loop(0, width // tile)
-    def _(j):
-        step(pl.multiple_of(j * tile, tile), tile)
-
-    if width % tile:
-        step(width // tile * tile, width % tile)
+    squares_ref[...] = scaled_blocks(blocks, [gain_ref[at] for at in places], scaled, zero)
+
+    def result(j, start, size):
+        columns = pl.ds(start, size)
+        place = sems.at[count * (full + 1) + j]
+        return pltpu.make_async_copy(sums.at[:, columns], sums_hbm.at[:, columns], place)
+
+    def step(j, start, size):
+        run(fetch(j, start, size), "wait")
+        columns = pl.ds(start, size)
+        sums[:, columns] = jnp.dot(scaled[...], whole[:, columns], preferred_element_type=F32)
+        result(j, start, size).start()
+
+    @pl.loop(0, full)
+    def _(j):
+        step(*part(j))
+
+    step(*last)
+
+    @pl.loop(0, full)
+    def _(j):
+        result(*part(j)).wait()
+
+    result(*last).wait()
 
 
 def late_kernel(shifts, early, units, place_ref, *refs):
     n = len(shifts)
-    blocks, gain_ref, whole_hbm, sums_ref, squares_ref, hidden_ref, own_ref = refs[:n], *refs[n : n + 6]
-    scaled, whole, sems = refs[n + 6 :]
-    fetch = rows_fetch(place_ref[0], shifts[early:], n, whole_hbm, whole, sems)
-    for copy in fetch:
-        copy.start()
+    blocks, gain_ref, whole_hbm, sums_hbm, squares_ref, hidden_ref, own_ref = refs[:n], *refs[n : n + 6]
+    scaled, whole, sums, sems = refs[n + 6 :]
+    tile = 256
     places = [lax.rem(place_ref[0] + shift + n, n) for shift in shifts]
+    fetch = tile_fetch(places[early:], whole_hbm, whole, sems, tile)
+    width = whole.shape[1]
+    tiles = pl.cdiv(width, tile)
+    apart = width - units
+    full, rest = units // tile, units % tile
+
+    def both(j, start, size):
+        copies = []
+        whole_tiles = size if size == tile else apart - full * tile
+        for k, first, size in ((0, 0, whole_tiles), (full + 1, apart, size)):
+            copies += fetch(k + j, first + start, size)
+            columns = pl.ds(first + start, size)
+            place = sems.at[(n - early) * tiles + k + j]
+            copies.append(pltpu.make_async_copy(sums_hbm.at[:, columns], sums.at[:, columns], place))
+        return copies
+
+    last = (full, full * tile, rest)
+
+    def part(j):
+        return j, pl.multiple_of(j * tile, tile), tile
+
+    @pl.loop(0, full)
+    def _(j):
+        run(both(*part(j)), "start")
+
+    run(both(*last), "start")
     gains = [gain_ref[at] for at in places[early:]]
     squares = scaled_blocks(blocks[early:], gains, scaled, squares_ref[...])
     scale = lax.rsqrt(squares / whole_hbm.shape[0] + EPSILON)
@@ -236,15 +288,13 @@
     first = pl.multiple_of(place_ref[0] * own, own)
     for at, block in zip(places, blocks):
         own_ref[at] = block[pl.ds(first, own), :]
-    for copy in fetch:
-        copy.wait()
-    apart, tile = whole.shape[1] - units, 256
-
-    def step(start, size):
+
+    def step(j, start, size):
+        run(both(j, start, size), "wait")
         gate, upward = (
             scale
             * (
-                sums_ref[:, pl.ds(at, size)]
+                sums[:, pl.ds(at, size)]
                 + jnp.dot(scaled[...], whole[:, pl.ds(at, size)], preferred_element_type=F32)
             )
             for at in (start, apart + start)
@@ -252,11 +302,11 @@
         value = gate * (1.0 / (1.0 + jnp.exp(-gate))) * upward
         hidden_ref[:, pl.ds(start, size)] = value.astype(BF16)
 
-    @pl.loop(0, units // tile)
-    def _(j):
-        step(pl.multiple_of(j * tile, tile), tile)
-
-    step(units // tile * tile, units % tile)
+    @pl.loop(0, full)
+    def _(j):
+        step(*part(j))
+
+    step(*last)
 
 
 def down_kernel(tile, hidden_ref, weight_hbm, out_hbm, weight, out, sems):
@@ -289,11 +339,16 @@
 def call(kernel, out_shape, specs, flops, scratch=(), mib=16, out_space=VMEM):
     def run(*args):
         moved = sum(a.size * a.dtype.itemsize for a in args)
+        if isinstance(out_shape, tuple):
+            spaces = out_space if isinstance(out_space, tuple) else (out_space,) * len(out_shape)
+            outs = tuple(pl.BlockSpec(memory_space=space) for space in spaces)
+        else:
+            outs = pl.BlockSpec(memory_space=out_space)
         return pl.pallas_call(
             kernel,
             out_shape=out_shape,
             in_specs=specs,
-            out_specs=jax.tree.map(lambda _: pl.BlockSpec(memory_space=out_space), out_shape),
+            out_specs=outs,
             scratch_shapes=scratch,
             compiler_params=pltpu.CompilerParams(vmem_limit_bytes=mib << 20),
             cost_estimate=pl.CostEstimate(flops=flops, bytes_accessed=moved, transcendentals=0),
@@ -464,13 +519,23 @@
     here = plane.reshape(1)
     padded = 2 * units + gap
     gains = llm_gain.reshape(n, 1, width)
+    tiles = pl.cdiv(padded, 256)
+
+    def scratch(count):
+        return [
+            pltpu.VMEM((seq_count, count * width), BF16),
+            pltpu.VMEM((count * width, padded), BF16),
+            pltpu.VMEM((seq_count, padded), F32),
+            pltpu.SemaphoreType.DMA(((count + 1) * tiles,)),
+        ]
+
     blocks = [sequence]
     a = b = sequence
     for k in range(1, n // 2 + 1):
         a = lax.ppermute(a, "tensor", shifted("tensor", 1))
         if k < n // 2:
             b = lax.ppermute(b, "tensor", shifted("tensor", -1))
-        if k == 3:
+        if k == n // 2 - 1:
             sums, squares = call(
                 functools.partial(early_kernel, shifts[:early]),
                 (
@@ -479,12 +544,9 @@
                 ),
                 [smem] + [vmem] * (early + 1) + [hbm],
                 4 * seq_count * early * width * units,
-                scratch=[
-                    pltpu.VMEM((seq_count, early * width), BF16),
-                    pltpu.VMEM((early * width, padded), BF16),
-                    pltpu.SemaphoreType.DMA((early,)),
-                ],
+                scratch=scratch(early),
                 mib=48,
+                out_space=(HBM, VMEM),
             )(here, *blocks, gains, whole)
             a, b, sums = lax.optimization_barrier((a, b, sums))
         blocks.append(a)
@@ -496,13 +558,9 @@
             jax.ShapeDtypeStruct((seq_count, units), BF16),
             jax.ShapeDtypeStruct((n, own_count, width), BF16),
         ),
-        [smem] + [vmem] * (n + 1) + [hbm] + [vmem] * 2,
+        [smem] + [vmem] * (n + 1) + [hbm] * 2 + [vmem],
         4 * seq_count * (n - early) * width * units,
-        scratch=[
-            pltpu.VMEM((seq_count, (n - early) * width), BF16),
-            pltpu.VMEM(((n - early) * width, padded), BF16),
-            pltpu.SemaphoreType.DMA((n - early,)),
-        ],
+        scratch=scratch(n - early),
         mib=48,
     )(here, *blocks, gains, whole, sums, squares)
     down_tile = 512

time: 250 us -> 242 us (0.968)
  Pallas kernels: 57.7 us -> 50 us
    pallas_call x9, Pallas kernels: 57.7 us -> 50 us  [run(): pl.pallas_call(kernel, out_shape=out_shape, in_specs=specs, out_specs=out...]
  transfers between devices with their start and end apart: 22 -> 22, of which waited for: 9 -> 10; matrix products, arithmetic and copies ran while one was open for 3% -> 3% of each run, Pallas kernels for 19% -> 17%
where the time goes in v5:
time: 242 us
  waiting for transfers between devices  128 us (53%)
  Pallas kernels  50 us (21%)
  starting transfers between devices  35 us (14%)
  between operations  13.5 us (6%)
  local copies, waits for them, and re-layouts  12.4 us (5%)
    reduce_scatter x1, waiting for transfers between devices, body(): lax.psum_scatter(terms, 'tensor', scatter_dimension=0, tiled=True)  53 us
    pallas_call x9, Pallas kernels, run(): pl.pallas_call(kernel, out_shape=out_shape, in_specs=specs, out_specs=out...  50 us
    ppermute x4, waiting for transfers between devices, body(): a = lax.ppermute(a, 'tensor', shifted('tensor', 1))  31.5 us
    ppermute x3, waiting for transfers between devices, body(): ups.append(lax.ppermute(ups[-1], 'tensor', shifted('tensor', 1)))  22.4 us
    all_to_all x1, waiting for transfers between devices, body(): lax.all_to_all(outgoing.reshape(owner_count, capacity, width), 'dp', spli...  19.4 us
    ppermute x3, starting transfers between devices, body(): downs.append(lax.ppermute(away, 'tensor', shifted('tensor', -1)))  8.04 us
    all_to_all x1, starting transfers between devices, body(): lax.all_to_all(outgoing.reshape(owner_count, capacity, width), 'dp', spli...  7.37 us
    ppermute x3, starting transfers between devices, body(): b = lax.ppermute(b, 'tensor', shifted('tensor', -1))  5.21 us
  transfers between devices with their start and end apart: 22, of which 10 were waited for; matrix products, arithmetic and copies ran while one was open for 3% of the time, Pallas kernels for 17%

profile of v5, /device:TPU:1, one launch (start us, length us, event | category | flops | bytes accessed | tf_op | source)
XLA Modules:
  0.0 241.7 jit_solution(10342994961700752)
XLA Ops:
  6.6 2.0 concatenate.3
  8.8 2.5 %collective-permute-start = (bf16[80,1280]{1,0:T(8,128)(2,1)S(1)}, bf16[80,1280]{1,0:T(8,128)(2,1)S(1)}, u32[]{:S(2)}, u32[]{:S(2)}) collective-permute-start(bf16[80,1280]{1,0:T(8,128)(2,1)S(1)} %constant_dynamic-slice_fusion.1.refs_0_.refs_7_), channel_id=1, source_target_pairs={{0,1},{1,2},{2,3},{3,4},{4,5},{5,6},{6,7},{7,0},{8,9},{9,10},{10,1... | collective-permute-start | bytes 614408 | tf_op jit(solution)/shard_map/ppermute | solution.py:404
  11.3 4.0 %collective-permute-start.1 = (bf16[80,1280]{1,0:T(8,128)(2,1)S(1)}, bf16[80,1280]{1,0:T(8,128)(2,1)S(1)}, u32[]{:S(2)}, u32[]{:S(2)}) collective-permute-start(bf16[80,1280]{1,0:T(8,128)(2,1)S(1)} %constant_dynamic-slice_fusion.1.refs_0_.refs_7_), channel_id=1, source_target_pairs={{0,7},{1,0},{2,1},{3,2},{4,3},{5,4},{6,5},{7,6},{8,15},{9,8},{10,9... | collective-permute-start | bytes 614408 | tf_op jit(solution)/shard_map/ppermute | solution.py:405
  15.6 1.3 copy-done.10
  16.8 2.9 %shard_map.136.context_ref = bf16[160,512]{1,0:T(8,128)(2,1)S(1)} custom-call(s32[1]{0:T(128)} %bitcast.3.core_ref, bf16[512,1280]{1,0:T(8,128)(2,1)S(1)} %copy-done.2, s32[512,1]{1,0:T(8,128)S(1)} %copy.23.column_ref, s32[1,512]{1,0:T(1,128)S(1)} %copy-done.14, f32[1,1280]{1,0:T(1,128)S(1)} %broadcast_in_dim.33.gain_ref, bf16[3,160,1280]{2,1,0:T(8,128)(2,1)S(1)} %bitcast.18), custom_call_target="tpu_custom_call" | custom-call | flops 796917760 | bytes 2548740 | tf_op jit(solution)/shard_map/pallas_call | solution.py:347
  19.8 0.3 collective-permute-done.above_ref.refs_1_.refs_8_
  20.3 2.7 %collective-permute-start.7 = (bf16[1440,128]{1,0:T(8,128)(2,1)S(1)}, bf16[1440,128]{1,0:T(8,128)(2,1)S(1)}, u32[]{:S(2)}, u32[]{:S(2)}) collective-permute-start(bf16[1440,128]{1,0:T(8,128)(2,1)S(1)} %get-tuple-element.17), channel_id=1, source_target_pairs={{0,7},{1,0},{2,1},{3,2},{4,3},{5,4},{6,5},{7,6},{8,15},{9,8},{10,9... | collective-permute-start | bytes 1105928 | tf_op jit(solution)/shard_map/ppermute | solution.py:413
  23.0 7.4 %collective-permute-done.2.refs_3_.refs_1_ = bf16[1440,128]{1,0:T(8,128)(2,1)S(1)} collective-permute-done((bf16[1440,128]{1,0:T(8,128)(2,1)S(1)}, bf16[1440,128]{1,0:T(8,128)(2,1)S(1)}, u32[]{:S(2)}, u32[]{:S(2)}) %collective-permute-start.2) | collective-permute-done | bytes 368672 | tf_op jit(solution)/shard_map/ppermute | solution.py:411
  30.4 2.7 %collective-permute-start.8 = (bf16[1440,128]{1,0:T(8,128)(2,1)S(1)}, bf16[1440,128]{1,0:T(8,128)(2,1)S(1)}, u32[]{:S(2)}, u32[]{:S(2)}) collective-permute-start(bf16[1440,128]{1,0:T(8,128)(2,1)S(1)} %collective-permute-done.7.refs_4_.refs_2_), channel_id=1, source_target_pairs={{0,7},{1,0},{2,1},{3,2},{4,3},{5,4},{6,5},{7,6},{8,15},{9,8},{10,9... | collective-permute-start | bytes 1105928 | tf_op jit(solution)/shard_map/ppermute | solution.py:413
  33.0 6.6 %collective-permute-done.3.refs_5_.refs_3_ = bf16[1440,128]{1,0:T(8,128)(2,1)S(1)} collective-permute-done((bf16[1440,128]{1,0:T(8,128)(2,1)S(1)}, bf16[1440,128]{1,0:T(8,128)(2,1)S(1)}, u32[]{:S(2)}, u32[]{:S(2)}) %collective-permute-start.3) | collective-permute-done | bytes 368672 | tf_op jit(solution)/shard_map/ppermute | solution.py:411
  39.6 1.4 shard_map.138
  41.0 3.0 %collective-permute-start.10 = (bf16[7,800,128]{2,1,0:T(8,128)(2,1)}, bf16[7,800,128]{2,1,0:T(8,128)(2,1)}, u32[]{:S(2)}, u32[]{:S(2)}) collective-permute-start(bf16[7,800,128]{2,1,0:T(8,128)(2,1)} %shard_map.138), channel_id=1, source_target_pairs={{0,8},{8,0},{16,24},{24,16},{32,40},{40,32},{48,56},{56,48},{64,72... | collective-permute-start | bytes 4300808 | tf_op jit(solution)/shard_map/ppermute | solution.py:431
  44.6 2.7 %collective-permute-start.9 = (bf16[640,128]{1,0:T(8,128)(2,1)S(1)}, bf16[640,128]{1,0:T(8,128)(2,1)S(1)}, u32[]{:S(2)}, u32[]{:S(2)}) collective-permute-start(bf16[640,128]{1,0:T(8,128)(2,1)S(1)} %slice.13), channel_id=1, source_target_pairs={{0,7},{1,0},{2,1},{3,2},{4,3},{5,4},{6,5},{7,6},{8,15},{9,8},{10,9... | collective-permute-start | bytes 491528 | tf_op jit(solution)/shard_map/ppermute | solution.py:413
  47.3 8.4 %collective-permute-done.4.refs_5_.refs_1_ = bf16[1440,128]{1,0:T(8,128)(2,1)S(1)} collective-permute-done((bf16[1440,128]{1,0:T(8,128)(2,1)S(1)}, bf16[1440,128]{1,0:T(8,128)(2,1)S(1)}, u32[]{:S(2)}, u32[]{:S(2)}) %collective-permute-start.4) | collective-permute-done | bytes 368672 | tf_op jit(solution)/shard_map/ppermute | solution.py:411
  55.8 1.1 collective-permute-start.6
  56.9 0.8 fusion.2
  57.7 1.3 select_n.51.refs_6_
  59.0 1.3 copy.26.refs_7_
  60.3 0.6 broadcast_in_dim.34.refs_4_
  60.9 0.7 copy-done.18
  61.6 7.2 %shard_map.139.refs_3_ = f32[512,1280]{1,0:T(8,128)} custom-call(bf16[1440,128]{1,0:T(8,128)(2,1)} %copy-done.13, bf16[1440,128]{1,0:T(8,128)(2,1)} %copy-done.7, bf16[1440,128]{1,0:T(8,128)(2,1)} %copy-done.8, bf16[1440,128]{1,0:T(8,128)(2,1)} %copy-done.9, bf16[1440,128]{1,0:T(8,128)(2,1)} %copy-done.3, bf16[1440,128]{1,0:T(8,128)(2,1)} %copy-done.15, ...), custom_call_target="tpu_custom_call" | custom-call | flops 1677721600 | bytes 5734400 | tf_op jit(solution)/shard_map/pallas_call | solution.py:347
  68.8 0.6 copy-done.17
  69.5 0.2 copy-done.16
  69.7 7.7 %shard_map.140 = bf16[1024,448]{1,0:T(8,128)(2,1)} custom-call(bf16[640,128]{1,0:T(8,128)(2,1)} %copy-done.17, bf16[1440,128]{1,0:T(8,128)(2,1)} %copy-done.15, bf16[1440,128]{1,0:T(8,128)(2,1)} %copy-done.16, f32[512,1280]{1,0:T(8,128)} %shard_map.139.refs_3_, f32[1,1280]{1,0:T(1,128)} %broadcast_in_dim.34.refs_4_, bf16[448,5120]{1,0:T(8,128)(2,1)} %bitcast.21, ...), custom_call_target="tpu_custom_call" | custom-call | flops 587202560 | bytes 9036800 | tf_op jit(solution)/shard_map/pallas_call | solution.py:347
  77.4 7.4 %all-to-all-start = ((bf16[32,32,448]{2,1,0:T(8,128)(2,1)}), bf16[32,32,448]{2,1,0:T(8,128)(2,1)S(1)}, u32[]{:S(2)}, u32[]{:S(2)}) async-start(bf16[32,32,448]{2,1,0:T(8,128)(2,1)} %bitcast.22), calls=%async_computation | async-start | bytes 2097152 | tf_op jit(solution)/shard_map/all_to_all | solution.py:494
  84.8 0.2 dynamic-slice_reduce_fusion
  85.0 0.7 fusion.7
  86.0 19.4 %all-to-all-done = bf16[32,32,448]{2,1,0:T(8,128)(2,1)S(1)} async-done(((bf16[32,32,448]{2,1,0:T(8,128)(2,1)}), bf16[32,32,448]{2,1,0:T(8,128)(2,1)S(1)}, u32[]{:S(2)}, u32[]{:S(2)}) %all-to-all-start) | async-done | bytes 917536 | tf_op jit(solution)/shard_map/all_to_all | solution.py:494
  105.4 0.7 shard_map.141.refs_0_
  106.1 2.0 collective-permute-start.11
  108.2 1.2 collective-permute-start.12
  109.3 10.6 %collective-permute-done.11.refs_1_ = bf16[512,448]{1,0:T(8,128)(2,1)S(1)} collective-permute-done((bf16[512,448]{1,0:T(8,128)(2,1)S(1)}, bf16[512,448]{1,0:T(8,128)(2,1)S(1)}, u32[]{:S(2)}, u32[]{:S(2)}) %collective-permute-start.11) | collective-permute-done | bytes 458784 | tf_op jit(solution)/shard_map/ppermute | solution.py:535
  120.0 0.9 collective-permute-start.13
  120.9 1.7 collective-permute-start.14
  122.7 9.7 %collective-permute-done.13.refs_3_ = bf16[512,448]{1,0:T(8,128)(2,1)S(1)} collective-permute-done((bf16[512,448]{1,0:T(8,128)(2,1)S(1)}, bf16[512,448]{1,0:T(8,128)(2,1)S(1)}, u32[]{:S(2)}, u32[]{:S(2)}) %collective-permute-start.13) | collective-permute-done | bytes 458784 | tf_op jit(solution)/shard_map/ppermute | solution.py:535
  132.4 0.4 collective-permute-start.15
  132.8 2.3 collective-permute-start.16
  135.1 10.6 %shard_map.142 = (f32[512,2464]{1,0:T(8,128)}, f32[512,1]{1,0:T(8,128)S(1)}) custom-call(s32[1]{0:T(128)} %bitcast.place_ref, bf16[512,448]{1,0:T(8,128)(2,1)S(1)} %shard_map.141.refs_0_, bf16[512,448]{1,0:T(8,128)(2,1)S(1)} %collective-permute-done.11.refs_1_, bf16[512,448]{1,0:T(8,128)(2,1)S(1)} %collective-permute-done.12.refs_2_, ...), custom_call_target="tpu_custom_call" | custom-call | flops 5431623680 | bytes 19970052 | tf_op jit(solution)/shard_map/pallas_call | solution.py:347
  145.9 11.1 %collective-permute-done.17.refs_7_ = bf16[512,448]{1,0:T(8,128)(2,1)S(1)} collective-permute-done((bf16[512,448]{1,0:T(8,128)(2,1)S(1)}, bf16[512,448]{1,0:T(8,128)(2,1)S(1)}, u32[]{:S(2)}, u32[]{:S(2)}) %collective-permute-start.17) | collective-permute-done | bytes 458784 | tf_op jit(solution)/shard_map/ppermute | solution.py:535
  157.0 9.6 %shard_map.143 = (bf16[512,1184]{1,0:T(8,128)(2,1)}, bf16[8,64,448]{2,1,0:T(8,128)(2,1)S(1)}) custom-call(s32[1]{0:T(128)} %bitcast.place_ref, bf16[512,448]{1,0:T(8,128)(2,1)S(1)} %shard_map.141.refs_0_, bf16[512,448]{1,0:T(8,128)(2,1)S(1)} %collective-permute-done.11.refs_1_, bf16[512,448]{1,0:T(8,128)(2,1)S(1)} %collective-permute-done.12.refs_2_, ...), custom_call_target="tpu_custom_call" | custom-call | flops 3258974208 | bytes 26394628 | tf_op jit(solution)/shard_map/pallas_call | solution.py:347
  166.6 0.8 copy-done.11
  167.4 1.1 all-gather.5.cloned.1.call-done.weight_hbm
  168.5 9.7 %shard_map.144 = bf16[512,3584]{1,0:T(8,128)(2,1)} custom-call(bf16[512,1184]{1,0:T(8,128)(2,1)} %get-tuple-element.25.hidden_ref, bf16[3584,1184]{1,0:T(8,128)(2,1)} %all-gather.5.cloned.1.call-done.weight_hbm), custom_call_target="tpu_custom_call" | custom-call | flops 4345298944 | bytes 9699328 | tf_op jit(solution)/shard_map/pallas_call | solution.py:347
  178.2 1.0 copy-done.12
  179.4 0.6 copy.27
  180.0 0.4 reshape.165
  180.4 53.0 %reduce-scatter.2.cloned.1.call-done = bf16[64,3584]{1,0:T(8,128)(2,1)} async-done(((bf16[512,3584]{1,0:T(8,128)(2,1)}), bf16[64,3584]{1,0:T(8,128)(2,1)}) %reduce-scatter.2.cloned.1.call-update) | async-done | bytes 458768 | tf_op jit(solution)/shard_map/reduce_scatter | solution.py:580
  233.3 1.9 add_convert_fusion
  (86 shorter events, 1.8 us)
Async XLA Ops:
  6.5 2.2 copy-start
  6.5 8.8 %copy-start.14 = (s32[1,512]{1,0:T(1,128)S(1)}, s32[1,512]{1,0:T(1,128)}, u32[]{:S(2)}) copy-start(s32[1,512]{1,0:T(1,128)} %row_ref.1) | copy-start | bytes 6148
  6.5 9.0 %copy-start.21 = (f32[1280]{0:T(1024)S(1)}, f32[1280]{0:T(1024)}, u32[]{:S(2)}) copy-start(f32[1280]{0:T(1024)} %param.16) | copy-start | bytes 15364
  6.5 9.0 %copy-start.2 = (bf16[512,1280]{1,0:T(8,128)(2,1)S(1)}, bf16[512,1280]{1,0:T(8,128)(2,1)}, u32[]{:S(2)}) copy-start(bf16[512,1280]{1,0:T(8,128)(2,1)} %refs_11_.1) | copy-start | bytes 3932164
  6.5 128.6 %all-gather.3.cloned.1.call-start = ((), (), s32[]{:S(2)}) async-start(), calls=%async_computation.2 | async-start | bytes 18923520 | tf_op jit(solution)/shard_map/all_gather | solution.py:438
  8.7 159.8 %all-gather.5.cloned.1.call-start = ((), (), s32[]{:S(2)}) async-start(), calls=%async_computation.3 | async-start | bytes 9461760 | tf_op jit(solution)/shard_map/all_gather | solution.py:493
  8.8 30.8 %copy-start.4 = (bf16[80,1280]{1,0:T(8,128)(2,1)}, bf16[80,1280]{1,0:T(8,128)(2,1)S(1)}, u32[]{:S(2)}) copy-start(bf16[80,1280]{1,0:T(8,128)(2,1)S(1)} %constant_dynamic-slice_fusion.1.refs_0_.refs_7_) | copy-start | bytes 614404
  8.8 11.3 %collective-permute-start = (bf16[80,1280]{1,0:T(8,128)(2,1)S(1)}, bf16[80,1280]{1,0:T(8,128)(2,1)S(1)}, u32[]{:S(2)}, u32[]{:S(2)}) collective-permute-start(bf16[80,1280]{1,0:T(8,128)(2,1)S(1)} %constant_dynamic-slice_fusion.1.refs_0_.refs_7_), channel_id=1, source_target_pairs={{0,1},{1,2},{2,3},{3,4},{4,5},{5,6},{6,7},{7,0},{8,9},{9,10},{10,1... | collective-permute-start | bytes 614408 | tf_op jit(solution)/shard_map/ppermute | solution.py:404
  11.3 8.7 %collective-permute-start.1 = (bf16[80,1280]{1,0:T(8,128)(2,1)S(1)}, bf16[80,1280]{1,0:T(8,128)(2,1)S(1)}, u32[]{:S(2)}, u32[]{:S(2)}) collective-permute-start(bf16[80,1280]{1,0:T(8,128)(2,1)S(1)} %constant_dynamic-slice_fusion.1.refs_0_.refs_7_), channel_id=1, source_target_pairs={{0,7},{1,0},{2,1},{3,2},{4,3},{5,4},{6,5},{7,6},{8,15},{9,8},{10,9... | collective-permute-start | bytes 614408 | tf_op jit(solution)/shard_map/ppermute | solution.py:405
  15.5 1.3 copy-start.10
  20.1 20.9 %copy-start.5 = (bf16[80,1280]{1,0:T(8,128)(2,1)}, bf16[80,1280]{1,0:T(8,128)(2,1)S(1)}, u32[]{:S(2)}) copy-start(bf16[80,1280]{1,0:T(8,128)(2,1)S(1)} %collective-permute-done.above_ref.refs_1_.refs_8_) | copy-start | bytes 614404
  20.1 20.9 %copy-start.6 = (bf16[80,1280]{1,0:T(8,128)(2,1)}, bf16[80,1280]{1,0:T(8,128)(2,1)S(1)}, u32[]{:S(2)}) copy-start(bf16[80,1280]{1,0:T(8,128)(2,1)S(1)} %collective-permute-done.1.below_ref.refs_2_.refs_9_) | copy-start | bytes 614404
  20.2 2.8 %copy-start.13 = (bf16[1440,128]{1,0:T(8,128)(2,1)}, bf16[1440,128]{1,0:T(8,128)(2,1)S(1)}, u32[]{:S(2)}) copy-start(bf16[1440,128]{1,0:T(8,128)(2,1)S(1)} %get-tuple-element.16.refs_0_) | copy-start | bytes 1105924
  20.2 23.8 %copy-start.19 = (s32[32,32]{1,0:T(8,128)S(1)}, s32[32,32]{1,0:T(8,128)}, u32[]{:S(2)}) copy-start(s32[32,32]{1,0:T(8,128)} %param.22) | copy-start | bytes 12292
  20.2 10.1 %collective-permute-start.2 = (bf16[1440,128]{1,0:T(8,128)(2,1)S(1)}, bf16[1440,128]{1,0:T(8,128)(2,1)S(1)}, u32[]{:S(2)}, u32[]{:S(2)}) collective-permute-start(bf16[1440,128]{1,0:T(8,128)(2,1)S(1)} %get-tuple-element.16.refs_0_), channel_id=1, source_target_pairs={{0,1},{1,2},{2,3},{3,4},{4,5},{5,6},{6,7},{7,0},{8,9},{9,10},{10,1... | collective-permute-start | bytes 1105928 | tf_op jit(solution)/shard_map/ppermute | solution.py:411
  20.3 36.6 %copy-start.23 = (bf16[384,448]{0,1:T(8,128)(2,1)S(1)}, bf16[384,448]{0,1:T(8,128)(2,1)}, u32[]{:S(2)}) copy-start(bf16[384,448]{0,1:T(8,128)(2,1)} %param.21) | copy-start | bytes 1032196
  20.3 10.0 %collective-permute-start.7 = (bf16[1440,128]{1,0:T(8,128)(2,1)S(1)}, bf16[1440,128]{1,0:T(8,128)(2,1)S(1)}, u32[]{:S(2)}, u32[]{:S(2)}) collective-permute-start(bf16[1440,128]{1,0:T(8,128)(2,1)S(1)} %get-tuple-element.17), channel_id=1, source_target_pairs={{0,7},{1,0},{2,1},{3,2},{4,3},{5,4},{6,5},{7,6},{8,15},{9,8},{10,9... | collective-permute-start | bytes 1105928 | tf_op jit(solution)/shard_map/ppermute | solution.py:413
  30.4 14.2 %copy-start.7 = (bf16[1440,128]{1,0:T(8,128)(2,1)}, bf16[1440,128]{1,0:T(8,128)(2,1)S(1)}, u32[]{:S(2)}) copy-start(bf16[1440,128]{1,0:T(8,128)(2,1)S(1)} %collective-permute-done.2.refs_3_.refs_1_) | copy-start | bytes 1105924
  30.4 9.2 %collective-permute-start.3 = (bf16[1440,128]{1,0:T(8,128)(2,1)S(1)}, bf16[1440,128]{1,0:T(8,128)(2,1)S(1)}, u32[]{:S(2)}, u32[]{:S(2)}) collective-permute-start(bf16[1440,128]{1,0:T(8,128)(2,1)S(1)} %collective-permute-done.2.refs_3_.refs_1_), channel_id=1, source_target_pairs={{0,1},{1,2},{2,3},{3,4},{4,5},{5,6},{6,7},{7,0},{8,9},{9,10},{10,1... | collective-permute-start | bytes 1105928 | tf_op jit(solution)/shard_map/ppermute | solution.py:411
  30.4 14.2 %copy-start.8 = (bf16[1440,128]{1,0:T(8,128)(2,1)}, bf16[1440,128]{1,0:T(8,128)(2,1)S(1)}, u32[]{:S(2)}) copy-start(bf16[1440,128]{1,0:T(8,128)(2,1)S(1)} %collective-permute-done.7.refs_4_.refs_2_) | copy-start | bytes 1105924
  30.4 9.2 %collective-permute-start.8 = (bf16[1440,128]{1,0:T(8,128)(2,1)S(1)}, bf16[1440,128]{1,0:T(8,128)(2,1)S(1)}, u32[]{:S(2)}, u32[]{:S(2)}) collective-permute-start(bf16[1440,128]{1,0:T(8,128)(2,1)S(1)} %collective-permute-done.7.refs_4_.refs_2_), channel_id=1, source_target_pairs={{0,7},{1,0},{2,1},{3,2},{4,3},{5,4},{6,5},{7,6},{8,15},{9,8},{10,9... | collective-permute-start | bytes 1105928 | tf_op jit(solution)/shard_map/ppermute | solution.py:413
  39.6 4.9 %copy-start.9 = (bf16[1440,128]{1,0:T(8,128)(2,1)}, bf16[1440,128]{1,0:T(8,128)(2,1)S(1)}, u32[]{:S(2)}) copy-start(bf16[1440,128]{1,0:T(8,128)(2,1)S(1)} %collective-permute-done.3.refs_5_.refs_3_) | copy-start | bytes 1105924
  39.6 4.9 %copy-start.3 = (bf16[1440,128]{1,0:T(8,128)(2,1)}, bf16[1440,128]{1,0:T(8,128)(2,1)S(1)}, u32[]{:S(2)}) copy-start(bf16[1440,128]{1,0:T(8,128)(2,1)S(1)} %collective-permute-done.8.refs_6_.refs_4_) | copy-start | bytes 1105924
  41.0 19.9 %collective-permute-start.10 = (bf16[7,800,128]{2,1,0:T(8,128)(2,1)}, bf16[7,800,128]{2,1,0:T(8,128)(2,1)}, u32[]{:S(2)}, u32[]{:S(2)}) collective-permute-start(bf16[7,800,128]{2,1,0:T(8,128)(2,1)} %shard_map.138), channel_id=1, source_target_pairs={{0,8},{8,0},{16,24},{24,16},{32,40},{40,32},{48,56},{56,48},{64,72... | collective-permute-start | bytes 4300808 | tf_op jit(solution)/shard_map/ppermute | solution.py:431
  44.2 11.5 %collective-permute-start.4 = (bf16[1440,128]{1,0:T(8,128)(2,1)S(1)}, bf16[1440,128]{1,0:T(8,128)(2,1)S(1)}, u32[]{:S(2)}, u32[]{:S(2)}) collective-permute-start(bf16[1440,128]{1,0:T(8,128)(2,1)S(1)} %collective-permute-done.3.refs_5_.refs_3_), channel_id=1, source_target_pairs={{0,1},{1,2},{2,3},{3,4},{4,5},{5,6},{6,7},{7,0},{8,9},{9,10},{10,1... | collective-permute-start | bytes 1105928 | tf_op jit(solution)/shard_map/ppermute | solution.py:411
  44.6 16.4 %collective-permute-start.9 = (bf16[640,128]{1,0:T(8,128)(2,1)S(1)}, bf16[640,128]{1,0:T(8,128)(2,1)S(1)}, u32[]{:S(2)}, u32[]{:S(2)}) collective-permute-start(bf16[640,128]{1,0:T(8,128)(2,1)S(1)} %slice.13), channel_id=1, source_target_pairs={{0,7},{1,0},{2,1},{3,2},{4,3},{5,4},{6,5},{7,6},{8,15},{9,8},{10,9... | collective-permute-start | bytes 491528 | tf_op jit(solution)/shard_map/ppermute | solution.py:413
  55.7 4.6 %copy-start.15 = (bf16[1440,128]{1,0:T(8,128)(2,1)}, bf16[1440,128]{1,0:T(8,128)(2,1)S(1)}, u32[]{:S(2)}) copy-start(bf16[1440,128]{1,0:T(8,128)(2,1)S(1)} %collective-permute-done.4.refs_5_.refs_1_) | copy-start | bytes 1105924
  55.7 4.6 %copy-start.22 = (f32[1280]{0:T(1024)S(1)}, f32[1280]{0:T(1024)}, u32[]{:S(2)}) copy-start(f32[1280]{0:T(1024)} %param.19) | copy-start | bytes 15364
  55.7 13.1 %collective-permute-start.5 = (bf16[640,128]{1,0:T(8,128)(2,1)S(1)}, bf16[640,128]{1,0:T(8,128)(2,1)S(1)}, u32[]{:S(2)}, u32[]{:S(2)}) collective-permute-start(bf16[640,128]{1,0:T(8,128)(2,1)S(1)} %slice.12), channel_id=1, source_target_pairs={{0,1},{1,2},{2,3},{3,4},{4,5},{5,6},{6,7},{7,0},{8,9},{9,10},{10,1... | collective-permute-start | bytes 491528 | tf_op jit(solution)/shard_map/ppermute | solution.py:414
  55.8 13.0 %collective-permute-start.6 = (bf16[1440,128]{1,0:T(8,128)(2,1)S(1)}, bf16[1440,128]{1,0:T(8,128)(2,1)S(1)}, u32[]{:S(2)}, u32[]{:S(2)}) collective-permute-start(bf16[1440,128]{1,0:T(8,128)(2,1)S(1)} %collective-permute-done.4.refs_5_.refs_1_), channel_id=1, source_target_pairs={{0,8},{8,0},{16,24},{24,16},{32,40},{40,32},{48,56},{56,48},{64,72... | collective-permute-start | bytes 1105928 | tf_op jit(solution)/shard_map/ppermute | solution.py:432
  60.9 0.7 copy-start.18
  68.8 0.7 copy-start.17
  68.8 0.8 copy-start.16
  77.4 45.2 %copy-start.20 = (f32[3584]{0:T(1024)S(1)}, f32[3584]{0:T(1024)}, u32[]{:S(2)}) copy-start(f32[3584]{0:T(1024)} %param.24) | copy-start | bytes 43012
  77.4 28.0 %all-to-all-start = ((bf16[32,32,448]{2,1,0:T(8,128)(2,1)}), bf16[32,32,448]{2,1,0:T(8,128)(2,1)S(1)}, u32[]{:S(2)}, u32[]{:S(2)}) async-start(bf16[32,32,448]{2,1,0:T(8,128)(2,1)} %bitcast.22), calls=%async_computation | async-start | bytes 2097152 | tf_op jit(solution)/shard_map/all_to_all | solution.py:494
  84.8 148.5 %reduce-scatter.2.cloned.1.call-start = ((), (), s32[]{:S(2)}) async-start(), calls=%async_computation.4 | async-start | bytes 4128768 | tf_op jit(solution)/shard_map/reduce_scatter | solution.py:580
  106.1 13.8 %collective-permute-start.11 = (bf16[512,448]{1,0:T(8,128)(2,1)S(1)}, bf16[512,448]{1,0:T(8,128)(2,1)S(1)}, u32[]{:S(2)}, u32[]{:S(2)}) collective-permute-start(bf16[512,448]{1,0:T(8,128)(2,1)S(1)} %shard_map.141.refs_0_), channel_id=1, source_target_pairs={{0,1},{1,2},{2,3},{3,4},{4,5},{5,6},{6,7},{7,0},{8,9},{9,10},{10,1... | collective-permute-start | bytes 1376264 | tf_op jit(solution)/shard_map/ppermute | solution.py:535
  108.2 12.7 %collective-permute-start.12 = (bf16[512,448]{1,0:T(8,128)(2,1)S(1)}, bf16[512,448]{1,0:T(8,128)(2,1)S(1)}, u32[]{:S(2)}, u32[]{:S(2)}) collective-permute-start(bf16[512,448]{1,0:T(8,128)(2,1)S(1)} %shard_map.141.refs_0_), channel_id=1, source_target_pairs={{0,7},{1,0},{2,1},{3,2},{4,3},{5,4},{6,5},{7,6},{8,15},{9,8},{10,9... | collective-permute-start | bytes 1376264 | tf_op jit(solution)/shard_map/ppermute | solution.py:537
  120.0 12.5 %collective-permute-start.13 = (bf16[512,448]{1,0:T(8,128)(2,1)S(1)}, bf16[512,448]{1,0:T(8,128)(2,1)S(1)}, u32[]{:S(2)}, u32[]{:S(2)}) collective-permute-start(bf16[512,448]{1,0:T(8,128)(2,1)S(1)} %collective-permute-done.11.refs_1_), channel_id=1, source_target_pairs={{0,1},{1,2},{2,3},{3,4},{4,5},{5,6},{6,7},{7,0},{8,9},{9,10},{10,1... | collective-permute-start | bytes 1376264 | tf_op jit(solution)/shard_map/ppermute | solution.py:535
  120.9 11.9 %collective-permute-start.14 = (bf16[512,448]{1,0:T(8,128)(2,1)S(1)}, bf16[512,448]{1,0:T(8,128)(2,1)S(1)}, u32[]{:S(2)}, u32[]{:S(2)}) collective-permute-start(bf16[512,448]{1,0:T(8,128)(2,1)S(1)} %collective-permute-done.12.refs_2_), channel_id=1, source_target_pairs={{0,7},{1,0},{2,1},{3,2},{4,3},{5,4},{6,5},{7,6},{8,15},{9,8},{10,9... | collective-permute-start | bytes 1376264 | tf_op jit(solution)/shard_map/ppermute | solution.py:537
  132.4 13.3 %collective-permute-start.15 = (bf16[512,448]{1,0:T(8,128)(2,1)S(1)}, bf16[512,448]{1,0:T(8,128)(2,1)S(1)}, u32[]{:S(2)}, u32[]{:S(2)}) collective-permute-start(bf16[512,448]{1,0:T(8,128)(2,1)S(1)} %collective-permute-done.13.refs_3_), channel_id=1, source_target_pairs={{0,1},{1,2},{2,3},{3,4},{4,5},{5,6},{6,7},{7,0},{8,9},{9,10},{10,1... | collective-permute-start | bytes 1376264 | tf_op jit(solution)/shard_map/ppermute | solution.py:535
  132.8 13.0 %collective-permute-start.16 = (bf16[512,448]{1,0:T(8,128)(2,1)S(1)}, bf16[512,448]{1,0:T(8,128)(2,1)}, u32[]{:S(2)}, u32[]{:S(2)}) collective-permute-start(bf16[512,448]{1,0:T(8,128)(2,1)S(1)} %collective-permute-done.14.refs_4_), channel_id=1, source_target_pairs={{0,7},{1,0},{2,1},{3,2},{4,3},{5,4},{6,5},{7,6},{8,15},{9,8},{10,9... | collective-permute-start | bytes 1376264 | tf_op jit(solution)/shard_map/ppermute | solution.py:537
  145.8 11.2 %collective-permute-start.17 = (bf16[512,448]{1,0:T(8,128)(2,1)S(1)}, bf16[512,448]{1,0:T(8,128)(2,1)S(1)}, u32[]{:S(2)}, u32[]{:S(2)}) collective-permute-start(bf16[512,448]{1,0:T(8,128)(2,1)S(1)} %collective-permute-done.15.refs_5_), channel_id=1, source_target_pairs={{0,1},{1,2},{2,3},{3,4},{4,5},{5,6},{6,7},{7,0},{8,9},{9,10},{10,1... | collective-permute-start | bytes 1376264 | tf_op jit(solution)/shard_map/ppermute | solution.py:535
  166.6 0.8 copy-start.11
  178.2 1.0 copy-start.12
  179.3 55.9 %copy-start.1 = (bf16[160,1280]{1,0:T(8,128)(2,1)S(1)}, bf16[160,1280]{1,0:T(8,128)(2,1)}, u32[]{:S(2)}) copy-start(bf16[160,1280]{1,0:T(8,128)(2,1)} %param.18) | copy-start | bytes 1228804
Sparse Core Ops, SparseCore 0:
  9.9 94.1 all-gather.2
  106.7 61.7 all-gather.4
  178.3 54.9 reduce-scatter.1

commit v6 on v5

--- a/solution.py
+++ b/solution.py
@@ -204,10 +204,11 @@
     return squares
 
 
-def early_kernel(shifts, place_ref, *refs):
+def early_kernel(shifts, follows, place_ref, *refs):
     count = len(shifts)
-    blocks, gain_ref, whole_hbm, sums_hbm, squares_ref = refs[:count], *refs[count : count + 4]
-    scaled, whole, sums, sems = refs[count + 4 :]
+    blocks, gain_ref, whole_hbm = refs[:count], refs[count], refs[count + 1]
+    before = refs[count + 2 : count + 4] if follows else None
+    sums_hbm, squares_ref, scaled, whole, sums, sems = refs[count + 2 + 2 * follows :]
     n, tile, width = gain_ref.shape[0], 256, sums.shape[1]
     places = [lax.rem(place_ref[0] + shift + n, n) for shift in shifts]
     fetch = tile_fetch(places, whole_hbm, whole, sems, tile)
@@ -217,13 +218,21 @@
     def part(j):
         return j, pl.multiple_of(j * tile, tile), tile
 
+    def operands(j, start, size):
+        copies = fetch(j, start, size)
+        if follows:
+            columns = pl.ds(start, size)
+            place = sems.at[(count + 1) * (full + 1) + j]
+            copies.append(pltpu.make_async_copy(before[0].at[:, columns], sums.at[:, columns], place))
+        return copies
+
     @pl.loop(0, full)
     def _(j):
-        run(fetch(*part(j)), "start")
-
-    run(fetch(*last), "start")
-    zero = jnp.zeros((blocks[0].shape[0], 1), F32)
-    squares_ref[...] = scaled_blocks(blocks, [gain_ref[at] for at in places], scaled, zero)
+        run(operands(*part(j)), "start")
+
+    run(operands(*last), "start")
+    squares = before[1][...] if follows else jnp.zeros((blocks[0].shape[0], 1), F32)
+    squares_ref[...] = scaled_blocks(blocks, [gain_ref[at] for at in places], scaled, squares)
 
     def result(j, start, size):
         columns = pl.ds(start, size)
@@ -231,9 +240,10 @@
         return pltpu.make_async_copy(sums.at[:, columns], sums_hbm.at[:, columns], place)
 
     def step(j, start, size):
-        run(fetch(j, start, size), "wait")
+        run(operands(j, start, size), "wait")
         columns = pl.ds(start, size)
-        sums[:, columns] = jnp.dot(scaled[...], whole[:, columns], preferred_element_type=F32)
+        total = jnp.dot(scaled[...], whole[:, columns], preferred_element_type=F32)
+        sums[:, columns] = sums[:, columns] + total if follows else total
         result(j, start, size).start()
 
     @pl.loop(0, full)
@@ -515,7 +525,8 @@
     for k in range(1, n // 2):
         shifts += [-k, k]
     shifts.append(-(n // 2))
-    early = 5
+    stages = ((0, 5), (5, 7))
+    early = stages[-1][1]
     here = plane.reshape(1)
     padded = 2 * units + gap
     gains = llm_gain.reshape(n, 1, width)
@@ -526,28 +537,32 @@
             pltpu.VMEM((seq_count, count * width), BF16),
             pltpu.VMEM((count * width, padded), BF16),
             pltpu.VMEM((seq_count, padded), F32),
-            pltpu.SemaphoreType.DMA(((count + 1) * tiles,)),
+            pltpu.SemaphoreType.DMA(((count + 2) * tiles,)),
         ]
 
+    def products(first, last, blocks, before):
+        return call(
+            functools.partial(early_kernel, shifts[first:last], len(before) // 2),
+            (
+                jax.ShapeDtypeStruct((seq_count, padded), F32),
+                jax.ShapeDtypeStruct((seq_count, 1), F32),
+            ),
+            [smem] + [vmem] * (last - first + 1) + [hbm] + [hbm, vmem][: len(before)],
+            4 * seq_count * (last - first) * width * units,
+            scratch=scratch(last - first),
+            mib=48,
+            out_space=(HBM, VMEM),
+        )(here, *blocks[first:last], gains, whole, *before)
+
     blocks = [sequence]
+    sums = ()
     a = b = sequence
     for k in range(1, n // 2 + 1):
         a = lax.ppermute(a, "tensor", shifted("tensor", 1))
         if k < n // 2:
             b = lax.ppermute(b, "tensor", shifted("tensor", -1))
-        if k == n // 2 - 1:
-            sums, squares = call(
-                functools.partial(early_kernel, shifts[:early]),
-                (
-                    jax.ShapeDtypeStruct((seq_count, padded), F32),
-                    jax.ShapeDtypeStruct((seq_count, 1), F32),
-                ),
-                [smem] + [vmem] * (early + 1) + [hbm],
-                4 * seq_count * early * width * units,
-                scratch=scratch(early),
-                mib=48,
-                out_space=(HBM, VMEM),
-            )(here, *blocks, gains, whole)
+        if k >= n // 2 - 1:
+            sums = products(*stages[k - n // 2 + 1], blocks, tuple(sums))
             a, b, sums = lax.optimization_barrier((a, b, sums))
         blocks.append(a)
         if k < n // 2:
@@ -562,7 +577,7 @@
         4 * seq_count * (n - early) * width * units,
         scratch=scratch(n - early),
         mib=48,
-    )(here, *blocks, gains, whole, sums, squares)
+    )(here, *blocks, gains, whole, *sums)
     down_tile = 512
     terms = call(
         functools.partial(down_kernel, down_tile),

time: 242 us -> 240 us (level)
  waiting for transfers between devices: 128 us -> 120 us
  Pallas kernels: 50 us -> 54.9 us
    ppermute x4, waiting for transfers between devices: 31.5 us -> 24.5 us  [body(): a = lax.ppermute(a, 'tensor', shifted('tensor', 1))]
    pallas_call x9 -> x10, Pallas kernels: 50 us -> 54.9 us  [run(): pl.pallas_call(kernel, out_shape=out_shape, in_specs=specs, out_specs=out...]
  transfers between devices with their start and end apart: 22 -> 22, of which waited for: 10 -> 10; matrix products, arithmetic and copies ran while one was open for 3% -> 3% of each run, Pallas kernels for 17% -> 19%
where the time goes in v6:
time: 240 us
  waiting for transfers between devices  120 us (50%)
  Pallas kernels  54.9 us (23%)
  starting transfers between devices  35 us (15%)
  between operations  13.6 us (6%)
  local copies, waits for them, and re-layouts  12.4 us (5%)
  other arithmetic  2.41 us (1%)
    pallas_call x10, Pallas kernels, run(): pl.pallas_call(kernel, out_shape=out_shape, in_specs=specs, out_specs=out...  54.9 us
    reduce_scatter x1, waiting for transfers between devices, body(): lax.psum_scatter(terms, 'tensor', scatter_dimension=0, tiled=True)  50.7 us
    ppermute x4, waiting for transfers between devices, body(): a = lax.ppermute(a, 'tensor', shifted('tensor', 1))  24.5 us
    ppermute x3, waiting for transfers between devices, body(): ups.append(lax.ppermute(ups[-1], 'tensor', shifted('tensor', 1)))  22.4 us
    all_to_all x1, waiting for transfers between devices, body(): lax.all_to_all(outgoing.reshape(owner_count, capacity, width), 'dp', spli...  19.4 us
    ppermute x3, starting transfers between devices, body(): downs.append(lax.ppermute(away, 'tensor', shifted('tensor', -1)))  8.04 us
    all_to_all x1, starting transfers between devices, body(): lax.all_to_all(outgoing.reshape(owner_count, capacity, width), 'dp', spli...  7.37 us
    ppermute x3, starting transfers between devices, body(): b = lax.ppermute(b, 'tensor', shifted('tensor', -1))  7.16 us
  transfers between devices with their start and end apart: 22, of which 10 were waited for; matrix products, arithmetic and copies ran while one was open for 3% of the time, Pallas kernels for 19%

profile of v6, /device:TPU:1, one launch (start us, length us, event | category | flops | bytes accessed | tf_op | source)
XLA Modules:
  0.0 239.5 jit_solution(4158082847146372276)
XLA Ops:
  6.6 2.1 concatenate.3
  8.8 2.5 %collective-permute-start = (bf16[80,1280]{1,0:T(8,128)(2,1)S(1)}, bf16[80,1280]{1,0:T(8,128)(2,1)S(1)}, u32[]{:S(2)}, u32[]{:S(2)}) collective-permute-start(bf16[80,1280]{1,0:T(8,128)(2,1)S(1)} %constant_dynamic-slice_fusion.1.refs_0_.refs_7_), channel_id=1, source_target_pairs={{0,1},{1,2},{2,3},{3,4},{4,5},{5,6},{6,7},{7,0},{8,9},{9,10},{10,1... | collective-permute-start | bytes 614408 | tf_op jit(solution)/shard_map/ppermute | solution.py:414
  11.3 4.0 %collective-permute-start.1 = (bf16[80,1280]{1,0:T(8,128)(2,1)S(1)}, bf16[80,1280]{1,0:T(8,128)(2,1)S(1)}, u32[]{:S(2)}, u32[]{:S(2)}) collective-permute-start(bf16[80,1280]{1,0:T(8,128)(2,1)S(1)} %constant_dynamic-slice_fusion.1.refs_0_.refs_7_), channel_id=1, source_target_pairs={{0,7},{1,0},{2,1},{3,2},{4,3},{5,4},{6,5},{7,6},{8,15},{9,8},{10,9... | collective-permute-start | bytes 614408 | tf_op jit(solution)/shard_map/ppermute | solution.py:415
  15.4 0.1 copy.23.column_ref
  15.6 1.3 copy-done.10
  16.8 2.9 %shard_map.136.context_ref = bf16[160,512]{1,0:T(8,128)(2,1)S(1)} custom-call(s32[1]{0:T(128)} %bitcast.3.core_ref, bf16[512,1280]{1,0:T(8,128)(2,1)S(1)} %copy-done.2, s32[512,1]{1,0:T(8,128)S(1)} %copy.23.column_ref, s32[1,512]{1,0:T(1,128)S(1)} %copy-done.14, f32[1,1280]{1,0:T(1,128)S(1)} %broadcast_in_dim.33.gain_ref, bf16[3,160,1280]{2,1,0:T(8,128)(2,1)S(1)} %bitcast.18), custom_call_target="tpu_custom_call" | custom-call | flops 796917760 | bytes 2548740 | tf_op jit(solution)/shard_map/pallas_call | solution.py:357
  19.8 0.3 collective-permute-done.above_ref.refs_1_.refs_8_
  20.3 2.7 %collective-permute-start.7 = (bf16[1440,128]{1,0:T(8,128)(2,1)S(1)}, bf16[1440,128]{1,0:T(8,128)(2,1)S(1)}, u32[]{:S(2)}, u32[]{:S(2)}) collective-permute-start(bf16[1440,128]{1,0:T(8,128)(2,1)S(1)} %get-tuple-element.23), channel_id=1, source_target_pairs={{0,7},{1,0},{2,1},{3,2},{4,3},{5,4},{6,5},{7,6},{8,15},{9,8},{10,9... | collective-permute-start | bytes 1105928 | tf_op jit(solution)/shard_map/ppermute | solution.py:423
  23.0 7.4 %collective-permute-done.2.refs_3_.refs_1_ = bf16[1440,128]{1,0:T(8,128)(2,1)S(1)} collective-permute-done((bf16[1440,128]{1,0:T(8,128)(2,1)S(1)}, bf16[1440,128]{1,0:T(8,128)(2,1)S(1)}, u32[]{:S(2)}, u32[]{:S(2)}) %collective-permute-start.2) | collective-permute-done | bytes 368672 | tf_op jit(solution)/shard_map/ppermute | solution.py:421
  30.4 2.7 %collective-permute-start.8 = (bf16[1440,128]{1,0:T(8,128)(2,1)S(1)}, bf16[1440,128]{1,0:T(8,128)(2,1)S(1)}, u32[]{:S(2)}, u32[]{:S(2)}) collective-permute-start(bf16[1440,128]{1,0:T(8,128)(2,1)S(1)} %collective-permute-done.7.refs_4_.refs_2_), channel_id=1, source_target_pairs={{0,7},{1,0},{2,1},{3,2},{4,3},{5,4},{6,5},{7,6},{8,15},{9,8},{10,9... | collective-permute-start | bytes 1105928 | tf_op jit(solution)/shard_map/ppermute | solution.py:423
  33.1 6.6 %collective-permute-done.3.refs_5_.refs_3_ = bf16[1440,128]{1,0:T(8,128)(2,1)S(1)} collective-permute-done((bf16[1440,128]{1,0:T(8,128)(2,1)S(1)}, bf16[1440,128]{1,0:T(8,128)(2,1)S(1)}, u32[]{:S(2)}, u32[]{:S(2)}) %collective-permute-start.3) | collective-permute-done | bytes 368672 | tf_op jit(solution)/shard_map/ppermute | solution.py:421
  39.6 1.4 shard_map.138
  41.0 3.0 %collective-permute-start.10 = (bf16[7,800,128]{2,1,0:T(8,128)(2,1)}, bf16[7,800,128]{2,1,0:T(8,128)(2,1)}, u32[]{:S(2)}, u32[]{:S(2)}) collective-permute-start(bf16[7,800,128]{2,1,0:T(8,128)(2,1)} %shard_map.138), channel_id=1, source_target_pairs={{0,8},{8,0},{16,24},{24,16},{32,40},{40,32},{48,56},{56,48},{64,72... | collective-permute-start | bytes 4300808 | tf_op jit(solution)/shard_map/ppermute | solution.py:441
  44.6 2.7 %collective-permute-start.9 = (bf16[640,128]{1,0:T(8,128)(2,1)S(1)}, bf16[640,128]{1,0:T(8,128)(2,1)S(1)}, u32[]{:S(2)}, u32[]{:S(2)}) collective-permute-start(bf16[640,128]{1,0:T(8,128)(2,1)S(1)} %slice.13), channel_id=1, source_target_pairs={{0,7},{1,0},{2,1},{3,2},{4,3},{5,4},{6,5},{7,6},{8,15},{9,8},{10,9... | collective-permute-start | bytes 491528 | tf_op jit(solution)/shard_map/ppermute | solution.py:423
  47.3 8.4 %collective-permute-done.4.refs_5_.refs_1_ = bf16[1440,128]{1,0:T(8,128)(2,1)S(1)} collective-permute-done((bf16[1440,128]{1,0:T(8,128)(2,1)S(1)}, bf16[1440,128]{1,0:T(8,128)(2,1)S(1)}, u32[]{:S(2)}, u32[]{:S(2)}) %collective-permute-start.4) | collective-permute-done | bytes 368672 | tf_op jit(solution)/shard_map/ppermute | solution.py:421
  55.9 1.1 collective-permute-start.6
  56.9 0.8 fusion.2
  57.7 1.3 select_n.51.refs_6_
  59.0 1.3 copy.26.refs_7_
  60.4 0.6 broadcast_in_dim.34.refs_4_
  61.0 0.7 copy-done.18
  61.6 7.2 %shard_map.139.refs_3_ = f32[512,1280]{1,0:T(8,128)} custom-call(bf16[1440,128]{1,0:T(8,128)(2,1)} %copy-done.13, bf16[1440,128]{1,0:T(8,128)(2,1)} %copy-done.7, bf16[1440,128]{1,0:T(8,128)(2,1)} %copy-done.8, bf16[1440,128]{1,0:T(8,128)(2,1)} %copy-done.9, bf16[1440,128]{1,0:T(8,128)(2,1)} %copy-done.3, bf16[1440,128]{1,0:T(8,128)(2,1)} %copy-done.15, ...), custom_call_target="tpu_custom_call" | custom-call | flops 1677721600 | bytes 5734400 | tf_op jit(solution)/shard_map/pallas_call | solution.py:357
  68.9 0.6 copy-done.17
  69.5 0.2 copy-done.16
  69.6 7.7 %shard_map.140 = bf16[1024,448]{1,0:T(8,128)(2,1)} custom-call(bf16[640,128]{1,0:T(8,128)(2,1)} %copy-done.17, bf16[1440,128]{1,0:T(8,128)(2,1)} %copy-done.15, bf16[1440,128]{1,0:T(8,128)(2,1)} %copy-done.16, f32[512,1280]{1,0:T(8,128)} %shard_map.139.refs_3_, f32[1,1280]{1,0:T(1,128)} %broadcast_in_dim.34.refs_4_, bf16[448,5120]{1,0:T(8,128)(2,1)} %bitcast.21, ...), custom_call_target="tpu_custom_call" | custom-call | flops 587202560 | bytes 9036800 | tf_op jit(solution)/shard_map/pallas_call | solution.py:357
  77.4 7.4 %all-to-all-start = ((bf16[32,32,448]{2,1,0:T(8,128)(2,1)}), bf16[32,32,448]{2,1,0:T(8,128)(2,1)S(1)}, u32[]{:S(2)}, u32[]{:S(2)}) async-start(bf16[32,32,448]{2,1,0:T(8,128)(2,1)} %bitcast.22), calls=%async_computation | async-start | bytes 2097152 | tf_op jit(solution)/shard_map/all_to_all | solution.py:504
  84.9 0.2 dynamic-slice_reduce_fusion
  85.0 0.7 fusion.7
  86.0 19.4 %all-to-all-done = bf16[32,32,448]{2,1,0:T(8,128)(2,1)S(1)} async-done(((bf16[32,32,448]{2,1,0:T(8,128)(2,1)}), bf16[32,32,448]{2,1,0:T(8,128)(2,1)S(1)}, u32[]{:S(2)}, u32[]{:S(2)}) %all-to-all-start) | async-done | bytes 917536 | tf_op jit(solution)/shard_map/all_to_all | solution.py:504
  105.4 0.7 shard_map.141.refs_0_
  106.1 1.4 collective-permute-start.11
  107.5 1.8 collective-permute-start.12
  109.3 10.6 %collective-permute-done.11.refs_1_ = bf16[512,448]{1,0:T(8,128)(2,1)S(1)} collective-permute-done((bf16[512,448]{1,0:T(8,128)(2,1)S(1)}, bf16[512,448]{1,0:T(8,128)(2,1)S(1)}, u32[]{:S(2)}, u32[]{:S(2)}) %collective-permute-start.11) | collective-permute-done | bytes 458784 | tf_op jit(solution)/shard_map/ppermute | solution.py:561
  120.0 2.7 %collective-permute-start.14 = (bf16[512,448]{1,0:T(8,128)(2,1)S(1)}, bf16[512,448]{1,0:T(8,128)(2,1)}, u32[]{:S(2)}, u32[]{:S(2)}) collective-permute-start(bf16[512,448]{1,0:T(8,128)(2,1)S(1)} %collective-permute-done.12.refs_2_), channel_id=1, source_target_pairs={{0,7},{1,0},{2,1},{3,2},{4,3},{5,4},{6,5},{7,6},{8,15},{9,8},{10,9... | collective-permute-start | bytes 1376264 | tf_op jit(solution)/shard_map/ppermute | solution.py:563
  122.7 9.7 %collective-permute-done.13.refs_3_ = bf16[512,448]{1,0:T(8,128)(2,1)S(1)} collective-permute-done((bf16[512,448]{1,0:T(8,128)(2,1)S(1)}, bf16[512,448]{1,0:T(8,128)(2,1)S(1)}, u32[]{:S(2)}, u32[]{:S(2)}) %collective-permute-start.13) | collective-permute-done | bytes 458784 | tf_op jit(solution)/shard_map/ppermute | solution.py:561
  132.4 2.7 %collective-permute-start.16 = (bf16[512,448]{1,0:T(8,128)(2,1)}, bf16[512,448]{1,0:T(8,128)(2,1)S(1)}, u32[]{:S(2)}, u32[]{:S(2)}) collective-permute-start(bf16[512,448]{1,0:T(8,128)(2,1)} %collective-permute-done.14.refs_4_), channel_id=1, source_target_pairs={{0,7},{1,0},{2,1},{3,2},{4,3},{5,4},{6,5},{7,6},{8,15},{9,8},{10,9... | collective-permute-start | bytes 1376264 | tf_op jit(solution)/shard_map/ppermute | solution.py:563
  135.1 11.8 %shard_map.142 = (f32[512,2464]{1,0:T(8,128)}, f32[512,1]{1,0:T(8,128)S(1)}) custom-call(s32[1]{0:T(128)} %bitcast.place_ref, bf16[512,448]{1,0:T(8,128)(2,1)S(1)} %shard_map.141.refs_0_, bf16[512,448]{1,0:T(8,128)(2,1)S(1)} %collective-permute-done.11.refs_1_, bf16[512,448]{1,0:T(8,128)(2,1)S(1)} %collective-permute-done.12.refs_2_, ...), custom_call_target="tpu_custom_call" | custom-call | flops 5431623680 | bytes 19970052 | tf_op jit(solution)/shard_map/pallas_call | solution.py:357
  147.0 7.0 %shard_map.143 = (f32[512,2464]{1,0:T(8,128)}, f32[512,1]{1,0:T(8,128)S(1)}) custom-call(s32[1]{0:T(128)} %bitcast.place_ref, bf16[512,448]{1,0:T(8,128)(2,1)S(1)} %collective-permute-done.15.refs_0_.refs_5_, bf16[512,448]{1,0:T(8,128)(2,1)S(1)} %collective-permute-done.16.refs_1_.refs_6_, f32[8,1,448]{2,1,0:T(1,128)S(1)} %reshape.164.refs_5_.refs_2_.refs_8_, ...), custom_call_target="tpu_custom_call" | custom-call | flops 2172649472 | bytes 23642116 | tf_op jit(solution)/shard_map/pallas_call | solution.py:357
  154.0 4.1 %collective-permute-done.17.refs_7_ = bf16[512,448]{1,0:T(8,128)(2,1)S(1)} collective-permute-done((bf16[512,448]{1,0:T(8,128)(2,1)S(1)}, bf16[512,448]{1,0:T(8,128)(2,1)S(1)}, u32[]{:S(2)}, u32[]{:S(2)}) %collective-permute-start.17) | collective-permute-done | bytes 458784 | tf_op jit(solution)/shard_map/ppermute | solution.py:561
  158.1 6.5 %shard_map.144 = (bf16[512,1184]{1,0:T(8,128)(2,1)}, bf16[8,64,448]{2,1,0:T(8,128)(2,1)S(1)}) custom-call(s32[1]{0:T(128)} %bitcast.place_ref, bf16[512,448]{1,0:T(8,128)(2,1)S(1)} %shard_map.141.refs_0_, bf16[512,448]{1,0:T(8,128)(2,1)S(1)} %collective-permute-done.11.refs_1_, bf16[512,448]{1,0:T(8,128)(2,1)S(1)} %collective-permute-done.12.refs_2_, ...), custom_call_target="tpu_custom_call" | custom-call | flops 1086324736 | bytes 26394628 | tf_op jit(solution)/shard_map/pallas_call | solution.py:357
  164.6 0.8 copy-done.11
  165.4 3.1 %all-gather.5.cloned.1.call-done.weight_hbm = bf16[3584,1184]{1,0:T(8,128)(2,1)} async-done(((bf16[112,1184]{1,0:T(8,128)(2,1)}), bf16[3584,1184]{1,0:T(8,128)(2,1)}) %all-gather.5.cloned.1.call-update) | async-done | bytes 8486928 | tf_op jit(solution)/shard_map/all_gather | solution.py:503
  168.5 9.7 %shard_map.145 = bf16[512,3584]{1,0:T(8,128)(2,1)} custom-call(bf16[512,1184]{1,0:T(8,128)(2,1)} %get-tuple-element.37.hidden_ref, bf16[3584,1184]{1,0:T(8,128)(2,1)} %all-gather.5.cloned.1.call-done.weight_hbm), custom_call_target="tpu_custom_call" | custom-call | flops 4345298944 | bytes 9699328 | tf_op jit(solution)/shard_map/pallas_call | solution.py:357
  178.2 1.0 copy-done.12
  179.3 0.6 copy.27
  180.0 0.4 reshape.165
  180.4 50.7 %reduce-scatter.2.cloned.1.call-done = bf16[64,3584]{1,0:T(8,128)(2,1)} async-done(((bf16[512,3584]{1,0:T(8,128)(2,1)}), bf16[64,3584]{1,0:T(8,128)(2,1)}) %reduce-scatter.2.cloned.1.call-update) | async-done | bytes 458768 | tf_op jit(solution)/shard_map/reduce_scatter | solution.py:595
  231.1 1.9 add_convert_fusion
  (87 shorter events, 1.7 us)
Async XLA Ops:
  6.5 2.2 copy-start
  6.5 8.8 %copy-start.14 = (s32[1,512]{1,0:T(1,128)S(1)}, s32[1,512]{1,0:T(1,128)}, u32[]{:S(2)}) copy-start(s32[1,512]{1,0:T(1,128)} %row_ref.1) | copy-start | bytes 6148
  6.5 9.0 %copy-start.21 = (f32[1280]{0:T(1024)S(1)}, f32[1280]{0:T(1024)}, u32[]{:S(2)}) copy-start(f32[1280]{0:T(1024)} %param.16) | copy-start | bytes 15364
  6.5 9.0 %copy-start.2 = (bf16[512,1280]{1,0:T(8,128)(2,1)S(1)}, bf16[512,1280]{1,0:T(8,128)(2,1)}, u32[]{:S(2)}) copy-start(bf16[512,1280]{1,0:T(8,128)(2,1)} %refs_11_.1) | copy-start | bytes 3932164
  6.5 128.6 %all-gather.3.cloned.1.call-start = ((), (), s32[]{:S(2)}) async-start(), calls=%async_computation.2 | async-start | bytes 18923520 | tf_op jit(solution)/shard_map/all_gather | solution.py:448
  8.7 159.8 %all-gather.5.cloned.1.call-start = ((), (), s32[]{:S(2)}) async-start(), calls=%async_computation.3 | async-start | bytes 9461760 | tf_op jit(solution)/shard_map/all_gather | solution.py:503
  8.8 30.8 %copy-start.4 = (bf16[80,1280]{1,0:T(8,128)(2,1)}, bf16[80,1280]{1,0:T(8,128)(2,1)S(1)}, u32[]{:S(2)}) copy-start(bf16[80,1280]{1,0:T(8,128)(2,1)S(1)} %constant_dynamic-slice_fusion.1.refs_0_.refs_7_) | copy-start | bytes 614404
  8.8 11.3 %collective-permute-start = (bf16[80,1280]{1,0:T(8,128)(2,1)S(1)}, bf16[80,1280]{1,0:T(8,128)(2,1)S(1)}, u32[]{:S(2)}, u32[]{:S(2)}) collective-permute-start(bf16[80,1280]{1,0:T(8,128)(2,1)S(1)} %constant_dynamic-slice_fusion.1.refs_0_.refs_7_), channel_id=1, source_target_pairs={{0,1},{1,2},{2,3},{3,4},{4,5},{5,6},{6,7},{7,0},{8,9},{9,10},{10,1... | collective-permute-start | bytes 614408 | tf_op jit(solution)/shard_map/ppermute | solution.py:414
  11.3 8.7 %collective-permute-start.1 = (bf16[80,1280]{1,0:T(8,128)(2,1)S(1)}, bf16[80,1280]{1,0:T(8,128)(2,1)S(1)}, u32[]{:S(2)}, u32[]{:S(2)}) collective-permute-start(bf16[80,1280]{1,0:T(8,128)(2,1)S(1)} %constant_dynamic-slice_fusion.1.refs_0_.refs_7_), channel_id=1, source_target_pairs={{0,7},{1,0},{2,1},{3,2},{4,3},{5,4},{6,5},{7,6},{8,15},{9,8},{10,9... | collective-permute-start | bytes 614408 | tf_op jit(solution)/shard_map/ppermute | solution.py:415
  15.6 1.3 copy-start.10
  20.1 20.9 %copy-start.5 = (bf16[80,1280]{1,0:T(8,128)(2,1)}, bf16[80,1280]{1,0:T(8,128)(2,1)S(1)}, u32[]{:S(2)}) copy-start(bf16[80,1280]{1,0:T(8,128)(2,1)S(1)} %collective-permute-done.above_ref.refs_1_.refs_8_) | copy-start | bytes 614404
  20.1 20.9 %copy-start.6 = (bf16[80,1280]{1,0:T(8,128)(2,1)}, bf16[80,1280]{1,0:T(8,128)(2,1)S(1)}, u32[]{:S(2)}) copy-start(bf16[80,1280]{1,0:T(8,128)(2,1)S(1)} %collective-permute-done.1.below_ref.refs_2_.refs_9_) | copy-start | bytes 614404
  20.2 2.8 %copy-start.13 = (bf16[1440,128]{1,0:T(8,128)(2,1)}, bf16[1440,128]{1,0:T(8,128)(2,1)S(1)}, u32[]{:S(2)}) copy-start(bf16[1440,128]{1,0:T(8,128)(2,1)S(1)} %get-tuple-element.22.refs_0_) | copy-start | bytes 1105924
  20.2 23.8 %copy-start.19 = (s32[32,32]{1,0:T(8,128)S(1)}, s32[32,32]{1,0:T(8,128)}, u32[]{:S(2)}) copy-start(s32[32,32]{1,0:T(8,128)} %param.22) | copy-start | bytes 12292
  20.2 10.1 %collective-permute-start.2 = (bf16[1440,128]{1,0:T(8,128)(2,1)S(1)}, bf16[1440,128]{1,0:T(8,128)(2,1)S(1)}, u32[]{:S(2)}, u32[]{:S(2)}) collective-permute-start(bf16[1440,128]{1,0:T(8,128)(2,1)S(1)} %get-tuple-element.22.refs_0_), channel_id=1, source_target_pairs={{0,1},{1,2},{2,3},{3,4},{4,5},{5,6},{6,7},{7,0},{8,9},{9,10},{10,1... | collective-permute-start | bytes 1105928 | tf_op jit(solution)/shard_map/ppermute | solution.py:421
  20.3 36.6 %copy-start.23 = (bf16[384,448]{0,1:T(8,128)(2,1)S(1)}, bf16[384,448]{0,1:T(8,128)(2,1)}, u32[]{:S(2)}) copy-start(bf16[384,448]{0,1:T(8,128)(2,1)} %param.21) | copy-start | bytes 1032196
  20.3 10.0 %collective-permute-start.7 = (bf16[1440,128]{1,0:T(8,128)(2,1)S(1)}, bf16[1440,128]{1,0:T(8,128)(2,1)S(1)}, u32[]{:S(2)}, u32[]{:S(2)}) collective-permute-start(bf16[1440,128]{1,0:T(8,128)(2,1)S(1)} %get-tuple-element.23), channel_id=1, source_target_pairs={{0,7},{1,0},{2,1},{3,2},{4,3},{5,4},{6,5},{7,6},{8,15},{9,8},{10,9... | collective-permute-start | bytes 1105928 | tf_op jit(solution)/shard_map/ppermute | solution.py:423
  30.4 14.2 %copy-start.7 = (bf16[1440,128]{1,0:T(8,128)(2,1)}, bf16[1440,128]{1,0:T(8,128)(2,1)S(1)}, u32[]{:S(2)}) copy-start(bf16[1440,128]{1,0:T(8,128)(2,1)S(1)} %collective-permute-done.2.refs_3_.refs_1_) | copy-start | bytes 1105924
  30.4 9.2 %collective-permute-start.3 = (bf16[1440,128]{1,0:T(8,128)(2,1)S(1)}, bf16[1440,128]{1,0:T(8,128)(2,1)S(1)}, u32[]{:S(2)}, u32[]{:S(2)}) collective-permute-start(bf16[1440,128]{1,0:T(8,128)(2,1)S(1)} %collective-permute-done.2.refs_3_.refs_1_), channel_id=1, source_target_pairs={{0,1},{1,2},{2,3},{3,4},{4,5},{5,6},{6,7},{7,0},{8,9},{9,10},{10,1... | collective-permute-start | bytes 1105928 | tf_op jit(solution)/shard_map/ppermute | solution.py:421
  30.4 14.2 %copy-start.8 = (bf16[1440,128]{1,0:T(8,128)(2,1)}, bf16[1440,128]{1,0:T(8,128)(2,1)S(1)}, u32[]{:S(2)}) copy-start(bf16[1440,128]{1,0:T(8,128)(2,1)S(1)} %collective-permute-done.7.refs_4_.refs_2_) | copy-start | bytes 1105924
  30.4 9.2 %collective-permute-start.8 = (bf16[1440,128]{1,0:T(8,128)(2,1)S(1)}, bf16[1440,128]{1,0:T(8,128)(2,1)S(1)}, u32[]{:S(2)}, u32[]{:S(2)}) collective-permute-start(bf16[1440,128]{1,0:T(8,128)(2,1)S(1)} %collective-permute-done.7.refs_4_.refs_2_), channel_id=1, source_target_pairs={{0,7},{1,0},{2,1},{3,2},{4,3},{5,4},{6,5},{7,6},{8,15},{9,8},{10,9... | collective-permute-start | bytes 1105928 | tf_op jit(solution)/shard_map/ppermute | solution.py:423
  39.6 4.9 %copy-start.9 = (bf16[1440,128]{1,0:T(8,128)(2,1)}, bf16[1440,128]{1,0:T(8,128)(2,1)S(1)}, u32[]{:S(2)}) copy-start(bf16[1440,128]{1,0:T(8,128)(2,1)S(1)} %collective-permute-done.3.refs_5_.refs_3_) | copy-start | bytes 1105924
  39.6 4.9 %copy-start.3 = (bf16[1440,128]{1,0:T(8,128)(2,1)}, bf16[1440,128]{1,0:T(8,128)(2,1)S(1)}, u32[]{:S(2)}) copy-start(bf16[1440,128]{1,0:T(8,128)(2,1)S(1)} %collective-permute-done.8.refs_6_.refs_4_) | copy-start | bytes 1105924
  41.0 19.9 %collective-permute-start.10 = (bf16[7,800,128]{2,1,0:T(8,128)(2,1)}, bf16[7,800,128]{2,1,0:T(8,128)(2,1)}, u32[]{:S(2)}, u32[]{:S(2)}) collective-permute-start(bf16[7,800,128]{2,1,0:T(8,128)(2,1)} %shard_map.138), channel_id=1, source_target_pairs={{0,8},{8,0},{16,24},{24,16},{32,40},{40,32},{48,56},{56,48},{64,72... | collective-permute-start | bytes 4300808 | tf_op jit(solution)/shard_map/ppermute | solution.py:441
  44.2 11.5 %collective-permute-start.4 = (bf16[1440,128]{1,0:T(8,128)(2,1)S(1)}, bf16[1440,128]{1,0:T(8,128)(2,1)S(1)}, u32[]{:S(2)}, u32[]{:S(2)}) collective-permute-start(bf16[1440,128]{1,0:T(8,128)(2,1)S(1)} %collective-permute-done.3.refs_5_.refs_3_), channel_id=1, source_target_pairs={{0,1},{1,2},{2,3},{3,4},{4,5},{5,6},{6,7},{7,0},{8,9},{9,10},{10,1... | collective-permute-start | bytes 1105928 | tf_op jit(solution)/shard_map/ppermute | solution.py:421
  44.6 16.4 %collective-permute-start.9 = (bf16[640,128]{1,0:T(8,128)(2,1)S(1)}, bf16[640,128]{1,0:T(8,128)(2,1)S(1)}, u32[]{:S(2)}, u32[]{:S(2)}) collective-permute-start(bf16[640,128]{1,0:T(8,128)(2,1)S(1)} %slice.13), channel_id=1, source_target_pairs={{0,7},{1,0},{2,1},{3,2},{4,3},{5,4},{6,5},{7,6},{8,15},{9,8},{10,9... | collective-permute-start | bytes 491528 | tf_op jit(solution)/shard_map/ppermute | solution.py:423
  55.7 4.6 %copy-start.15 = (bf16[1440,128]{1,0:T(8,128)(2,1)}, bf16[1440,128]{1,0:T(8,128)(2,1)S(1)}, u32[]{:S(2)}) copy-start(bf16[1440,128]{1,0:T(8,128)(2,1)S(1)} %collective-permute-done.4.refs_5_.refs_1_) | copy-start | bytes 1105924
  55.8 4.6 %copy-start.22 = (f32[1280]{0:T(1024)S(1)}, f32[1280]{0:T(1024)}, u32[]{:S(2)}) copy-start(f32[1280]{0:T(1024)} %param.19) | copy-start | bytes 15364
  55.8 13.1 %collective-permute-start.5 = (bf16[640,128]{1,0:T(8,128)(2,1)S(1)}, bf16[640,128]{1,0:T(8,128)(2,1)S(1)}, u32[]{:S(2)}, u32[]{:S(2)}) collective-permute-start(bf16[640,128]{1,0:T(8,128)(2,1)S(1)} %slice.12), channel_id=1, source_target_pairs={{0,1},{1,2},{2,3},{3,4},{4,5},{5,6},{6,7},{7,0},{8,9},{9,10},{10,1... | collective-permute-start | bytes 491528 | tf_op jit(solution)/shard_map/ppermute | solution.py:424
  55.9 13.0 %collective-permute-start.6 = (bf16[1440,128]{1,0:T(8,128)(2,1)S(1)}, bf16[1440,128]{1,0:T(8,128)(2,1)S(1)}, u32[]{:S(2)}, u32[]{:S(2)}) collective-permute-start(bf16[1440,128]{1,0:T(8,128)(2,1)S(1)} %collective-permute-done.4.refs_5_.refs_1_), channel_id=1, source_target_pairs={{0,8},{8,0},{16,24},{24,16},{32,40},{40,32},{48,56},{56,48},{64,72... | collective-permute-start | bytes 1105928 | tf_op jit(solution)/shard_map/ppermute | solution.py:442
  61.0 0.7 copy-start.18
  68.8 0.7 copy-start.17
  68.8 0.8 copy-start.16
  77.4 45.2 %copy-start.20 = (f32[3584]{0:T(1024)S(1)}, f32[3584]{0:T(1024)}, u32[]{:S(2)}) copy-start(f32[3584]{0:T(1024)} %param.24) | copy-start | bytes 43012
  77.4 28.0 %all-to-all-start = ((bf16[32,32,448]{2,1,0:T(8,128)(2,1)}), bf16[32,32,448]{2,1,0:T(8,128)(2,1)S(1)}, u32[]{:S(2)}, u32[]{:S(2)}) async-start(bf16[32,32,448]{2,1,0:T(8,128)(2,1)} %bitcast.22), calls=%async_computation | async-start | bytes 2097152 | tf_op jit(solution)/shard_map/all_to_all | solution.py:504
  84.8 146.3 %reduce-scatter.2.cloned.1.call-start = ((), (), s32[]{:S(2)}) async-start(), calls=%async_computation.4 | async-start | bytes 4128768 | tf_op jit(solution)/shard_map/reduce_scatter | solution.py:595
  106.1 13.8 %collective-permute-start.11 = (bf16[512,448]{1,0:T(8,128)(2,1)S(1)}, bf16[512,448]{1,0:T(8,128)(2,1)S(1)}, u32[]{:S(2)}, u32[]{:S(2)}) collective-permute-start(bf16[512,448]{1,0:T(8,128)(2,1)S(1)} %shard_map.141.refs_0_), channel_id=1, source_target_pairs={{0,1},{1,2},{2,3},{3,4},{4,5},{5,6},{6,7},{7,0},{8,9},{9,10},{10,1... | collective-permute-start | bytes 1376264 | tf_op jit(solution)/shard_map/ppermute | solution.py:561
  107.5 12.5 %collective-permute-start.12 = (bf16[512,448]{1,0:T(8,128)(2,1)S(1)}, bf16[512,448]{1,0:T(8,128)(2,1)S(1)}, u32[]{:S(2)}, u32[]{:S(2)}) collective-permute-start(bf16[512,448]{1,0:T(8,128)(2,1)S(1)} %shard_map.141.refs_0_), channel_id=1, source_target_pairs={{0,7},{1,0},{2,1},{3,2},{4,3},{5,4},{6,5},{7,6},{8,15},{9,8},{10,9... | collective-permute-start | bytes 1376264 | tf_op jit(solution)/shard_map/ppermute | solution.py:563
  120.0 12.5 %collective-permute-start.13 = (bf16[512,448]{1,0:T(8,128)(2,1)S(1)}, bf16[512,448]{1,0:T(8,128)(2,1)S(1)}, u32[]{:S(2)}, u32[]{:S(2)}) collective-permute-start(bf16[512,448]{1,0:T(8,128)(2,1)S(1)} %collective-permute-done.11.refs_1_), channel_id=1, source_target_pairs={{0,1},{1,2},{2,3},{3,4},{4,5},{5,6},{6,7},{7,0},{8,9},{9,10},{10,1... | collective-permute-start | bytes 1376264 | tf_op jit(solution)/shard_map/ppermute | solution.py:561
  120.0 12.5 %collective-permute-start.14 = (bf16[512,448]{1,0:T(8,128)(2,1)S(1)}, bf16[512,448]{1,0:T(8,128)(2,1)}, u32[]{:S(2)}, u32[]{:S(2)}) collective-permute-start(bf16[512,448]{1,0:T(8,128)(2,1)S(1)} %collective-permute-done.12.refs_2_), channel_id=1, source_target_pairs={{0,7},{1,0},{2,1},{3,2},{4,3},{5,4},{6,5},{7,6},{8,15},{9,8},{10,9... | collective-permute-start | bytes 1376264 | tf_op jit(solution)/shard_map/ppermute | solution.py:563
  132.4 14.4 %collective-permute-start.15 = (bf16[512,448]{1,0:T(8,128)(2,1)S(1)}, bf16[512,448]{1,0:T(8,128)(2,1)S(1)}, u32[]{:S(2)}, u32[]{:S(2)}) collective-permute-start(bf16[512,448]{1,0:T(8,128)(2,1)S(1)} %collective-permute-done.13.refs_3_), channel_id=1, source_target_pairs={{0,1},{1,2},{2,3},{3,4},{4,5},{5,6},{6,7},{7,0},{8,9},{9,10},{10,1... | collective-permute-start | bytes 1376264 | tf_op jit(solution)/shard_map/ppermute | solution.py:561
  132.4 14.5 %collective-permute-start.16 = (bf16[512,448]{1,0:T(8,128)(2,1)}, bf16[512,448]{1,0:T(8,128)(2,1)S(1)}, u32[]{:S(2)}, u32[]{:S(2)}) collective-permute-start(bf16[512,448]{1,0:T(8,128)(2,1)} %collective-permute-done.14.refs_4_), channel_id=1, source_target_pairs={{0,7},{1,0},{2,1},{3,2},{4,3},{5,4},{6,5},{7,6},{8,15},{9,8},{10,9... | collective-permute-start | bytes 1376264 | tf_op jit(solution)/shard_map/ppermute | solution.py:563
  146.9 11.2 %collective-permute-start.17 = (bf16[512,448]{1,0:T(8,128)(2,1)S(1)}, bf16[512,448]{1,0:T(8,128)(2,1)S(1)}, u32[]{:S(2)}, u32[]{:S(2)}) collective-permute-start(bf16[512,448]{1,0:T(8,128)(2,1)S(1)} %collective-permute-done.15.refs_0_.refs_5_), channel_id=1, source_target_pairs={{0,1},{1,2},{2,3},{3,4},{4,5},{5,6},{6,7},{7,0},{8,9},{9,10},{10,1... | collective-permute-start | bytes 1376264 | tf_op jit(solution)/shard_map/ppermute | solution.py:561
  164.6 0.8 copy-start.11
  178.2 1.0 copy-start.12
  179.3 53.6 %copy-start.1 = (bf16[160,1280]{1,0:T(8,128)(2,1)S(1)}, bf16[160,1280]{1,0:T(8,128)(2,1)}, u32[]{:S(2)}) copy-start(bf16[160,1280]{1,0:T(8,128)(2,1)} %param.18) | copy-start | bytes 1228804
Sparse Core Ops, SparseCore 0:
  9.9 94.1 all-gather.2
  106.7 61.7 all-gather.4
  178.3 52.7 reduce-scatter.1

commit v7 on v6

--- a/solution.py
+++ b/solution.py
@@ -409,6 +409,18 @@
         jnp.swapaxes(qkv_weight, 1, 2),
     )
 
+    video_rows = patch_count // 4
+    seq_count = video_rows + audio.shape[0]
+    capacity = 2 * seq_count // owner_count
+    sent_lengths = span_lengths[owner]
+    starts = jnp.cumsum(sent_lengths) - sent_lengths
+    slot_index = jnp.arange(capacity, dtype=jnp.int32)
+    row_of_slot = jnp.where(
+        slot_index[None, :] < sent_lengths[:, None], starts[:, None] + slot_index[None, :], -1
+    ).reshape(-1)
+    row = jnp.arange(seq_count, dtype=jnp.int32)
+    select = (row_of_slot[:, None] == row[None, video_rows:]).astype(BF16)
+    from_audio = jnp.dot(select, audio, preferred_element_type=F32).astype(BF16)
     group = 2 * HEAD_VIT
     own_head = lax.dynamic_slice_in_dim(out_weight, core * HEAD_VIT, HEAD_VIT, 0)
     above = lax.ppermute(own_head, "tensor", shifted("tensor", 1))
@@ -418,9 +430,12 @@
     up, down = call(pack_kernel, (payload, payload), [vmem] * 3, 0)(context, above, below)
     ups, downs = [up], [down]
     for k in range(1, n // 2):
+        if k == 2:
+            ups[-1], from_audio, slot_column = lax.optimization_barrier(
+                (ups[-1], from_audio, row_of_slot[:, None])
+            )
         ups.append(lax.ppermute(ups[-1], "tensor", shifted("tensor", 1)))
-        away = downs[-1] if k < n // 2 - 1 else downs[-1][:split]
-        downs.append(lax.ppermute(away, "tensor", shifted("tensor", -1)))
+        downs.append(lax.ppermute(downs[-1], "tensor", shifted("tensor", -1)))
     ups.append(lax.ppermute(ups[-1][:split], "tensor", shifted("tensor", 1)))
     contexts = [up]
     tall = []
@@ -447,18 +462,6 @@
     )
     whole = lax.all_gather(stacked, "dp", axis=0, tiled=True)
 
-    video_rows = patch_count // 4
-    seq_count = video_rows + audio.shape[0]
-    capacity = 2 * seq_count // owner_count
-    sent_lengths = span_lengths[owner]
-    starts = jnp.cumsum(sent_lengths) - sent_lengths
-    slot_index = jnp.arange(capacity, dtype=jnp.int32)
-    row_of_slot = jnp.where(
-        slot_index[None, :] < sent_lengths[:, None], starts[:, None] + slot_index[None, :], -1
-    ).reshape(-1)
-    row = jnp.arange(seq_count, dtype=jnp.int32)
-    select = (row_of_slot[:, None] == row[None, video_rows:]).astype(BF16)
-    from_audio = jnp.dot(select, audio, preferred_element_type=F32).astype(BF16)
     slots = owner_count * capacity
     width = audio.shape[1]
     operands = [*contexts[: n - 1], own_head, above, below, other, patches]
@@ -496,7 +499,7 @@
         sofar,
         merge_gain[None, :],
         merger_weight.T,
-        row_of_slot[:, None],
+        slot_column,
         from_audio,
     )
     down_turned, outgoing = lax.optimization_barrier((down_weight.T, outgoing))

time: 240 us -> 240 us (level)
  local copies, waits for them, and re-layouts: 12.4 us -> 9.22 us
    ppermute x3, waiting for transfers between devices: 22.4 us -> 19.6 us  [body(): ups.append(lax.ppermute(ups[-1], 'tensor', shifted('tensor', 1)))]
where the time goes in v7:
time: 240 us
  waiting for transfers between devices  121 us (50%)
  Pallas kernels  55.2 us (23%)
  starting transfers between devices  35.4 us (15%)
  between operations  13.5 us (6%)
  local copies, waits for them, and re-layouts  9.22 us (4%)
  matrix products  2.74 us (1%)
  other arithmetic  2.41 us (1%)
    pallas_call x10, Pallas kernels, run(): pl.pallas_call(kernel, out_shape=out_shape, in_specs=specs, out_specs=out...  55.2 us
    reduce_scatter x1, waiting for transfers between devices, body(): lax.psum_scatter(terms, 'tensor', scatter_dimension=0, tiled=True)  51 us
    ppermute x4, waiting for transfers between devices, body(): a = lax.ppermute(a, 'tensor', shifted('tensor', 1))  22.7 us
    all_to_all x1, waiting for transfers between devices, body(): lax.all_to_all(outgoing.reshape(owner_count, capacity, width), 'dp', spli...  21.5 us
    ppermute x3, waiting for transfers between devices, body(): ups.append(lax.ppermute(ups[-1], 'tensor', shifted('tensor', 1)))  19.6 us
    ppermute x3, starting transfers between devices, body(): downs.append(lax.ppermute(downs[-1], 'tensor', shifted('tensor', -1)))  8.01 us
    all_to_all x1, starting transfers between devices, body(): lax.all_to_all(outgoing.reshape(owner_count, capacity, width), 'dp', spli...  7.61 us
    ppermute x3, starting transfers between devices, body(): b = lax.ppermute(b, 'tensor', shifted('tensor', -1))  7.2 us
  transfers between devices with their start and end apart: 22, of which 10 were waited for; matrix products, arithmetic and copies ran while one was open for 3% of the time, Pallas kernels for 19%

profile of v7, /device:TPU:1, one launch (start us, length us, event | category | flops | bytes accessed | tf_op | source)
XLA Modules:
  0.0 239.8 jit_solution(9022323255812356568)
XLA Ops:
  6.6 2.1 concatenate.3
  8.8 2.5 %collective-permute-start = (bf16[80,1280]{1,0:T(8,128)(2,1)S(1)}, bf16[80,1280]{1,0:T(8,128)(2,1)S(1)}, u32[]{:S(2)}, u32[]{:S(2)}) collective-permute-start(bf16[80,1280]{1,0:T(8,128)(2,1)S(1)} %constant_dynamic-slice_fusion.1.refs_0_.refs_7_), channel_id=1, source_target_pairs={{0,1},{1,2},{2,3},{3,4},{4,5},{5,6},{6,7},{7,0},{8,9},{9,10},{10,1... | collective-permute-start | bytes 614408 | tf_op jit(solution)/shard_map/ppermute | solution.py:426
  11.4 4.0 %collective-permute-start.1 = (bf16[80,1280]{1,0:T(8,128)(2,1)S(1)}, bf16[80,1280]{1,0:T(8,128)(2,1)S(1)}, u32[]{:S(2)}, u32[]{:S(2)}) collective-permute-start(bf16[80,1280]{1,0:T(8,128)(2,1)S(1)} %constant_dynamic-slice_fusion.1.refs_0_.refs_7_), channel_id=1, source_target_pairs={{0,7},{1,0},{2,1},{3,2},{4,3},{5,4},{6,5},{7,6},{8,15},{9,8},{10,9... | collective-permute-start | bytes 614408 | tf_op jit(solution)/shard_map/ppermute | solution.py:427
  15.4 0.1 copy.18.column_ref
  15.8 0.1 reduce.1
  15.9 2.9 %shard_map.136.context_ref = bf16[160,512]{1,0:T(8,128)(2,1)S(1)} custom-call(s32[1]{0:T(128)} %bitcast.3.core_ref, bf16[512,1280]{1,0:T(8,128)(2,1)S(1)} %copy-done.2, s32[512,1]{1,0:T(8,128)S(1)} %copy.18.column_ref, s32[1,512]{1,0:T(1,128)S(1)} %copy-done.14, f32[1,1280]{1,0:T(1,128)S(1)} %broadcast_in_dim.33.gain_ref, bf16[3,160,1280]{2,1,0:T(8,128)(2,1)S(1)} %bitcast.18), custom_call_target="tpu_custom_call" | custom-call | flops 796917760 | bytes 2548740 | tf_op jit(solution)/shard_map/pallas_call | solution.py:357
  18.9 1.3 collective-permute-done.above_ref.refs_1_.refs_8_
  20.3 2.7 %collective-permute-start.7 = (bf16[1440,128]{1,0:T(8,128)(2,1)S(1)}, bf16[1440,128]{1,0:T(8,128)(2,1)S(1)}, u32[]{:S(2)}, u32[]{:S(2)}) collective-permute-start(bf16[1440,128]{1,0:T(8,128)(2,1)S(1)} %get-tuple-element.27), channel_id=1, source_target_pairs={{0,7},{1,0},{2,1},{3,2},{4,3},{5,4},{6,5},{7,6},{8,15},{9,8},{10,9... | collective-permute-start | bytes 1105928 | tf_op jit(solution)/shard_map/ppermute | solution.py:438
  23.2 2.7 %fusion.2.refs_7_ = bf16[1024,448]{1,0:T(8,128)(2,1)} fusion(bf16[384,448]{0,1:T(8,128)(2,1)} %param.21, s32[384]{0:T(512)S(1)} %slice.6, s32[1024]{0:T(1024)S(1)} %select_n.49), kind=kOutput, calls=%fused_computation.2 | convolution fusion | flops 353173504 | bytes 1267200 | tf_op jit(solution)/shard_map/dot_general | solution.py:423
  26.0 4.4 %collective-permute-done.2.refs_3_.refs_1_ = bf16[1440,128]{1,0:T(8,128)(2,1)S(1)} collective-permute-done((bf16[1440,128]{1,0:T(8,128)(2,1)S(1)}, bf16[1440,128]{1,0:T(8,128)(2,1)S(1)}, u32[]{:S(2)}, u32[]{:S(2)}) %collective-permute-start.2) | collective-permute-done | bytes 368672 | tf_op jit(solution)/shard_map/ppermute | solution.py:437
  30.4 2.7 %collective-permute-start.8 = (bf16[1440,128]{1,0:T(8,128)(2,1)S(1)}, bf16[1440,128]{1,0:T(8,128)(2,1)S(1)}, u32[]{:S(2)}, u32[]{:S(2)}) collective-permute-start(bf16[1440,128]{1,0:T(8,128)(2,1)S(1)} %collective-permute-done.7.refs_4_.refs_2_), channel_id=1, source_target_pairs={{0,7},{1,0},{2,1},{3,2},{4,3},{5,4},{6,5},{7,6},{8,15},{9,8},{10,9... | collective-permute-start | bytes 1105928 | tf_op jit(solution)/shard_map/ppermute | solution.py:438
  33.1 6.6 %collective-permute-done.3.refs_5_.refs_3_ = bf16[1440,128]{1,0:T(8,128)(2,1)S(1)} collective-permute-done((bf16[1440,128]{1,0:T(8,128)(2,1)S(1)}, bf16[1440,128]{1,0:T(8,128)(2,1)S(1)}, u32[]{:S(2)}, u32[]{:S(2)}) %collective-permute-start.3) | collective-permute-done | bytes 368672 | tf_op jit(solution)/shard_map/ppermute | solution.py:437
  39.7 1.3 shard_map.138
  41.0 3.0 %collective-permute-start.10 = (bf16[7,800,128]{2,1,0:T(8,128)(2,1)}, bf16[7,800,128]{2,1,0:T(8,128)(2,1)S(1)}, u32[]{:S(2)}, u32[]{:S(2)}) collective-permute-start(bf16[7,800,128]{2,1,0:T(8,128)(2,1)} %shard_map.138), channel_id=1, source_target_pairs={{0,8},{8,0},{16,24},{24,16},{32,40},{40,32},{48,56},{56,48},{64,72... | collective-permute-start | bytes 4300808 | tf_op jit(solution)/shard_map/ppermute | solution.py:456
  44.0 2.7 %collective-permute-start.9 = (bf16[1440,128]{1,0:T(8,128)(2,1)S(1)}, bf16[1440,128]{1,0:T(8,128)(2,1)}, u32[]{:S(2)}, u32[]{:S(2)}) collective-permute-start(bf16[1440,128]{1,0:T(8,128)(2,1)S(1)} %collective-permute-done.8.refs_6_.refs_4_), channel_id=1, source_target_pairs={{0,7},{1,0},{2,1},{3,2},{4,3},{5,4},{6,5},{7,6},{8,15},{9,8},{10,9... | collective-permute-start | bytes 1105928 | tf_op jit(solution)/shard_map/ppermute | solution.py:438
  46.7 8.7 %collective-permute-done.4.refs_5_.refs_1_ = bf16[1440,128]{1,0:T(8,128)(2,1)S(1)} collective-permute-done((bf16[1440,128]{1,0:T(8,128)(2,1)S(1)}, bf16[1440,128]{1,0:T(8,128)(2,1)S(1)}, u32[]{:S(2)}, u32[]{:S(2)}) %collective-permute-start.4) | collective-permute-done | bytes 368672 | tf_op jit(solution)/shard_map/ppermute | solution.py:437
  55.3 0.9 collective-permute-start.6
  56.2 0.3 collective-permute-start.5
  56.5 0.6 broadcast_in_dim.34.refs_4_
  57.1 1.0 copy.21.refs_6_
  58.2 1.1 copy-done.16
  59.3 7.2 %shard_map.139.refs_3_ = f32[512,1280]{1,0:T(8,128)} custom-call(bf16[1440,128]{1,0:T(8,128)(2,1)} %copy-done.13, bf16[1440,128]{1,0:T(8,128)(2,1)} %copy-done.6, bf16[1440,128]{1,0:T(8,128)(2,1)} %copy-done.7, bf16[1440,128]{1,0:T(8,128)(2,1)} %copy-done.8, bf16[1440,128]{1,0:T(8,128)(2,1)} %copy-done.9, bf16[1440,128]{1,0:T(8,128)(2,1)} %copy-done.15, ...), custom_call_target="tpu_custom_call" | custom-call | flops 1677721600 | bytes 5939200 | tf_op jit(solution)/shard_map/pallas_call | solution.py:357
  66.6 7.8 %shard_map.140 = bf16[1024,448]{1,0:T(8,128)(2,1)} custom-call(bf16[640,128]{1,0:T(8,128)(2,1)} %collective-permute-done.5.refs_0_, bf16[1440,128]{1,0:T(8,128)(2,1)} %copy-done.15, bf16[1440,128]{1,0:T(8,128)(2,1)} %collective-permute-done.6.refs_2_, f32[512,1280]{1,0:T(8,128)} %shard_map.139.refs_3_, f32[1,1280]{1,0:T(1,128)} %broadcast_in_dim.34.refs_4_, ...), custom_call_target="tpu_custom_call" | custom-call | flops 587202560 | bytes 9036800 | tf_op jit(solution)/shard_map/pallas_call | solution.py:357
  74.4 7.6 %all-to-all-start = ((bf16[32,32,448]{2,1,0:T(8,128)(2,1)}), bf16[32,32,448]{2,1,0:T(8,128)(2,1)S(1)}, u32[]{:S(2)}, u32[]{:S(2)}) async-start(bf16[32,32,448]{2,1,0:T(8,128)(2,1)} %bitcast.22), calls=%async_computation | async-start | bytes 2097152 | tf_op jit(solution)/shard_map/all_to_all | solution.py:507
  82.0 0.2 dynamic-slice_reduce_fusion
  82.2 0.7 fusion.7
  83.2 21.5 %all-to-all-done = bf16[32,32,448]{2,1,0:T(8,128)(2,1)S(1)} async-done(((bf16[32,32,448]{2,1,0:T(8,128)(2,1)}), bf16[32,32,448]{2,1,0:T(8,128)(2,1)S(1)}, u32[]{:S(2)}, u32[]{:S(2)}) %all-to-all-start) | async-done | bytes 917536 | tf_op jit(solution)/shard_map/all_to_all | solution.py:507
  104.6 0.7 shard_map.141.refs_0_
  105.3 1.4 collective-permute-start.11
  106.7 1.8 collective-permute-start.12
  108.5 10.0 %collective-permute-done.11.refs_1_ = bf16[512,448]{1,0:T(8,128)(2,1)S(1)} collective-permute-done((bf16[512,448]{1,0:T(8,128)(2,1)S(1)}, bf16[512,448]{1,0:T(8,128)(2,1)S(1)}, u32[]{:S(2)}, u32[]{:S(2)}) %collective-permute-start.11) | collective-permute-done | bytes 458784 | tf_op jit(solution)/shard_map/ppermute | solution.py:564
  118.5 2.7 %collective-permute-start.14 = (bf16[512,448]{1,0:T(8,128)(2,1)S(1)}, bf16[512,448]{1,0:T(8,128)(2,1)}, u32[]{:S(2)}, u32[]{:S(2)}) collective-permute-start(bf16[512,448]{1,0:T(8,128)(2,1)S(1)} %collective-permute-done.12.refs_2_), channel_id=1, source_target_pairs={{0,7},{1,0},{2,1},{3,2},{4,3},{5,4},{6,5},{7,6},{8,15},{9,8},{10,9... | collective-permute-start | bytes 1376264 | tf_op jit(solution)/shard_map/ppermute | solution.py:566
  121.3 9.2 %collective-permute-done.13.refs_3_ = bf16[512,448]{1,0:T(8,128)(2,1)S(1)} collective-permute-done((bf16[512,448]{1,0:T(8,128)(2,1)S(1)}, bf16[512,448]{1,0:T(8,128)(2,1)S(1)}, u32[]{:S(2)}, u32[]{:S(2)}) %collective-permute-start.13) | collective-permute-done | bytes 458784 | tf_op jit(solution)/shard_map/ppermute | solution.py:564
  130.4 2.7 %collective-permute-start.16 = (bf16[512,448]{1,0:T(8,128)(2,1)}, bf16[512,448]{1,0:T(8,128)(2,1)S(1)}, u32[]{:S(2)}, u32[]{:S(2)}) collective-permute-start(bf16[512,448]{1,0:T(8,128)(2,1)} %collective-permute-done.14.refs_4_), channel_id=1, source_target_pairs={{0,7},{1,0},{2,1},{3,2},{4,3},{5,4},{6,5},{7,6},{8,15},{9,8},{10,9... | collective-permute-start | bytes 1376264 | tf_op jit(solution)/shard_map/ppermute | solution.py:566
  133.1 11.8 %shard_map.142 = (f32[512,2464]{1,0:T(8,128)}, f32[512,1]{1,0:T(8,128)S(1)}) custom-call(s32[1]{0:T(128)} %bitcast.place_ref, bf16[512,448]{1,0:T(8,128)(2,1)S(1)} %shard_map.141.refs_0_, bf16[512,448]{1,0:T(8,128)(2,1)S(1)} %collective-permute-done.11.refs_1_, bf16[512,448]{1,0:T(8,128)(2,1)S(1)} %collective-permute-done.12.refs_2_, ...), custom_call_target="tpu_custom_call" | custom-call | flops 5431623680 | bytes 19970052 | tf_op jit(solution)/shard_map/pallas_call | solution.py:357
  144.9 0.3 collective-permute-start.17
  145.2 7.0 %shard_map.143 = (f32[512,2464]{1,0:T(8,128)}, f32[512,1]{1,0:T(8,128)S(1)}) custom-call(s32[1]{0:T(128)} %bitcast.place_ref, bf16[512,448]{1,0:T(8,128)(2,1)S(1)} %collective-permute-done.15.refs_0_.refs_5_, bf16[512,448]{1,0:T(8,128)(2,1)S(1)} %collective-permute-done.16.refs_1_.refs_6_, f32[8,1,448]{2,1,0:T(1,128)S(1)} %reshape.164.refs_5_.refs_2_.refs_8_, ...), custom_call_target="tpu_custom_call" | custom-call | flops 2172649472 | bytes 23642116 | tf_op jit(solution)/shard_map/pallas_call | solution.py:357
  152.2 3.5 %collective-permute-done.17.refs_7_ = bf16[512,448]{1,0:T(8,128)(2,1)S(1)} collective-permute-done((bf16[512,448]{1,0:T(8,128)(2,1)S(1)}, bf16[512,448]{1,0:T(8,128)(2,1)S(1)}, u32[]{:S(2)}, u32[]{:S(2)}) %collective-permute-start.17) | collective-permute-done | bytes 458784 | tf_op jit(solution)/shard_map/ppermute | solution.py:564
  155.8 6.6 %shard_map.144 = (bf16[512,1184]{1,0:T(8,128)(2,1)}, bf16[8,64,448]{2,1,0:T(8,128)(2,1)S(1)}) custom-call(s32[1]{0:T(128)} %bitcast.place_ref, bf16[512,448]{1,0:T(8,128)(2,1)S(1)} %shard_map.141.refs_0_, bf16[512,448]{1,0:T(8,128)(2,1)S(1)} %collective-permute-done.11.refs_1_, bf16[512,448]{1,0:T(8,128)(2,1)S(1)} %collective-permute-done.12.refs_2_, ...), custom_call_target="tpu_custom_call" | custom-call | flops 1086324736 | bytes 26394628 | tf_op jit(solution)/shard_map/pallas_call | solution.py:357
  162.4 0.8 copy-done.11
  163.2 5.3 %all-gather.5.cloned.1.call-done.weight_hbm = bf16[3584,1184]{1,0:T(8,128)(2,1)} async-done(((bf16[112,1184]{1,0:T(8,128)(2,1)}), bf16[3584,1184]{1,0:T(8,128)(2,1)}) %all-gather.5.cloned.1.call-update) | async-done | bytes 8486928 | tf_op jit(solution)/shard_map/all_gather | solution.py:506
  168.5 9.7 %shard_map.145 = bf16[512,3584]{1,0:T(8,128)(2,1)} custom-call(bf16[512,1184]{1,0:T(8,128)(2,1)} %get-tuple-element.43.hidden_ref, bf16[3584,1184]{1,0:T(8,128)(2,1)} %all-gather.5.cloned.1.call-done.weight_hbm), custom_call_target="tpu_custom_call" | custom-call | flops 4345298944 | bytes 9699328 | tf_op jit(solution)/shard_map/pallas_call | solution.py:357
  178.3 1.0 copy-done.12
  179.3 0.1 convert_bitcast_fusion
  179.4 0.6 copy.22
  180.0 0.4 reshape.165
  180.4 51.0 %reduce-scatter.2.cloned.1.call-done = bf16[64,3584]{1,0:T(8,128)(2,1)} async-done(((bf16[512,3584]{1,0:T(8,128)(2,1)}), bf16[64,3584]{1,0:T(8,128)(2,1)}) %reduce-scatter.2.cloned.1.call-update) | async-done | bytes 458768 | tf_op jit(solution)/shard_map/reduce_scatter | solution.py:598
  231.4 1.9 add_convert_fusion
  (80 shorter events, 1.3 us)
Async XLA Ops:
  6.5 2.2 copy-start
  6.5 8.9 %copy-start.14 = (s32[1,512]{1,0:T(1,128)S(1)}, s32[1,512]{1,0:T(1,128)}, u32[]{:S(2)}) copy-start(s32[1,512]{1,0:T(1,128)} %row_ref.1) | copy-start | bytes 6148
  6.5 9.0 %copy-start.19 = (f32[1280]{0:T(1024)S(1)}, f32[1280]{0:T(1024)}, u32[]{:S(2)}) copy-start(f32[1280]{0:T(1024)} %param.16) | copy-start | bytes 15364
  6.5 9.0 %copy-start.17 = (s32[32,32]{1,0:T(8,128)S(1)}, s32[32,32]{1,0:T(8,128)}, u32[]{:S(2)}) copy-start(s32[32,32]{1,0:T(8,128)} %param.22) | copy-start | bytes 12292
  6.5 9.3 %copy-start.10 = (bf16[3,1280,160]{1,2,0:T(8,128)(2,1)S(1)}, bf16[3,1280,160]{1,2,0:T(8,128)(2,1)}, u32[]{:S(2)}) copy-start(bf16[3,1280,160]{1,2,0:T(8,128)(2,1)} %param.17) | copy-start | bytes 3686404
  6.5 9.3 %copy-start.2 = (bf16[512,1280]{1,0:T(8,128)(2,1)S(1)}, bf16[512,1280]{1,0:T(8,128)(2,1)}, u32[]{:S(2)}) copy-start(bf16[512,1280]{1,0:T(8,128)(2,1)} %refs_11_.1) | copy-start | bytes 3932164
  6.6 126.6 %all-gather.3.cloned.1.call-start = ((), (), s32[]{:S(2)}) async-start(), calls=%async_computation.2 | async-start | bytes 18923520 | tf_op jit(solution)/shard_map/all_gather | solution.py:463
  8.7 159.8 %all-gather.5.cloned.1.call-start = ((), (), s32[]{:S(2)}) async-start(), calls=%async_computation.3 | async-start | bytes 9461760 | tf_op jit(solution)/shard_map/all_gather | solution.py:506
  8.8 30.8 %copy-start.3 = (bf16[80,1280]{1,0:T(8,128)(2,1)}, bf16[80,1280]{1,0:T(8,128)(2,1)S(1)}, u32[]{:S(2)}) copy-start(bf16[80,1280]{1,0:T(8,128)(2,1)S(1)} %constant_dynamic-slice_fusion.1.refs_0_.refs_7_) | copy-start | bytes 614404
  8.8 11.3 %collective-permute-start = (bf16[80,1280]{1,0:T(8,128)(2,1)S(1)}, bf16[80,1280]{1,0:T(8,128)(2,1)S(1)}, u32[]{:S(2)}, u32[]{:S(2)}) collective-permute-start(bf16[80,1280]{1,0:T(8,128)(2,1)S(1)} %constant_dynamic-slice_fusion.1.refs_0_.refs_7_), channel_id=1, source_target_pairs={{0,1},{1,2},{2,3},{3,4},{4,5},{5,6},{6,7},{7,0},{8,9},{9,10},{10,1... | collective-permute-start | bytes 614408 | tf_op jit(solution)/shard_map/ppermute | solution.py:426
  11.4 8.7 %collective-permute-start.1 = (bf16[80,1280]{1,0:T(8,128)(2,1)S(1)}, bf16[80,1280]{1,0:T(8,128)(2,1)S(1)}, u32[]{:S(2)}, u32[]{:S(2)}) collective-permute-start(bf16[80,1280]{1,0:T(8,128)(2,1)S(1)} %constant_dynamic-slice_fusion.1.refs_0_.refs_7_), channel_id=1, source_target_pairs={{0,7},{1,0},{2,1},{3,2},{4,3},{5,4},{6,5},{7,6},{8,15},{9,8},{10,9... | collective-permute-start | bytes 614408 | tf_op jit(solution)/shard_map/ppermute | solution.py:427
  20.1 20.9 %copy-start.4 = (bf16[80,1280]{1,0:T(8,128)(2,1)}, bf16[80,1280]{1,0:T(8,128)(2,1)S(1)}, u32[]{:S(2)}) copy-start(bf16[80,1280]{1,0:T(8,128)(2,1)S(1)} %collective-permute-done.above_ref.refs_1_.refs_8_) | copy-start | bytes 614404
  20.1 20.9 %copy-start.5 = (bf16[80,1280]{1,0:T(8,128)(2,1)}, bf16[80,1280]{1,0:T(8,128)(2,1)S(1)}, u32[]{:S(2)}) copy-start(bf16[80,1280]{1,0:T(8,128)(2,1)S(1)} %collective-permute-done.1.below_ref.refs_2_.refs_9_) | copy-start | bytes 614404
  20.2 5.7 %copy-start.13 = (bf16[1440,128]{1,0:T(8,128)(2,1)}, bf16[1440,128]{1,0:T(8,128)(2,1)S(1)}, u32[]{:S(2)}) copy-start(bf16[1440,128]{1,0:T(8,128)(2,1)S(1)} %get-tuple-element.25.refs_0_) | copy-start | bytes 1105924
  20.3 10.1 %collective-permute-start.2 = (bf16[1440,128]{1,0:T(8,128)(2,1)S(1)}, bf16[1440,128]{1,0:T(8,128)(2,1)S(1)}, u32[]{:S(2)}, u32[]{:S(2)}) collective-permute-start(bf16[1440,128]{1,0:T(8,128)(2,1)S(1)} %get-tuple-element.25.refs_0_), channel_id=1, source_target_pairs={{0,1},{1,2},{2,3},{3,4},{4,5},{5,6},{6,7},{7,0},{8,9},{9,10},{10,1... | collective-permute-start | bytes 1105928 | tf_op jit(solution)/shard_map/ppermute | solution.py:437
  20.3 10.1 %collective-permute-start.7 = (bf16[1440,128]{1,0:T(8,128)(2,1)S(1)}, bf16[1440,128]{1,0:T(8,128)(2,1)S(1)}, u32[]{:S(2)}, u32[]{:S(2)}) collective-permute-start(bf16[1440,128]{1,0:T(8,128)(2,1)S(1)} %get-tuple-element.27), channel_id=1, source_target_pairs={{0,7},{1,0},{2,1},{3,2},{4,3},{5,4},{6,5},{7,6},{8,15},{9,8},{10,9... | collective-permute-start | bytes 1105928 | tf_op jit(solution)/shard_map/ppermute | solution.py:438
  26.0 30.5 %copy-start.20 = (f32[1280]{0:T(1024)S(1)}, f32[1280]{0:T(1024)}, u32[]{:S(2)}) copy-start(f32[1280]{0:T(1024)} %param.19) | copy-start | bytes 15364
  30.4 27.7 %copy-start.6 = (bf16[1440,128]{1,0:T(8,128)(2,1)}, bf16[1440,128]{1,0:T(8,128)(2,1)S(1)}, u32[]{:S(2)}) copy-start(bf16[1440,128]{1,0:T(8,128)(2,1)S(1)} %collective-permute-done.2.refs_3_.refs_1_) | copy-start | bytes 1105924
  30.4 9.2 %collective-permute-start.3 = (bf16[1440,128]{1,0:T(8,128)(2,1)S(1)}, bf16[1440,128]{1,0:T(8,128)(2,1)S(1)}, u32[]{:S(2)}, u32[]{:S(2)}) collective-permute-start(bf16[1440,128]{1,0:T(8,128)(2,1)S(1)} %collective-permute-done.2.refs_3_.refs_1_), channel_id=1, source_target_pairs={{0,1},{1,2},{2,3},{3,4},{4,5},{5,6},{6,7},{7,0},{8,9},{9,10},{10,1... | collective-permute-start | bytes 1105928 | tf_op jit(solution)/shard_map/ppermute | solution.py:437
  30.4 27.7 %copy-start.7 = (bf16[1440,128]{1,0:T(8,128)(2,1)}, bf16[1440,128]{1,0:T(8,128)(2,1)S(1)}, u32[]{:S(2)}) copy-start(bf16[1440,128]{1,0:T(8,128)(2,1)S(1)} %collective-permute-done.7.refs_4_.refs_2_) | copy-start | bytes 1105924
  30.4 9.2 %collective-permute-start.8 = (bf16[1440,128]{1,0:T(8,128)(2,1)S(1)}, bf16[1440,128]{1,0:T(8,128)(2,1)S(1)}, u32[]{:S(2)}, u32[]{:S(2)}) collective-permute-start(bf16[1440,128]{1,0:T(8,128)(2,1)S(1)} %collective-permute-done.7.refs_4_.refs_2_), channel_id=1, source_target_pairs={{0,7},{1,0},{2,1},{3,2},{4,3},{5,4},{6,5},{7,6},{8,15},{9,8},{10,9... | collective-permute-start | bytes 1105928 | tf_op jit(solution)/shard_map/ppermute | solution.py:438
  39.6 18.5 %copy-start.8 = (bf16[1440,128]{1,0:T(8,128)(2,1)}, bf16[1440,128]{1,0:T(8,128)(2,1)S(1)}, u32[]{:S(2)}) copy-start(bf16[1440,128]{1,0:T(8,128)(2,1)S(1)} %collective-permute-done.3.refs_5_.refs_3_) | copy-start | bytes 1105924
  39.7 18.5 %copy-start.9 = (bf16[1440,128]{1,0:T(8,128)(2,1)}, bf16[1440,128]{1,0:T(8,128)(2,1)S(1)}, u32[]{:S(2)}) copy-start(bf16[1440,128]{1,0:T(8,128)(2,1)S(1)} %collective-permute-done.8.refs_6_.refs_4_) | copy-start | bytes 1105924
  41.0 17.1 %collective-permute-start.10 = (bf16[7,800,128]{2,1,0:T(8,128)(2,1)}, bf16[7,800,128]{2,1,0:T(8,128)(2,1)S(1)}, u32[]{:S(2)}, u32[]{:S(2)}) collective-permute-start(bf16[7,800,128]{2,1,0:T(8,128)(2,1)} %shard_map.138), channel_id=1, source_target_pairs={{0,8},{8,0},{16,24},{24,16},{32,40},{40,32},{48,56},{56,48},{64,72... | collective-permute-start | bytes 4300808 | tf_op jit(solution)/shard_map/ppermute | solution.py:456
  44.0 11.4 %collective-permute-start.4 = (bf16[1440,128]{1,0:T(8,128)(2,1)S(1)}, bf16[1440,128]{1,0:T(8,128)(2,1)S(1)}, u32[]{:S(2)}, u32[]{:S(2)}) collective-permute-start(bf16[1440,128]{1,0:T(8,128)(2,1)S(1)} %collective-permute-done.3.refs_5_.refs_3_), channel_id=1, source_target_pairs={{0,1},{1,2},{2,3},{3,4},{4,5},{5,6},{6,7},{7,0},{8,9},{9,10},{10,1... | collective-permute-start | bytes 1105928 | tf_op jit(solution)/shard_map/ppermute | solution.py:437
  44.0 14.2 %collective-permute-start.9 = (bf16[1440,128]{1,0:T(8,128)(2,1)S(1)}, bf16[1440,128]{1,0:T(8,128)(2,1)}, u32[]{:S(2)}, u32[]{:S(2)}) collective-permute-start(bf16[1440,128]{1,0:T(8,128)(2,1)S(1)} %collective-permute-done.8.refs_6_.refs_4_), channel_id=1, source_target_pairs={{0,7},{1,0},{2,1},{3,2},{4,3},{5,4},{6,5},{7,6},{8,15},{9,8},{10,9... | collective-permute-start | bytes 1105928 | tf_op jit(solution)/shard_map/ppermute | solution.py:438
  55.3 2.8 %copy-start.15 = (bf16[1440,128]{1,0:T(8,128)(2,1)}, bf16[1440,128]{1,0:T(8,128)(2,1)S(1)}, u32[]{:S(2)}) copy-start(bf16[1440,128]{1,0:T(8,128)(2,1)S(1)} %collective-permute-done.4.refs_5_.refs_1_) | copy-start | bytes 1105924
  55.3 11.2 %collective-permute-start.6 = (bf16[1440,128]{1,0:T(8,128)(2,1)S(1)}, bf16[1440,128]{1,0:T(8,128)(2,1)}, u32[]{:S(2)}, u32[]{:S(2)}) collective-permute-start(bf16[1440,128]{1,0:T(8,128)(2,1)S(1)} %collective-permute-done.4.refs_5_.refs_1_), channel_id=1, source_target_pairs={{0,8},{8,0},{16,24},{24,16},{32,40},{40,32},{48,56},{56,48},{64,72... | collective-permute-start | bytes 1105928 | tf_op jit(solution)/shard_map/ppermute | solution.py:457
  56.2 10.3 %collective-permute-start.5 = (bf16[640,128]{1,0:T(8,128)(2,1)S(1)}, bf16[640,128]{1,0:T(8,128)(2,1)}, u32[]{:S(2)}, u32[]{:S(2)}) collective-permute-start(bf16[640,128]{1,0:T(8,128)(2,1)S(1)} %slice.8), channel_id=1, source_target_pairs={{0,1},{1,2},{2,3},{3,4},{4,5},{5,6},{6,7},{7,0},{8,9},{9,10},{10,1... | collective-permute-start | bytes 491528 | tf_op jit(solution)/shard_map/ppermute | solution.py:439
  58.2 1.1 copy-start.16
  74.3 46.9 %copy-start.18 = (f32[3584]{0:T(1024)S(1)}, f32[3584]{0:T(1024)}, u32[]{:S(2)}) copy-start(f32[3584]{0:T(1024)} %param.24) | copy-start | bytes 43012
  74.4 30.3 %all-to-all-start = ((bf16[32,32,448]{2,1,0:T(8,128)(2,1)}), bf16[32,32,448]{2,1,0:T(8,128)(2,1)S(1)}, u32[]{:S(2)}, u32[]{:S(2)}) async-start(bf16[32,32,448]{2,1,0:T(8,128)(2,1)} %bitcast.22), calls=%async_computation | async-start | bytes 2097152 | tf_op jit(solution)/shard_map/all_to_all | solution.py:507
  82.0 149.5 %reduce-scatter.2.cloned.1.call-start = ((), (), s32[]{:S(2)}) async-start(), calls=%async_computation.4 | async-start | bytes 4128768 | tf_op jit(solution)/shard_map/reduce_scatter | solution.py:598
  105.3 13.2 %collective-permute-start.11 = (bf16[512,448]{1,0:T(8,128)(2,1)S(1)}, bf16[512,448]{1,0:T(8,128)(2,1)S(1)}, u32[]{:S(2)}, u32[]{:S(2)}) collective-permute-start(bf16[512,448]{1,0:T(8,128)(2,1)S(1)} %shard_map.141.refs_0_), channel_id=1, source_target_pairs={{0,1},{1,2},{2,3},{3,4},{4,5},{5,6},{6,7},{7,0},{8,9},{9,10},{10,1... | collective-permute-start | bytes 1376264 | tf_op jit(solution)/shard_map/ppermute | solution.py:564
  106.7 11.8 %collective-permute-start.12 = (bf16[512,448]{1,0:T(8,128)(2,1)S(1)}, bf16[512,448]{1,0:T(8,128)(2,1)S(1)}, u32[]{:S(2)}, u32[]{:S(2)}) collective-permute-start(bf16[512,448]{1,0:T(8,128)(2,1)S(1)} %shard_map.141.refs_0_), channel_id=1, source_target_pairs={{0,7},{1,0},{2,1},{3,2},{4,3},{5,4},{6,5},{7,6},{8,15},{9,8},{10,9... | collective-permute-start | bytes 1376264 | tf_op jit(solution)/shard_map/ppermute | solution.py:566
  118.5 11.9 %collective-permute-start.13 = (bf16[512,448]{1,0:T(8,128)(2,1)S(1)}, bf16[512,448]{1,0:T(8,128)(2,1)S(1)}, u32[]{:S(2)}, u32[]{:S(2)}) collective-permute-start(bf16[512,448]{1,0:T(8,128)(2,1)S(1)} %collective-permute-done.11.refs_1_), channel_id=1, source_target_pairs={{0,1},{1,2},{2,3},{3,4},{4,5},{5,6},{6,7},{7,0},{8,9},{9,10},{10,1... | collective-permute-start | bytes 1376264 | tf_op jit(solution)/shard_map/ppermute | solution.py:564
  118.5 11.9 %collective-permute-start.14 = (bf16[512,448]{1,0:T(8,128)(2,1)S(1)}, bf16[512,448]{1,0:T(8,128)(2,1)}, u32[]{:S(2)}, u32[]{:S(2)}) collective-permute-start(bf16[512,448]{1,0:T(8,128)(2,1)S(1)} %collective-permute-done.12.refs_2_), channel_id=1, source_target_pairs={{0,7},{1,0},{2,1},{3,2},{4,3},{5,4},{6,5},{7,6},{8,15},{9,8},{10,9... | collective-permute-start | bytes 1376264 | tf_op jit(solution)/shard_map/ppermute | solution.py:566
  130.4 14.5 %collective-permute-start.15 = (bf16[512,448]{1,0:T(8,128)(2,1)S(1)}, bf16[512,448]{1,0:T(8,128)(2,1)S(1)}, u32[]{:S(2)}, u32[]{:S(2)}) collective-permute-start(bf16[512,448]{1,0:T(8,128)(2,1)S(1)} %collective-permute-done.13.refs_3_), channel_id=1, source_target_pairs={{0,1},{1,2},{2,3},{3,4},{4,5},{5,6},{6,7},{7,0},{8,9},{9,10},{10,1... | collective-permute-start | bytes 1376264 | tf_op jit(solution)/shard_map/ppermute | solution.py:564
  130.4 14.5 %collective-permute-start.16 = (bf16[512,448]{1,0:T(8,128)(2,1)}, bf16[512,448]{1,0:T(8,128)(2,1)S(1)}, u32[]{:S(2)}, u32[]{:S(2)}) collective-permute-start(bf16[512,448]{1,0:T(8,128)(2,1)} %collective-permute-done.14.refs_4_), channel_id=1, source_target_pairs={{0,7},{1,0},{2,1},{3,2},{4,3},{5,4},{6,5},{7,6},{8,15},{9,8},{10,9... | collective-permute-start | bytes 1376264 | tf_op jit(solution)/shard_map/ppermute | solution.py:566
  144.9 10.8 %collective-permute-start.17 = (bf16[512,448]{1,0:T(8,128)(2,1)S(1)}, bf16[512,448]{1,0:T(8,128)(2,1)S(1)}, u32[]{:S(2)}, u32[]{:S(2)}) collective-permute-start(bf16[512,448]{1,0:T(8,128)(2,1)S(1)} %collective-permute-done.15.refs_0_.refs_5_), channel_id=1, source_target_pairs={{0,1},{1,2},{2,3},{3,4},{4,5},{5,6},{6,7},{7,0},{8,9},{9,10},{10,1... | collective-permute-start | bytes 1376264 | tf_op jit(solution)/shard_map/ppermute | solution.py:564
  162.4 0.8 copy-start.11
  178.2 1.0 copy-start.12
  179.4 53.9 %copy-start.1 = (bf16[160,1280]{1,0:T(8,128)(2,1)S(1)}, bf16[160,1280]{1,0:T(8,128)(2,1)}, u32[]{:S(2)}) copy-start(bf16[160,1280]{1,0:T(8,128)(2,1)} %param.18) | copy-start | bytes 1228804
Sparse Core Ops, SparseCore 0:
  9.9 96.0 all-gather.2
  108.6 59.8 all-gather.4
  178.4 53.0 reduce-scatter.1
